TPU v7x, 32 devices: a whole 2x2x4 slice. The times are simulated.
32 devices in a mesh: row: 16 (over z, y, core), col: 2 (over x).
Axes of the slice: x: 2, y: 2, z: 4, core: 2. Of those that a mesh axis runs over, the one named last changes fastest.
Arguments:
- latents: bfloat16 [16, 1152, 1024], P('row', 'col'), may hold values from -6 to 6
- labels: int32 [16], replicated, may hold values from 0 to 1000
- timesteps: int32 [16], replicated, may hold values from 0 to 999
- label_table: bfloat16 [1152, 1001], P('col'), may hold values from -6 to 6
- ada_weight: bfloat16 [6, 1152, 1152], P(None, 'col'), may hold values from -0.1875 to 0.1875
- ada_bias: bfloat16 [6, 1152], P(None, 'col'), may hold values from -3 to 3
- qkv_weight: bfloat16 [1152, 3, 1152], P('row', None, 'col'), may hold values from -0.1875 to 0.1875
- qv_bias: bfloat16 [2, 1152], P(None, 'col'), may hold values from -3 to 3
- proj_weight: bfloat16 [1152, 1152], P('col', 'row'), may hold values from -2 to 2
- proj_bias: bfloat16 [1152], P('col'), may hold values from -3 to 3
- expand_weight: bfloat16 [1152, 4608], P('row', 'col'), may hold values from -0.1875 to 0.1875
- expand_bias: bfloat16 [4608], P('col'), may hold values from -3 to 3
- contract_weight: bfloat16 [4608, 1152], P('col', 'row'), may hold values from -0.09375 to 0.09375
- contract_bias: bfloat16 [1152], P('col'), may hold values from -3 to 3
- cotangent: bfloat16 [16, 1152, 1024], P('row', 'col'), may hold values from -6 to 6
Outputs:
- block_out: float32 [16, 1152, 1024], P('row', 'col')
- grad_latents: float32 [16, 1152, 1024], P('row', 'col')
- grad_qkv: float32 [1152, 3, 1152], P('row', None, 'col')
- grad_qv_bias: float32 [2, 1152], P(None, 'col')
- grad_proj: float32 [1152, 1152], P('col', 'row')
- grad_proj_bias: float32 [1152], P('col')
- grad_expand: float32 [1152, 4608], P('row', 'col')
- grad_expand_bias: float32 [4608], P('col')
- grad_contract: float32 [4608, 1152], P('col', 'row')
- grad_contract_bias: float32 [1152], P('col')
- grad_ada: float32 [6, 1152, 1152], P(None, 'col')
- grad_ada_bias: float32 [6, 1152], P(None, 'col')
- grad_cond: float32 [16, 1152], P('row', 'col')
- grad_table: float32 [1152, 1001], P('col')
All inputs are finite; a program needn't handle non-finite values.
Results may differ from a plain program's by a relative error of at most 0.023.
Values may be sent and summed in bfloat16 or wider, within the bound.
No kernel may reach another device: no remote copies, remote signals or barrier semaphores. Data moves between devices by JAX's collectives and lax.ppermute only.
A program may use at most 256 MiB of HBM per device.

v0:
```python
import math

import jax
import jax.numpy as jnp
from jax import lax
from jax.sharding import PartitionSpec as P

D = 1152
HEAD = 72
CLASSES = 1001


EPSILON = 1e-06
GELU_COEF = 0.7978845608028654


def gelu_tanh(values):
    return (
        0.5 * values * (1.0 + jnp.tanh(GELU_COEF * (values + 0.044715 * values * values * values)))
    )


def feature_sums(first_part, second_part):
    return lax.psum((jnp.sum(first_part, axis=1), jnp.sum(second_part, axis=1)), "col")


def norm_forward(values):
    total, squares = feature_sums(values, values * values)
    average = (total / D)[:, None, :]
    spread = (squares / D)[:, None, :] - average * average
    inverse = lax.rsqrt(spread + EPSILON)
    return ((values - average) * inverse, inverse)


def norm_backward(grad_normed, normed, inverse):
    total, cross = feature_sums(grad_normed, grad_normed * normed)
    return inverse * (grad_normed - (total / D)[:, None, :] - normed * (cross / D)[:, None, :])


def gather_cols(values):
    return lax.all_gather(values, "col", axis=1, tiled=True)


def sum_cols(values):
    return lax.psum_scatter(
        values.astype(jnp.bfloat16), "col", scatter_dimension=1, tiled=True
    ).astype(jnp.float32)


def split_heads(values):
    return values.reshape(values.shape[0], values.shape[1] // HEAD, HEAD, values.shape[2])


def score_block(query_heads, key_heads):
    return jnp.einsum(
        "shdq,shdk->shqk", query_heads, key_heads, preferred_element_type=jnp.float32
    ) * (1.0 / math.sqrt(HEAD))


def on_device(
    latents,
    labels,
    timesteps,
    label_table,
    ada_weight,
    ada_bias,
    qkv_weight,
    qv_bias,
    proj_weight,
    proj_bias,
    expand_weight,
    expand_bias,
    contract_weight,
    contract_bias,
    cotangent,
):
    seq_count, col_width, length = latents.shape
    score_scale = 1.0 / math.sqrt(HEAD)
    feature = lax.axis_index("col") * col_width + jnp.arange(col_width, dtype=jnp.int32)
    half_width = D // 2
    frequency = jnp.exp(
        -math.log(10000.0) * (feature % half_width).astype(jnp.float32) / half_width
    )
    angles = timesteps.astype(jnp.float32)[:, None] * frequency[None, :]
    embedding = jnp.where(feature[None, :] < half_width, jnp.cos(angles), jnp.sin(angles))
    label_hits = labels[:, None] == jnp.arange(CLASSES, dtype=jnp.int32)[None, :]
    cond_all = (
        jnp.einsum(
            "sk,ck->sc",
            label_hits.astype(jnp.bfloat16),
            label_table,
            preferred_element_type=jnp.float32,
        )
        + embedding
    )
    silu_cond = jax.nn.silu(cond_all).astype(jnp.bfloat16)
    silu_all = lax.all_gather(silu_cond, "col", axis=1, tiled=True)
    first_seq = lax.axis_index("row") * seq_count
    silu_own = lax.dynamic_slice_in_dim(silu_all, first_seq, seq_count, 0)
    cond_own = lax.dynamic_slice_in_dim(cond_all, first_seq, seq_count, 0)
    flat_ada = ada_weight.reshape(6 * col_width, D)
    modulation = lax.dot_general(
        silu_own, flat_ada, (((1,), (1,)), ((), ())), preferred_element_type=jnp.float32
    ).reshape(seq_count, 6, col_width) + ada_bias.astype(jnp.float32)
    shift_first, scale_first, gate_first, shift_second, scale_second, gate_second = [
        modulation[:, position, :, None] for position in range(6)
    ]
    qkv_all, proj_all, expand_all, contract_all = (
        lax.all_gather(qkv_weight, "row", axis=0, tiled=True),
        lax.all_gather(proj_weight, "row", axis=1, tiled=True),
        lax.all_gather(expand_weight, "row", axis=0, tiled=True),
        lax.all_gather(contract_weight, "row", axis=1, tiled=True),
    )
    triple_all = qkv_all.reshape(D, 3 * col_width)
    start = latents.astype(jnp.float32)
    normed_first, inv_first = norm_forward(start)
    in_first = gather_cols((normed_first * (1.0 + scale_first) + shift_first).astype(jnp.bfloat16))
    triple = jnp.einsum(
        "sdl,dc->scl", in_first, triple_all, preferred_element_type=jnp.float32
    ).reshape(seq_count, 3, col_width, length)
    query_rows = (triple[:, 0] + qv_bias[0][:, None]).astype(jnp.bfloat16)
    key_rows = triple[:, 1].astype(jnp.bfloat16)
    value_rows = (triple[:, 2] + qv_bias[1][:, None]).astype(jnp.bfloat16)
    query_heads = split_heads(query_rows)
    key_heads = split_heads(key_rows)
    value_heads = split_heads(value_rows)
    scores = score_block(query_heads, key_heads)
    row_top = jnp.max(scores, axis=-1, keepdims=True)
    log_total = jnp.log(jnp.sum(jnp.exp(scores - row_top), axis=-1, keepdims=True)) + row_top
    soft_b = jnp.exp(scores - log_total).astype(jnp.bfloat16)
    attended = (
        jnp.einsum("shqk,shdk->shdq", soft_b, value_heads, preferred_element_type=jnp.float32)
        .reshape(seq_count, col_width, length)
        .astype(jnp.bfloat16)
    )
    proj_out = (
        sum_cols(jnp.einsum("sel,ed->sdl", attended, proj_all, preferred_element_type=jnp.float32))
        + proj_bias[:, None]
    )
    residual = start + gate_first * proj_out
    normed_second, inv_second = norm_forward(residual)
    in_second = gather_cols(
        (normed_second * (1.0 + scale_second) + shift_second).astype(jnp.bfloat16)
    )
    pre_act = (
        jnp.einsum("sdl,df->sfl", in_second, expand_all, preferred_element_type=jnp.float32)
        + expand_bias[:, None]
    )
    hidden = gelu_tanh(pre_act).astype(jnp.bfloat16)
    mlp_out = (
        sum_cols(
            jnp.einsum("sfl,fd->sdl", hidden, contract_all, preferred_element_type=jnp.float32)
        )
        + contract_bias[:, None]
    )
    block_out = residual + gate_second * mlp_out
    grad_out = cotangent.astype(jnp.float32)
    grad_mlp = grad_out * gate_second
    grad_mlp_all = gather_cols(grad_mlp.astype(jnp.bfloat16))
    contract_term = jnp.einsum(
        "sfl,sdl->fd", hidden, grad_mlp_all, preferred_element_type=jnp.float32
    )
    grad_hidden = jnp.einsum(
        "sdl,fd->sfl", grad_mlp_all, contract_all, preferred_element_type=jnp.float32
    )
    grad_pre = jax.vjp(gelu_tanh, pre_act)[1](grad_hidden)[0]
    grad_pre_b = grad_pre.astype(jnp.bfloat16)
    expand_term = jnp.einsum(
        "sdl,sfl->df", in_second, grad_pre_b, preferred_element_type=jnp.float32
    )
    grad_in_second = sum_cols(
        jnp.einsum("sfl,df->sdl", grad_pre_b, expand_all, preferred_element_type=jnp.float32)
    )
    grad_residual = grad_out + norm_backward(
        grad_in_second * (1.0 + scale_second), normed_second, inv_second
    )
    grad_proj_out = grad_residual * gate_first
    grad_proj_all = gather_cols(grad_proj_out.astype(jnp.bfloat16))
    proj_term = jnp.einsum(
        "sel,sdl->ed", attended, grad_proj_all, preferred_element_type=jnp.float32
    )
    grad_att = jnp.einsum(
        "sdl,ed->sel", grad_proj_all, proj_all, preferred_element_type=jnp.float32
    ).astype(jnp.bfloat16)
    soft = jnp.exp(score_block(query_heads, key_heads) - log_total)
    soft_again = soft.astype(jnp.bfloat16)
    grad_att_heads = split_heads(grad_att)
    grad_value_heads = jnp.einsum(
        "shqk,shdq->shdk", soft_again, grad_att_heads, preferred_element_type=jnp.float32
    )
    grad_soft = jnp.einsum(
        "shdq,shdk->shqk", grad_att_heads, value_heads, preferred_element_type=jnp.float32
    )
    row_delta = jnp.einsum(
        "shdq,shdq->shq", grad_att_heads, split_heads(attended), preferred_element_type=jnp.float32
    )[..., None]
    grad_scores = (soft * (grad_soft - row_delta)).astype(jnp.bfloat16)
    grad_query = (
        jnp.einsum(
            "shqk,shdk->shdq", grad_scores, key_heads, preferred_element_type=jnp.float32
        ).reshape(seq_count, col_width, length)
        * score_scale
    )
    grad_keys = (
        jnp.einsum(
            "shqk,shdq->shdk", grad_scores, query_heads, preferred_element_type=jnp.float32
        ).reshape(seq_count, col_width, length)
        * score_scale
    )
    grad_values = grad_value_heads.reshape(seq_count, col_width, length)
    grad_triple = (
        jnp.stack((grad_query, grad_keys, grad_values), axis=1)
        .astype(jnp.bfloat16)
        .reshape(seq_count, 3 * col_width, length)
    )
    triple_term = jnp.einsum(
        "sdl,scl->dc", in_first, grad_triple, preferred_element_type=jnp.float32
    ).reshape(D, 3, col_width)
    grad_in_first = sum_cols(
        jnp.einsum("scl,dc->sdl", grad_triple, triple_all, preferred_element_type=jnp.float32)
    )
    grad_latents = grad_residual + norm_backward(
        grad_in_first * (1.0 + scale_first), normed_first, inv_first
    )
    grad_offsets = jnp.stack(
        (
            jnp.sum(grad_in_first, axis=2),
            jnp.sum(grad_in_first * normed_first, axis=2),
            jnp.sum(grad_residual * proj_out, axis=2),
            jnp.sum(grad_in_second, axis=2),
            jnp.sum(grad_in_second * normed_second, axis=2),
            jnp.sum(grad_out * mlp_out, axis=2),
        ),
        axis=1,
    )
    qv_term = jnp.stack((jnp.sum(grad_query, axis=(0, 2)), jnp.sum(grad_values, axis=(0, 2))))
    proj_bias_term = jnp.sum(grad_proj_out, axis=(0, 2))
    expand_bias_term = jnp.sum(grad_pre, axis=(0, 2))
    contract_bias_term = jnp.sum(grad_mlp, axis=(0, 2))
    flat_grad = grad_offsets.reshape(seq_count, 6 * col_width)
    ada_part = jnp.dot(
        flat_grad.T, silu_own.astype(jnp.float32), precision=lax.Precision.HIGHEST
    ).reshape(6, col_width, D)
    grad_ada, grad_ada_bias, grad_qv_bias, grad_proj_bias, grad_expand_bias, grad_contract_bias = (
        lax.psum(ada_part.astype(jnp.bfloat16), "row").astype(jnp.float32),
        lax.psum(jnp.sum(grad_offsets, axis=0).astype(jnp.bfloat16), "row").astype(jnp.float32),
        lax.psum(qv_term.astype(jnp.bfloat16), "row").astype(jnp.float32),
        lax.psum(proj_bias_term.astype(jnp.bfloat16), "row").astype(jnp.float32),
        lax.psum(expand_bias_term.astype(jnp.bfloat16), "row").astype(jnp.float32),
        lax.psum(contract_bias_term.astype(jnp.bfloat16), "row").astype(jnp.float32),
    )
    grad_qkv, grad_proj, grad_expand, grad_contract = (
        lax.psum_scatter(
            triple_term.astype(jnp.bfloat16), "row", scatter_dimension=0, tiled=True
        ).astype(jnp.float32),
        lax.psum_scatter(
            proj_term.astype(jnp.bfloat16), "row", scatter_dimension=1, tiled=True
        ).astype(jnp.float32),
        lax.psum_scatter(
            expand_term.astype(jnp.bfloat16), "row", scatter_dimension=0, tiled=True
        ).astype(jnp.float32),
        lax.psum_scatter(
            contract_term.astype(jnp.bfloat16), "row", scatter_dimension=1, tiled=True
        ).astype(jnp.float32),
    )
    silu_term = jnp.dot(flat_grad, flat_ada.astype(jnp.float32), precision=lax.Precision.HIGHEST)
    grad_silu = lax.psum_scatter(silu_term, "col", scatter_dimension=1, tiled=True)
    grad_cond = jax.vjp(jax.nn.silu, cond_own)[1](grad_silu)[0]
    grad_cond_all = lax.all_gather(grad_cond, "row", axis=0, tiled=True)
    grad_table = jnp.dot(
        grad_cond_all.T, label_hits.astype(jnp.float32), precision=lax.Precision.HIGHEST
    )
    return (
        block_out,
        grad_latents,
        grad_qkv,
        grad_qv_bias,
        grad_proj,
        grad_proj_bias,
        grad_expand,
        grad_expand_bias,
        grad_contract,
        grad_contract_bias,
        grad_ada,
        grad_ada_bias,
        grad_cond,
        grad_table,
    )


def solution(mesh):
    in_specs = (
        P("row", "col", None),
        P(),
        P(),
        P("col", None),
        P(None, "col", None),
        P(None, "col"),
        P("row", None, "col"),
        P(None, "col"),
        P("col", "row"),
        P("col"),
        P("row", "col"),
        P("col"),
        P("col", "row"),
        P("col"),
        P("row", "col", None),
    )
    out_specs = (
        P("row", "col", None),
        P("row", "col", None),
        P("row", None, "col"),
        P(None, "col"),
        P("col", "row"),
        P("col"),
        P("row", "col"),
        P("col"),
        P("col", "row"),
        P("col"),
        P(None, "col", None),
        P(None, "col"),
        P("row", "col"),
        P("col", None),
    )
    return jax.shard_map(
        on_device, mesh=mesh, in_specs=in_specs, out_specs=out_specs, check_vma=False
    )
```

profile of v0, /device:TPU:1, one launch (start us, length us, event | category | flops | bytes accessed | tf_op | source)
XLA Modules:
  0.0 1181.8 jit_solution(1575103412695717229)
XLA Ops:
  10.4 3.9 all-gather
  14.8 3.9 all-reduce.4
  18.6 5.9 fusion.76
  27.7 36.8 %all-gather.13.cloned.1.call-done = bf16[1152,3,576]{2,0,1:T(8,128)(2,1)} async-done(((bf16[72,3,576]{2,0,1:T(8,128)(2,1)}), bf16[1152,3,576]{2,0,1:T(8,128)(2,1)}) %all-gather.13.cloned.1.call-update) | async-done | bytes 3981328 | tf_op jit(solution)/shard_map/all_gather | solution.py:109
  64.5 6.8 copy.52
  71.3 29.3 %all-gather.11.cloned.1.call-done = bf16[1,1152,1024]{2,1,0:T(8,128)(2,1)} async-done(((bf16[1,576,1024]{2,1,0:T(8,128)(2,1)}), bf16[1,1152,1024]{2,1,0:T(8,128)(2,1)}) %all-gather.11.cloned.1.call-update) | async-done | bytes 2359312 | tf_op jit(solution)/shard_map/all_gather | solution.py:41
  100.7 7.2 fusion.57
  109.2 13.2 %multiply_reduce_fusion = (f32[8,1024]{1,0:T(8,128)S(1)}, f32[8,1024,1024]{1,2,0:T(8,128)}) fusion(bf16[8,72,1024]{2,1,0:T(8,128)(2,1)S(1)} %bitcast.203, f32[8,72,1024]{2,1,0:T(8,128)S(1)} %bitcast.195, f32[8,72]{1,0:T(8,128)S(1)} %reshape.555), kind=kOutput, calls=%fused_computation.4 | convolution fusion | flops 1225908224 | bytes 37128448 | tf_op jit(solution)/shard_map/shdq,shdk->shqk/dot_general | solution.py:55
  122.4 13.7 %exponential_reduce_fusion = f32[8,1024]{1,0:T(8,128)S(1)} fusion(f32[8,1024,1024]{1,2,0:T(8,128)} %get-tuple-element.94, f32[8,1024]{1,0:T(8,128)S(1)} %get-tuple-element.93), kind=kLoop, calls=%fused_computation.2 | loop fusion | flops 25157632 | bytes 33619968 | tf_op jit(solution)/shard_map/reduce_sum | solution.py:129
  136.2 13.9 %fusion.64 = bf16[8,72,1024]{2,1,0:T(8,128)(2,1)S(1)} fusion(f32[8,1024,1024]{1,2,0:T(8,128)} %get-tuple-element.94, f32[8,1024]{1,0:T(8,128)S(1)} %log_add_fusion, f32[8,72,1024]{2,1,0:T(8,128)S(1)} %bitcast.197, f32[8,72]{1,0:T(8,128)S(1)} %reshape.554), kind=kOutput, calls=%fused_computation.122 | convolution fusion | flops 1234894848 | bytes 37128448 | tf_op jit(solution)/shard_map/shqk,shdk->shdq/dot_general | solution.py:132
  150.2 4.0 fusion.15
  154.2 7.9 copy.75
  162.1 4.7 copy.116
  168.1 33.6 %reduce-scatter.28.cloned.1.call-done = bf16[576,1024]{1,0:T(8,128)(2,1)} async-done(((bf16[1152,1024]{1,0:T(8,128)(2,1)}), bf16[576,1024]{1,0:T(8,128)(2,1)}) %reduce-scatter.28.cloned.1.call-update) | async-done | bytes 1179664
  201.7 2.5 reshape_bitcast_fusion.3
  205.6 3.9 all-reduce.3
  216.0 44.7 %all-gather.19.cloned.1.call-done = bf16[1152,2304]{1,0:T(8,128)(2,1)} async-done(((bf16[72,2304]{1,0:T(8,128)(2,1)}), bf16[1152,2304]{1,0:T(8,128)(2,1)}) %all-gather.19.cloned.1.call-update) | async-done | bytes 5308432 | tf_op jit(solution)/shard_map/all_gather | solution.py:111
  260.7 36.1 %all-gather.17.cloned.1.call-done = bf16[1,1152,1024]{2,1,0:T(8,128)(2,1)} async-done(((bf16[1,576,1024]{2,1,0:T(8,128)(2,1)}), bf16[1,1152,1024]{2,1,0:T(8,128)(2,1)}) %all-gather.17.cloned.1.call-update) | async-done | bytes 2359312 | tf_op jit(solution)/shard_map/all_gather | solution.py:41
  296.7 11.6 fusion.55
  308.3 26.6 %all-gather.23.cloned.1.call-done = bf16[1,1152,1024]{2,1,0:T(8,128)(2,1)} async-done(((bf16[1,576,1024]{2,1,0:T(8,128)(2,1)}), bf16[1,1152,1024]{2,1,0:T(8,128)(2,1)}) %all-gather.23.cloned.1.call-update) | async-done | bytes 2359312 | tf_op jit(solution)/shard_map/all_gather | solution.py:41
  334.9 59.1 %all-gather.21.cloned.1.call-done = bf16[2304,1152]{0,1:T(8,128)(2,1)} async-done(((bf16[2304,72]{0,1:T(8,128)(2,1)}), bf16[2304,1152]{0,1:T(8,128)(2,1)}) %all-gather.21.cloned.1.call-update) | async-done | bytes 5308432 | tf_op jit(solution)/shard_map/all_gather | solution.py:112
  394.0 19.1 %fusion.98 = (bf16[2304]{0:T(1024)(128)(2,1)}, bf16[2304,1024]{0,1:T(8,128)(2,1)S(1)}) fusion(bf16[2304,1152]{0,1:T(8,128)(2,1)} %all-gather.21.cloned.1.call-done, bf16[1,1152,1024]{2,1,0:T(8,128)(2,1)} %all-gather.23.cloned.1.call-done, f32[1024,2304]{1,0:T(8,128)} %fusion.55, f32[2304]{0:T(1024)S(1)} %convert_element_type.288), kind=kOutput, calls=%fused_computation.186 | convolution fusion | flops 5497157632 | bytes 21837312 | tf_op jit(solution)/shard_map/sdl,fd->sfl/dot_general | solution.py:163
  413.1 2.2 copy-done.47
  415.3 10.2 fusion.18
  425.5 11.4 copy.79
  437.0 4.7 copy.114
  441.7 13.4 %fusion.17 = bf16[1,1152,1024]{1,2,0:T(8,128)(2,1)} fusion(bf16[2304,1152]{0,1:T(8,128)(2,1)} %all-gather.21.cloned.1.call-done, f32[1024,2304]{1,0:T(8,128)} %fusion.55, f32[2304]{0:T(1024)S(1)} %convert_element_type.288), kind=kOutput, calls=%fused_computation.53 | convolution fusion | flops 5460590592 | bytes 17114112 | tf_op jit(solution)/shard_map/sfl,fd->sdl/dot_general | solution.py:152
  455.1 11.5 copy.77
  466.6 4.8 copy.115
  474.6 2.5 reshape_bitcast_fusion.1
  477.1 2.5 fusion.39
  479.6 4.5 all-reduce.2
  486.7 25.4 %reduce-scatter.30.cloned.1.call-done = bf16[576,1024]{1,0:T(8,128)(2,1)} async-done(((bf16[1152,1024]{1,0:T(8,128)(2,1)}), bf16[576,1024]{1,0:T(8,128)(2,1)}) %reduce-scatter.30.cloned.1.call-update) | async-done | bytes 1179664
  512.1 2.6 reshape_bitcast_fusion.2
  514.8 5.3 fusion.38
  522.8 36.1 %all-gather.25.cloned.1.call-done = bf16[1,1152,1024]{2,1,0:T(8,128)(2,1)} async-done(((bf16[1,576,1024]{2,1,0:T(8,128)(2,1)}), bf16[1,1152,1024]{2,1,0:T(8,128)(2,1)}) %all-gather.25.cloned.1.call-update) | async-done | bytes 2359312 | tf_op jit(solution)/shard_map/all_gather | solution.py:41
  558.9 3.8 fusion.61
  563.8 15.9 %fusion.97 = (bf16[8,72]{1,0:T(8,128)(2,1)}, bf16[8,72,1024]{2,1,0:T(8,128)(2,1)}) fusion(bf16[8,72,1024]{2,1,0:T(8,128)(2,1)S(1)} %bitcast.206, f32[8,1024,1024]{1,2,0:T(8,128)} %get-tuple-element.94, f32[8,1024]{1,0:T(8,128)S(1)} %copy-done.23), kind=kOutput, calls=%fused_computation.185 | convolution fusion | flops 1234304512 | bytes 35947648 | tf_op jit(solution)/shard_map/shqk,shdq->shdk/dot_general | solution.py:188
  579.7 22.4 %multiply_convert_fusion = bf16[8,1024,1024]{1,2,0:T(8,128)(2,1)} fusion(f32[8,1024,1024]{1,2,0:T(8,128)} %get-tuple-element.94, f32[8,1024]{1,0:T(8,128)} %fusion.48, f32[8,1024]{1,0:T(8,128)} %copy-done.22, bf16[8,72,1024]{2,1,0:T(8,128)(2,1)S(1)} %bitcast.207, f32[8,72,1024]{2,1,0:T(8,128)} %bitcast.198, f32[8,72]{1,0:T(8,128)S(1)} %reshape.554), kind=kOutput, calls=%fused_computation | convolution fusion | flops 1251082240 | bytes 53938432 | tf_op jit(solution)/shard_map/shdq,shdk->shqk/dot_general | solution.py:191
  602.2 12.1 %multiply_convert_fusion.3 = bf16[8,72,1024]{2,1,0:T(8,128)(2,1)} fusion(bf16[8,1024,1024]{1,2,0:T(8,128)(2,1)} %multiply_convert_fusion, f32[8,72,1024]{2,1,0:T(8,128)S(1)} %bitcast.196, f32[8,72]{1,0:T(8,128)S(1)} %reshape.555), kind=kOutput, calls=%fused_computation.106 | convolution fusion | flops 1210318848 | bytes 20318464 | tf_op jit(solution)/shard_map/shqk,shdq->shdk/dot_general | solution.py:205
  614.2 9.6 multiply_reduce_fusion.3
  626.0 6.4 fusion.16
  632.4 11.3 copy.81
  643.8 4.7 copy.113
  649.1 11.4 convolution_convert_fusion
  660.7 10.1 convolution_convert_fusion.1
  672.0 4.8 convolution_convert_fusion.7
  683.4 2.5 reshape_bitcast_fusion
  685.9 2.7 fusion.40
  692.6 12.1 %convolution_bitcast_fusion = f32[1152,1]{1,0:T(8,128)} fusion(f32[3456,1]{0,1:T(1,128)} %reshape.568, bf16[3456,1152]{1,0:T(8,128)(2,1)} %bitcast.194), kind=kOutput, calls=%fused_computation.64 | convolution fusion | flops 47775744 | bytes 7981056
  705.0 7.1 convolution_convert_fusion.2
  712.1 18.2 %copy.83 = bf16[1152,3,576]{2,1,0:T(4,128)(2,1)} copy(bf16[1152,3,576]{2,0,1:T(8,128)(2,1)S(1)} %convolution_convert_fusion.2) | data formatting | bytes 7962624
  730.3 12.3 %reshape.581 = bf16[1152,1728]{1,0:T(8,128)(2,1)} reshape(bf16[1152,3,576]{2,1,0:T(4,128)(2,1)} %copy.83) | data formatting | bytes 7962624
  743.4 4.2 multiply_convert_fusion.1
  751.8 12.4 %reduce-scatter.26.cloned.1.call-done = bf16[2304,72]{0,1:T(8,128)(2,1)} async-done(((bf16[2304,1152]{0,1:T(8,128)(2,1)}), bf16[2304,72]{0,1:T(8,128)(2,1)}) %reduce-scatter.26.cloned.1.call-update) | async-done | bytes 331792 | tf_op jit(solution)/shard_map/reduce_scatter | solution.py:262
  766.1 79.1 %reduce-scatter.24.cloned.1.call-done = bf16[72,2304]{1,0:T(8,128)(2,1)} async-done(((bf16[1152,2304]{1,0:T(8,128)(2,1)}), bf16[72,2304]{1,0:T(8,128)(2,1)}) %reduce-scatter.24.cloned.1.call-update) | async-done | bytes 331792 | tf_op jit(solution)/shard_map/reduce_scatter | solution.py:259
  847.1 58.3 %reduce-scatter.40.cloned.1.call-done = bf16[576,72]{0,1:T(8,128)(2,1)} async-done(((bf16[576,1152]{0,1:T(8,128)(2,1)}), bf16[576,72]{0,1:T(8,128)(2,1)}) %reduce-scatter.40.cloned.1.call-update) | async-done | bytes 82960
  908.2 55.8 %all-reduce.5 = (bf16[2,576]{1,0:T(2,128)(2,1)}, bf16[576]{0:T(1024)(128)(2,1)}, bf16[2304]{0:T(1024)(128)(2,1)}, bf16[576]{0:T(1024)(128)(2,1)}, bf16[6,576]{1,0:T(8,128)(2,1)}) all-reduce(bf16[2,576]{1,0:T(2,128)(2,1)} %pad_maximum_fusion.1, bf16[576]{0:T(1024)(128)(2,1)} %get-tuple-element.86, ...), channel_id=1, replica_groups=mesh['row'=16,'col'=2] {'row'}, use_global_device_ids=true, to_apply=%region_25.26 | all-reduce | flops 8064 | bytes 32256 | tf_op jit(solution)/shard_map/psum | solution.py:247
  970.5 4.9 all-reduce.1
  976.8 3.5 fusion.33
  982.2 23.0 %all-gather.1 = f32[16,1,576]{2,1,0:T(1,128)S(1)} all-gather(f32[1,1,576]{2,1,0:T(1,128)S(1)} %bitcast.249), channel_id=1, replica_groups=mesh['row'=16,'col'=2] {'row'}, dimensions={0}, use_global_device_ids=true | all-gather | bytes 39168 | tf_op jit(solution)/shard_map/all_gather | solution.py:269
  1005.2 2.7 fusion.68
  1009.9 154.5 %all-reduce.8.cloned.1.call-done = bf16[6,576,1152]{2,1,0:T(8,128)(2,1)} async-done(((bf16[6,576,1152]{2,1,0:T(8,128)(2,1)}), bf16[6,576,1152]{2,1,0:T(8,128)(2,1)}) %all-reduce.8.cloned.1.call-update) | async-done | bytes 7962640 | tf_op jit(solution)/shard_map/psum | solution.py:245
  1164.4 10.3 convert_element_type.327
  (197 shorter events, 65.0 us)
Async XLA Ops:
  7.2 1.5 copy-start
  7.2 7.2 copy-start.2
  7.2 57.3 %all-gather.13.cloned.1.call-start = ((), (), s32[]{:S(2)}) async-start(), calls=%async_computation.10 | async-start | bytes 4700160 | tf_op jit(solution)/shard_map/all_gather | solution.py:109
  7.9 92.7 %all-gather.11.cloned.1.call-start = ((), (), s32[]{:S(2)}) async-start(), calls=%async_computation.9 | async-start | bytes 3538944 | tf_op jit(solution)/shard_map/all_gather | solution.py:41
  14.4 10.1 copy-start.36
  18.6 5.9 copy-start.42
  24.5 3.0 copy-start.41
  25.2 46.1 %copy-start.28 = (f32[576]{0:T(1024)}, f32[576]{0:T(1024)S(1)}, u32[]{:S(2)}) copy-start(f32[576]{0:T(1024)S(1)} %get-tuple-element.62) | copy-start | bytes 6916
  25.2 179.1 %copy-start.34 = (f32[576]{0:T(1024)}, f32[576]{0:T(1024)S(1)}, u32[]{:S(2)}) copy-start(f32[576]{0:T(1024)S(1)} %get-tuple-element.63) | copy-start | bytes 6916
  25.2 46.1 %copy-start.26 = (f32[1,1024]{1,0:T(1,128)}, f32[1,1024]{1,0:T(1,128)S(1)}, u32[]{:S(2)}) copy-start(f32[1,1024]{1,0:T(1,128)S(1)} %get-tuple-element.99) | copy-start | bytes 12292
  25.2 46.1 %copy-start.30 = (f32[1024]{0:T(1024)}, f32[1024]{0:T(1024)S(1)}, u32[]{:S(2)}) copy-start(f32[1024]{0:T(1024)S(1)} %add_rsqrt_fusion.1) | copy-start | bytes 12292
  26.7 123.5 %all-gather.15.cloned.1.call-start = ((), (), s32[]{:S(2)}) async-start(), calls=%async_computation.11 | async-start | bytes 1566720 | tf_op jit(solution)/shard_map/all_gather | solution.py:110
  27.4 174.3 %reduce-scatter.28.cloned.1.call-start = ((), (), s32[]{:S(2)}) async-start(), calls=%async_computation.20 | async-start | bytes 3538944
  108.0 1.2 copy-start.12
  108.7 13.7 %copy-start.5 = (f32[1,1,576,1024]{3,2,1,0:T(8,128)}, f32[1,1,576,1024]{3,2,1,0:T(8,128)S(1)}, u32[]{:S(2)}) copy-start(f32[1,1,576,1024]{3,2,1,0:T(8,128)S(1)} %get-tuple-element.84) | copy-start | bytes 7077892
  108.8 27.4 %copy-start.7 = (f32[1,1,576,1024]{3,2,1,0:T(8,128)}, f32[1,1,576,1024]{3,2,1,0:T(8,128)S(1)}, u32[]{:S(2)}) copy-start(f32[1,1,576,1024]{3,2,1,0:T(8,128)S(1)} %get-tuple-element.83) | copy-start | bytes 7077892
  136.2 14.0 %copy-start.22 = (f32[8,1024]{1,0:T(8,128)}, f32[8,1024]{1,0:T(8,128)S(1)}, u32[]{:S(2)}) copy-start(f32[8,1024]{1,0:T(8,128)S(1)} %log_add_fusion) | copy-start | bytes 98308
  150.1 4.0 copy-start.15
  166.8 0.7 copy-start.44
  166.8 37.4 %copy-start.3 = (bf16[1,576,1024]{2,1,0:T(8,128)(2,1)S(1)}, bf16[1,576,1024]{2,1,0:T(8,128)(2,1)}, u32[]{:S(2)}) copy-start(bf16[1,576,1024]{2,1,0:T(8,128)(2,1)} %param.15) | copy-start | bytes 3538948
  166.8 93.8 %all-gather.19.cloned.1.call-start = ((), (), s32[]{:S(2)}) async-start(), calls=%async_computation.13 | async-start | bytes 5640192 | tf_op jit(solution)/shard_map/all_gather | solution.py:111
  167.4 129.3 %all-gather.17.cloned.1.call-start = ((), (), s32[]{:S(2)}) async-start(), calls=%async_computation.12 | async-start | bytes 3538944 | tf_op jit(solution)/shard_map/all_gather | solution.py:41
  201.7 2.5 copy-start.37
  204.2 1.4 copy-start.10
  210.2 2.3 copy-start.18
  212.4 122.5 %all-gather.23.cloned.1.call-start = ((), (), s32[]{:S(2)}) async-start(), calls=%async_computation.15 | async-start | bytes 3538944 | tf_op jit(solution)/shard_map/all_gather | solution.py:41
  214.5 179.6 %all-gather.21.cloned.1.call-start = ((), (), s32[]{:S(2)}) async-start(), calls=%async_computation.14 | async-start | bytes 5640192 | tf_op jit(solution)/shard_map/all_gather | solution.py:112
  215.2 259.4 %reduce-scatter.32.cloned.1.call-start = ((), (), s32[]{:S(2)}) async-start(), calls=%async_computation.22 | async-start | bytes 3538944
  216.0 225.8 %copy-start.39 = (f32[2304]{0:T(1024)}, f32[2304]{0:T(1024)S(1)}, u32[]{:S(2)}) copy-start(f32[2304]{0:T(1024)S(1)} %convert_element_type.288) | copy-start | bytes 27652
  413.1 2.2 copy-start.47
  441.7 70.4 %reduce-scatter.30.cloned.1.call-start = ((), (), s32[]{:S(2)}) async-start(), calls=%async_computation.21 | async-start | bytes 3538944
  471.4 0.7 copy-start.45
  471.4 87.6 %all-gather.25.cloned.1.call-start = ((), (), s32[]{:S(2)}) async-start(), calls=%async_computation.16 | async-start | bytes 3538944 | tf_op jit(solution)/shard_map/all_gather | solution.py:41
  512.1 2.6 copy-start.11
  512.1 2.7 copy-start.19
  512.1 2.7 copy-start.33
  514.8 6.7 copy-start.35
  520.1 1.4 copy-start.8
  522.7 40.0 %copy-start.16 = (bf16[8,72,1024]{2,1,0:T(8,128)(2,1)S(1)}, bf16[8,72,1024]{2,1,0:T(8,128)(2,1)}, u32[]{:S(2)}) copy-start(bf16[8,72,1024]{2,1,0:T(8,128)(2,1)} %copy-done.15) | copy-start | bytes 3538948
  522.7 160.7 %reduce-scatter.34.cloned.1.call-start = ((), (), s32[]{:S(2)}) async-start(), calls=%async_computation.23 | async-start | bytes 3538944
  562.8 1.1 copy-start.23
  579.7 22.4 %copy-start.6 = (f32[1,1,576,1024]{3,2,1,0:T(8,128)S(1)}, f32[1,1,576,1024]{3,2,1,0:T(8,128)}, u32[]{:S(2)}) copy-start(f32[1,1,576,1024]{3,2,1,0:T(8,128)} %copy-done.5) | copy-start | bytes 7077892
  602.1 12.1 %copy-start.13 = (bf16[1,1,576,1024]{3,2,1,0:T(8,128)(2,1)S(1)}, bf16[1,1,576,1024]{3,2,1,0:T(8,128)(2,1)}, u32[]{:S(2)}) copy-start(bf16[1,1,576,1024]{3,2,1,0:T(8,128)(2,1)} %copy-done.12) | copy-start | bytes 3538948
  614.2 9.7 copy-start.14
  614.2 9.7 copy-start.20
  623.9 2.1 copy-start.21
  648.4 0.7 copy-start.40
  648.5 115.7 %reduce-scatter.26.cloned.1.call-start = ((), (), s32[]{:S(2)}) async-start(), calls=%async_computation.18 | async-start | bytes 5640192 | tf_op jit(solution)/shard_map/reduce_scatter | solution.py:262
  660.6 184.6 %reduce-scatter.24.cloned.1.call-start = ((), (), s32[]{:S(2)}) async-start(), calls=%async_computation.17 | async-start | bytes 5640192 | tf_op jit(solution)/shard_map/reduce_scatter | solution.py:259
  670.7 1.3 copy-start.17
  670.7 7.7 copy-start.38
  670.7 234.6 %reduce-scatter.40.cloned.1.call-start = ((), (), s32[]{:S(2)}) async-start(), calls=%async_computation.26 | async-start | bytes 1566720
  676.8 9.1 copy-start.4
  676.8 9.1 copy-start.27
  676.8 9.1 copy-start.29
  676.8 9.1 copy-start.31
  676.8 303.5 %reduce-scatter.38.cloned.1.call-start = ((), (), s32[]{:S(2)}) async-start(), calls=%async_computation.25 | async-start | bytes 884736
  704.7 303.2 %reduce-scatter.36.cloned.1.call-start = ((), (), s32[]{:S(2)}) async-start(), calls=%async_computation.24 | async-start | bytes 4386816
  742.6 0.8 copy-start.24
  742.6 421.8 %all-reduce.8.cloned.1.call-start = ((), (), s32[]{:S(2)}) async-start(), calls=%async_computation.19 | async-start | bytes 15925248 | tf_op jit(solution)/shard_map/psum | solution.py:245
  747.7 229.1 %copy-start.9 = (f32[1,576,1024]{2,1,0:T(8,128)S(1)}, f32[1,576,1024]{2,1,0:T(8,128)}, u32[]{:S(2)}) copy-start(f32[1,576,1024]{2,1,0:T(8,128)} %copy-done.8) | copy-start | bytes 7077892
  976.8 28.4 %copy-start.46 = (s32[16]{0:T(128)S(1)}, s32[16]{0:T(128)}, u32[]{:S(2)}) copy-start(s32[16]{0:T(128)} %param.16) | copy-start | bytes 196
  982.2 192.5 %copy-start.43 = (f32[1,576]{1,0:T(1,128)}, f32[1,576]{1,0:T(1,128)S(1)}, u32[]{:S(2)}) copy-start(f32[1,576]{1,0:T(1,128)S(1)} %fusion.87) | copy-start | bytes 6916
  1164.4 10.3 copy-start.1
  (2 other events, 1.2 us)
Sparse Core Ops, SparseCore 0:
  10.2 54.2 all-gather.12
  66.6 33.9 all-gather.10
  102.8 39.7 all-gather.14
  166.9 34.7 reduce-scatter.27
  203.7 56.8 all-gather.18
  262.6 34.0 all-gather.16
  298.8 36.0 all-gather.22
  337.1 56.8 all-gather.20
  441.8 32.8 reduce-scatter.31
  477.3 34.7 reduce-scatter.29
  522.9 36.0 all-gather.24
  648.6 34.7 reduce-scatter.33
  687.4 76.7 reduce-scatter.25
  768.1 77.0 reduce-scatter.23
  848.8 56.4 reduce-scatter.39
  907.5 16.0 reduce-scatter.37
  927.3 69.4 reduce-scatter.35
  1000.9 163.4 all-reduce.7
where the time goes:
time: 1190 us; the launch traced here: 1180 us
  waiting for transfers between devices  638 us (54%)
  matrix products  218 us (18%)
  local copies, waits for them, and re-layouts  133 us (11%)
  blocking collectives  99.9 us (8%)
  other arithmetic  75.4 us (6%)
  between operations  15.2 us (1%)
    psum x1, waiting for transfers between devices, on_device(): lax.psum(ada_part.astype(jnp.bfloat16), 'row').astype(jnp.float32)  154 us
    all_gather x4, waiting for transfers between devices, gather_cols(): return lax.all_gather(values, 'col', axis=1, tiled=True)  128 us
    unnamed x25, waiting for transfers between devices  124 us
    unnamed x113, local copies, waits for them, and re-layouts  113 us
    reduce_scatter x1, waiting for transfers between devices, on_device(): lax.psum_scatter(expand_term.astype(jnp.bfloat16), 'row', scatter_dimensi...  79.1 us
    all_gather x1, waiting for transfers between devices, on_device(): lax.all_gather(contract_weight, 'row', axis=1, tiled=True)  59.1 us
    psum x1, blocking collectives, on_device(): lax.psum(qv_term.astype(jnp.bfloat16), 'row').astype(jnp.float32)  55.8 us
    all_gather x1, waiting for transfers between devices, on_device(): lax.all_gather(expand_weight, 'row', axis=0, tiled=True)  44.7 us
  transfers between devices with their start and end apart: 18, of which 15 were waited for; matrix products, arithmetic and copies ran while one was open for 21% of the time, Pallas kernels for 0%

commit v1 on v0

v1 whole, which is shorter than its diff:
```python
import math

import jax
import jax.numpy as jnp
from jax import lax
from jax.sharding import PartitionSpec as P

D = 1152
HEAD = 72
CLASSES = 1001
EPSILON = 1e-06
GELU_COEF = 0.7978845608028654
AXES = ("row", "col")
F32 = jnp.float32
BF16 = jnp.bfloat16
HIGH = lax.Precision.HIGHEST


def gelu_tanh(values):
    return (
        0.5 * values * (1.0 + jnp.tanh(GELU_COEF * (values + 0.044715 * values * values * values)))
    )


def mm(left, right):
    return lax.dot_general(left, right, (((1,), (0,)), ((), ())), preferred_element_type=F32)


def mm_tn(left, right):
    return lax.dot_general(left, right, (((0,), (0,)), ((), ())), preferred_element_type=F32)


def mm_nt(left, right):
    return lax.dot_general(left, right, (((1,), (1,)), ((), ())), preferred_element_type=F32)


class Links:
    def __init__(self, rows, cols):
        self.count = rows * cols
        self.col_bits = cols.bit_length() - 1
        self.row_bits = rows.bit_length() - 1
        self.flat = lax.axis_index("row") * cols + lax.axis_index("col")
        self.x = 0
        self.ch = list(range(1, self.col_bits))
        self.core = self.col_bits
        self.rh = list(range(self.core + 1, self.core + self.row_bits))[::-1]
        self.order = {
            "a": self.rh + [self.x],
            "b": self.rh[:-1] + [self.x] + self.rh[-1:],
        }

    def bit(self, which):
        return (self.flat >> which) & 1

    def exchange(self, values, which):
        pairs = [(i, i ^ (1 << which)) for i in range(self.count)]
        return lax.ppermute(values, AXES, pairs)

    def swap(self, values):
        low, high = 1, 1 << self.core
        pairs = []
        for i in range(self.count):
            kept = i & ~(low | high)
            pairs.append((i, kept | (high if i & low else 0) | (low if i & high else 0)))
        return lax.ppermute(values, AXES, pairs)

    def joined(self, mine, theirs, which):
        low = self.bit(which) == 0
        return jnp.where(low, jnp.stack([mine, theirs]), jnp.stack([theirs, mine]))

    def gather(self, values, order):
        for which in order:
            values = self.joined(values, self.exchange(values, which), which)
        return values

    def gather_rows(self, values, stream):
        order = self.order[stream]
        natural = self.rh + [self.x]
        got = self.gather(values, order)
        have = order[::-1]
        tail = list(range(len(have), got.ndim))
        got = got.transpose([have.index(w) for w in natural] + tail)
        return got.reshape((-1,) + values.shape[1:])

    def scatter_rows(self, values, stream, rows):
        natural = self.rh + [self.x]
        sums = values.reshape((2,) * len(natural) + (values.shape[0] // rows,) + values.shape[1:])
        for which in self.order[stream][::-1]:
            axis = natural.index(which)
            natural = natural[:axis] + natural[axis + 1 :]
            own = self.bit(which)
            sent = lax.dynamic_index_in_dim(sums, 1 - own, axis, keepdims=False)
            kept = lax.dynamic_index_in_dim(sums, own, axis, keepdims=False)
            sums = kept + self.exchange(sent, which)
        return sums

    def gather_pair(self, values):
        got = self.gather(values, [self.core] + self.ch)
        return got.reshape((-1,) + values.shape[1:])

    def sum_pair(self, values):
        for which in [self.core] + self.ch:
            values = values + self.exchange(values.astype(BF16), which).astype(F32)
        return values


def norm_forward(values):
    average = jnp.mean(values, axis=0, keepdims=True)
    spread = jnp.mean(values * values, axis=0, keepdims=True) - average * average
    inverse = lax.rsqrt(spread + EPSILON)
    return (values - average) * inverse, inverse


def norm_backward(grad_normed, normed, inverse):
    first = jnp.mean(grad_normed, axis=0, keepdims=True)
    cross = jnp.mean(grad_normed * normed, axis=0, keepdims=True)
    return inverse * (grad_normed - first - normed * cross)


def heads_of(values):
    return values.reshape(values.shape[0] // HEAD, HEAD, values.shape[1])


def attend(query, key, value):
    scale = 1.0 / math.sqrt(HEAD)
    query, key, value = heads_of(query), heads_of(key), heads_of(value)
    scores = jnp.einsum("hdk,hdq->hkq", key, query, preferred_element_type=F32) * scale
    top = jnp.max(scores, axis=1, keepdims=True)
    log_total = jnp.log(jnp.sum(jnp.exp(scores - top), axis=1, keepdims=True)) + top
    soft_b = jnp.exp(scores - log_total).astype(BF16)
    out = jnp.einsum("hdk,hkq->hdq", value, soft_b, preferred_element_type=F32)
    return out.reshape(-1, out.shape[2]).astype(BF16), log_total


def attend_back(query, key, value, log_total, attended, grad_att):
    scale = 1.0 / math.sqrt(HEAD)
    query, key, value = heads_of(query), heads_of(key), heads_of(value)
    attended, grad_att = heads_of(attended), heads_of(grad_att)
    scores = jnp.einsum("hdk,hdq->hkq", key, query, preferred_element_type=F32) * scale
    soft = jnp.exp(scores - log_total)
    soft_b = soft.astype(BF16)
    grad_value = jnp.einsum("hkq,hdq->hdk", soft_b, grad_att, preferred_element_type=F32)
    grad_soft = jnp.einsum("hdk,hdq->hkq", value, grad_att, preferred_element_type=F32)
    delta = jnp.sum(grad_att.astype(F32) * attended.astype(F32), axis=1, keepdims=True)
    grad_scores = (soft * (grad_soft - delta)).astype(BF16)
    grad_query = jnp.einsum("hdk,hkq->hdq", key, grad_scores, preferred_element_type=F32) * scale
    grad_key = jnp.einsum("hdq,hkq->hdk", query, grad_scores, preferred_element_type=F32) * scale
    flat = lambda v: v.reshape(-1, v.shape[2])
    return flat(grad_query), flat(grad_key), flat(grad_value)


def make_on_device(rows, cols):
    def on_device(
        latents,
        labels,
        timesteps,
        label_table,
        ada_weight,
        ada_bias,
        qkv_weight,
        qv_bias,
        proj_weight,
        proj_bias,
        expand_weight,
        expand_bias,
        contract_weight,
        contract_bias,
        cotangent,
    ):
        links = Links(rows, cols)
        length = latents.shape[2]
        width = latents.shape[1]
        half = width // 2
        hidden_width = expand_weight.shape[1]
        hidden_half = hidden_width // 2
        seqs = labels.shape[0]
        chunk = qkv_weight.shape[0]
        row, col = lax.axis_index("row"), lax.axis_index("col")
        own_x, own_core = links.bit(links.x), links.bit(links.core)
        part = (col >> 1 << 1) + own_core

        qkv_own = links.swap(qkv_weight.reshape(chunk, 3 * width)).reshape(chunk, 3, width)
        streams = ("a", "b")
        qkv_w = [
            links.gather_rows(qkv_own[:, :, i * half : (i + 1) * half].reshape(chunk, 3 * half), s)
            for i, s in enumerate(streams)
        ]
        latents_own = links.swap(latents[0])
        latents_full = links.gather_pair(latents_own)
        proj_own = links.swap(proj_weight.T)
        proj_w = [
            links.gather_rows(proj_own[:, i * half : (i + 1) * half], s)
            for i, s in enumerate(streams)
        ]
        expand_own = links.swap(expand_weight)
        expand_w = [
            links.gather_rows(expand_own[:, i * hidden_half : (i + 1) * hidden_half], s)
            for i, s in enumerate(streams)
        ]
        contract_own = links.swap(contract_weight.T)
        contract_w = [
            links.gather_rows(contract_own[:, i * hidden_half : (i + 1) * hidden_half], s)
            for i, s in enumerate(streams)
        ]
        cotangent_full = links.gather_pair(links.swap(cotangent[0]))
        bias_rows = [
            qv_bias.astype(F32),
            proj_bias.astype(F32)[None],
            contract_bias.astype(F32)[None],
            expand_bias.astype(F32).reshape(-1, width),
        ]
        bias_own = links.swap(jnp.concatenate(bias_rows, axis=0))
        qv_own = bias_own[:2, :, None]
        pair_bias = links.gather([bias_own[2:4]][0], [links.core] + links.ch)
        pair_bias = pair_bias.reshape(-1, 2, width).transpose(1, 0, 2).reshape(2, D, 1)
        proj_b, contract_b = pair_bias[0], pair_bias[1]
        expand_b = bias_own[4:].reshape(hidden_width, 1)

        feature = col * width + jnp.arange(width, dtype=jnp.int32)
        half_width = D // 2
        frequency = jnp.exp(-math.log(10000.0) * (feature % half_width).astype(F32) / half_width)
        angles = timesteps.astype(F32)[:, None] * frequency[None, :]
        embedding = jnp.where(feature[None, :] < half_width, jnp.cos(angles), jnp.sin(angles))
        label_hits = labels[:, None] == jnp.arange(CLASSES, dtype=jnp.int32)[None, :]
        cond_part = mm_nt(label_hits.astype(BF16), label_table) + embedding
        cond_all = links.gather(cond_part, [links.x] + links.ch)
        cond_all = cond_all.reshape(-1, seqs, width).transpose(1, 0, 2).reshape(seqs, D)
        silu_all = jax.nn.silu(cond_all).astype(BF16)
        flat_ada = ada_weight.reshape(6 * width, D)
        pair = lax.dynamic_slice_in_dim(silu_all, (row >> 1) * 2, 2, 0)
        pair_mod = mm_nt(pair, flat_ada) + ada_bias.astype(F32).reshape(1, 6 * width)
        mine = lax.dynamic_index_in_dim(pair_mod, own_x, 0)
        other = lax.dynamic_index_in_dim(pair_mod, 1 - own_x, 0)
        mod = links.joined(mine, links.exchange(other, links.x), links.x)
        mod = links.gather(mod, links.ch)
        mod = mod.reshape(-1, 6, width).transpose(1, 0, 2).reshape(6, D, 1)
        shift_first, scale_first, gate_first, shift_second, scale_second, gate_second = [
            mod[i] for i in range(6)
        ]
        own_part = lambda v: lax.dynamic_slice_in_dim(v, part * width, width, 0)

        start = latents_full.astype(F32)
        normed_first, inv_first = norm_forward(start)
        in_first = (normed_first * (1.0 + scale_first) + shift_first).astype(BF16)
        heads = []
        for i in range(2):
            triple = mm_tn(qkv_w[i], in_first)
            qb, vb = [qv_own[j, i * half : (i + 1) * half] for j in range(2)]
            query = (triple[:half] + qb).astype(BF16)
            key = triple[half : 2 * half].astype(BF16)
            value = (triple[2 * half :] + vb).astype(BF16)
            heads.append((query, key, value) + attend(query, key, value))
        proj_out = (
            links.sum_pair(sum(mm(proj_w[i], heads[i][3]) for i in range(2))) + proj_b
        )
        residual = start + gate_first * proj_out
        normed_second, inv_second = norm_forward(residual)
        in_second = (normed_second * (1.0 + scale_second) + shift_second).astype(BF16)
        pre_act = [
            mm_tn(expand_w[i], in_second) + expand_b[i * hidden_half : (i + 1) * hidden_half]
            for i in range(2)
        ]
        hidden = [gelu_tanh(v).astype(BF16) for v in pre_act]
        mlp_out = links.sum_pair(sum(mm(contract_w[i], hidden[i]) for i in range(2))) + contract_b
        mlp_own = own_part(mlp_out)
        block_own = own_part(residual) + own_part(gate_second) * mlp_own
        block_out = links.swap(block_own.astype(BF16)).astype(F32)[None]

        grad_out = cotangent_full.astype(F32)
        grad_mlp_b = (grad_out * gate_second).astype(BF16)
        pre_grads = []
        grad_contract = []
        grad_expand = []
        for i in range(2):
            grad_contract.append(
                links.scatter_rows(mm_nt(grad_mlp_b, hidden[i]).astype(BF16), streams[i], rows)
            )
            grad_hidden = mm_tn(contract_w[i], grad_mlp_b)
            grad_pre = jax.vjp(gelu_tanh, pre_act[i])[1](grad_hidden)[0]
            pre_grads.append((grad_pre.astype(BF16), jnp.sum(grad_pre, axis=1)))
        for i in range(2):
            grad_expand.append(
                links.scatter_rows(mm_nt(in_second, pre_grads[i][0]).astype(BF16), streams[i], rows)
            )
        grad_in_second = links.sum_pair(sum(mm(expand_w[i], pre_grads[i][0]) for i in range(2)))
        grad_residual = grad_out + norm_backward(
            grad_in_second * (1.0 + scale_second), normed_second, inv_second
        )
        grad_proj_out = grad_residual * gate_first
        grad_proj_b = grad_proj_out.astype(BF16)
        grad_proj = []
        triple_grads = []
        qv_sums = []
        grad_qkv = []
        for i in range(2):
            query, key, value, attended, log_total = heads[i]
            grad_proj.append(
                links.scatter_rows(mm_nt(grad_proj_b, attended).astype(BF16), streams[i], rows)
            )
            grad_att = mm_tn(proj_w[i], grad_proj_b).astype(BF16)
            gq, gk, gv = attend_back(query, key, value, log_total, attended, grad_att)
            qv_sums.append((jnp.sum(gq, axis=1), jnp.sum(gv, axis=1)))
            triple_grads.append(jnp.concatenate([v.astype(BF16) for v in (gq, gk, gv)], axis=0))
            grad_qkv.append(
                links.scatter_rows(mm_nt(in_first, triple_grads[i]).astype(BF16), streams[i], rows)
            )
        grad_in_first = links.sum_pair(sum(mm(qkv_w[i], triple_grads[i]) for i in range(2)))
        grad_latents_full = grad_residual + norm_backward(
            grad_in_first * (1.0 + scale_first), normed_first, inv_first
        )
        grad_latents = links.swap(own_part(grad_latents_full).astype(BF16)).astype(F32)[None]

        token_sum = lambda v: jnp.sum(v, axis=1)[None]
        own_out = own_part(grad_out)
        own_in_second = own_part(grad_in_second)
        own_in_first = own_part(grad_in_first)
        early = jnp.concatenate(
            [
                token_sum(own_part(grad_residual) * own_part(proj_out)),
                token_sum(own_in_second),
                token_sum(own_in_second * own_part(normed_second)),
                token_sum(own_out * mlp_own),
                token_sum(own_part(grad_proj_out)),
                token_sum(own_out * own_part(gate_second)),
                jnp.concatenate([p[1] for p in pre_grads]).reshape(-1, width),
            ],
            axis=0,
        )
        late = jnp.concatenate(
            [
                token_sum(own_in_first),
                token_sum(own_in_first * own_part(normed_first)),
                jnp.concatenate([s[0] for s in qv_sums])[None],
                jnp.concatenate([s[1] for s in qv_sums])[None],
            ],
            axis=0,
        )
        wide = lambda v: links.swap(links.gather_rows(v[None], "a"))
        early_all, late_all = wide(early), wide(late)
        grad_mod = jnp.concatenate([late_all[:, :2], early_all[:, :4]], axis=1)
        sums = jnp.sum(early_all[:, 4:], axis=0)
        grad_qv_bias = jnp.sum(late_all[:, 2:4], axis=0)
        grad_proj_bias, grad_contract_bias = sums[0], sums[1]
        grad_expand_bias = sums[2:].reshape(hidden_width)
        grad_ada_bias = jnp.sum(grad_mod, axis=0)
        flat_grad = grad_mod.reshape(seqs, 6 * width)
        grad_ada = lax.dot_general(
            flat_grad, silu_all.astype(F32), (((0,), (0,)), ((), ())), precision=HIGH
        ).reshape(6, width, D)
        grad_silu = jnp.dot(flat_grad, flat_ada.astype(F32), precision=HIGH)
        for which in [links.x] + links.ch:
            grad_silu = grad_silu + links.exchange(grad_silu, which)
        grad_cond_all = jax.vjp(jax.nn.silu, cond_all)[1](grad_silu)[0]
        grad_cond_cols = lax.dynamic_slice_in_dim(grad_cond_all, col * width, width, 1)
        grad_cond = lax.dynamic_slice_in_dim(grad_cond_cols, row, 1, 0)
        grad_table = lax.dot_general(
            grad_cond_cols, label_hits.astype(F32), (((0,), (0,)), ((), ())), precision=HIGH
        )

        back = lambda v: links.swap(jnp.concatenate(v, axis=1)).astype(F32)
        qkv_parts = [v.reshape(chunk, 3, half) for v in grad_qkv]
        qkv_back = jnp.concatenate(qkv_parts, axis=2).reshape(chunk, 3 * width)
        grad_qkv = links.swap(qkv_back).astype(F32).reshape(chunk, 3, width)
        return (
            block_out,
            grad_latents,
            grad_qkv,
            grad_qv_bias,
            back(grad_proj).T,
            grad_proj_bias,
            back(grad_expand),
            grad_expand_bias,
            back(grad_contract).T,
            grad_contract_bias,
            grad_ada,
            grad_ada_bias,
            grad_cond,
            grad_table,
        )

    return on_device


def solution(mesh):
    in_specs = (
        P("row", "col", None),
        P(),
        P(),
        P("col", None),
        P(None, "col", None),
        P(None, "col"),
        P("row", None, "col"),
        P(None, "col"),
        P("col", "row"),
        P("col"),
        P("row", "col"),
        P("col"),
        P("col", "row"),
        P("col"),
        P("row", "col", None),
    )
    out_specs = (
        P("row", "col", None),
        P("row", "col", None),
        P("row", None, "col"),
        P(None, "col"),
        P("col", "row"),
        P("col"),
        P("row", "col"),
        P("col"),
        P("col", "row"),
        P("col"),
        P(None, "col", None),
        P(None, "col"),
        P("row", "col"),
        P("col", None),
    )
    return jax.shard_map(
        make_on_device(mesh.shape["row"], mesh.shape["col"]),
        mesh=mesh,
        in_specs=in_specs,
        out_specs=out_specs,
        check_vma=False,
    )
```

time: 1190 us -> 852 us (0.72)
  waiting for transfers between devices: 638 us -> 271 us
  starting transfers between devices: 1.6 us -> 174 us
  blocking collectives: 99.9 us -> 0 us
  local copies, waits for them, and re-layouts: 133 us -> 67.6 us
  other arithmetic: 75.4 us -> 121 us
  matrix products: 218 us -> 206 us
    ppermute x0 -> x97, waiting for transfers between devices: none -> 271 us  [the longest x82 261 us: exchange(): return lax.ppermute(values, AXES, pairs)]
    all_gather x8 -> x0, waiting for transfers between devices: 269 us -> none  [the longest x4 128 us: gather_cols(): return lax.all_gather(values, 'col', axis=1, tiled=True)]
    ppermute x0 -> x97, starting transfers between devices: none -> 174 us  [the longest x82 107 us: exchange(): return lax.ppermute(values, AXES, pairs)]
    psum x1 -> x0, waiting for transfers between devices: 154 us -> none  [on_device(): lax.psum(ada_part.astype(jnp.bfloat16), 'row').astype(jnp.float32)]
    unnamed x25 -> x0, waiting for transfers between devices: 124 us -> none
    unnamed x113 -> x260, local copies, waits for them, and re-layouts: 113 us -> 15.1 us
    reduce_scatter x2 -> x0, waiting for transfers between devices: 91.5 us -> none  [the longest x1 79.1 us: on_device(): lax.psum_scatter(expand_term.astype(jnp.bfloat16), 'row', scatter_dimensi...]
    psum x5 -> x0, blocking collectives: 73 us -> none  [the longest x1 55.8 us: on_device(): lax.psum(qv_term.astype(jnp.bfloat16), 'row').astype(jnp.float32)]
  transfers between devices with their start and end apart: 18 -> 97, of which waited for: 15 -> 45; matrix products, arithmetic and copies ran while one was open for 21% -> 39% of each run, Pallas kernels for 0% -> 0%
where the time goes in v1:
time: 852 us; the launch traced here: 844 us
  waiting for transfers between devices  271 us (32%)
  matrix products  206 us (24%)
  starting transfers between devices  174 us (20%)
  other arithmetic  121 us (14%)
  local copies, waits for them, and re-layouts  67.6 us (8%)
    ppermute x82, waiting for transfers between devices, exchange(): return lax.ppermute(values, AXES, pairs)  261 us
    ppermute x82, starting transfers between devices, exchange(): return lax.ppermute(values, AXES, pairs)  107 us
    ppermute x15, starting transfers between devices, swap(): return lax.ppermute(values, AXES, pairs)  67.3 us
    dot_general x10, matrix products, mm_nt(): lax.dot_general(left, right, (((1,), (1,)), ((), ())), preferred_element_...  43.8 us
    dot_general x8, matrix products, mm(): lax.dot_general(left, right, (((1,), (0,)), ((), ())), preferred_element_...  34.6 us
    dot_general x8, matrix products, mm_tn(): lax.dot_general(left, right, (((0,), (0,)), ((), ())), preferred_element_...  31.8 us
    select_n x59, other arithmetic, joined(): return jnp.where(low, jnp.stack([mine, theirs]), jnp.stack([theirs, mine]))  20.4 us
    reduce_sum x2, other arithmetic, attend(): jnp.sum(jnp.exp(scores - top), axis=1, keepdims=True)  17.1 us
  transfers between devices with their start and end apart: 97, of which 45 were waited for; matrix products, arithmetic and copies ran while one was open for 39% of the time, Pallas kernels for 0%

profile of v1, /device:TPU:1, one launch (start us, length us, event | category | flops | bytes accessed | tf_op | source)
XLA Modules:
  0.0 843.8 jit_solution(7802008849193669874)
XLA Ops:
  3.6 4.5 collective-permute-start.14
  28.3 5.4 convolution_add_fusion.4
  80.5 6.2 collective-permute-done.10
  90.2 9.8 %collective-permute-done.35 = bf16[72,1152]{1,0:T(8,128)(2,1)S(1)} collective-permute-done((bf16[72,1152]{1,0:T(8,128)(2,1)S(1)}, bf16[72,1152]{1,0:T(8,128)(2,1)S(1)}, u32[]{:S(2)}, u32[]{:S(2)}) %collective-permute-start.35) | collective-permute-done | bytes 165920 | tf_op jit(solution)/shard_map/ppermute | solution.py:57
  102.0 14.1 %collective-permute-done.31 = bf16[72,1152]{1,0:T(8,128)(2,1)S(1)} collective-permute-done((bf16[72,1152]{1,0:T(8,128)(2,1)S(1)}, bf16[72,1152]{1,0:T(8,128)(2,1)S(1)}, u32[]{:S(2)}, u32[]{:S(2)}) %collective-permute-start.31) | collective-permute-done | bytes 165920 | tf_op jit(solution)/shard_map/ppermute | solution.py:57
  117.0 9.0 %collective-permute-done.11 = bf16[2,72,864]{2,1,0:T(8,128)(2,1)S(1)} collective-permute-done((bf16[2,72,864]{2,1,0:T(8,128)(2,1)S(1)}, bf16[2,72,864]{2,1,0:T(8,128)(2,1)S(1)}, u32[]{:S(2)}, u32[]{:S(2)}) %collective-permute-start.11) | collective-permute-done | bytes 248864 | tf_op jit(solution)/shard_map/ppermute | solution.py:57
  129.9 4.2 collective-permute-done.18
  137.1 16.2 %collective-permute-done.40 = bf16[2,72,1152]{2,1,0:T(8,128)(2,1)S(1)} collective-permute-done((bf16[2,72,1152]{2,1,0:T(8,128)(2,1)S(1)}, bf16[2,72,1152]{2,1,0:T(8,128)(2,1)S(1)}, u32[]{:S(2)}, u32[]{:S(2)}) %collective-permute-start.40) | collective-permute-done | bytes 331808 | tf_op jit(solution)/shard_map/ppermute | solution.py:57
  157.5 4.3 collective-permute-done.12
  164.1 13.2 %collective-permute-done.41 = bf16[2,2,72,1152]{3,2,1,0:T(8,128)(2,1)S(1)} collective-permute-done((bf16[2,2,72,1152]{3,2,1,0:T(8,128)(2,1)S(1)}, bf16[2,2,72,1152]{3,2,1,0:T(8,128)(2,1)S(1)}, u32[]{:S(2)}, u32[]{:S(2)}) %collective-permute-start.41) | collective-permute-done | bytes 663584 | tf_op jit(solution)/shard_map/ppermute | solution.py:57
  184.3 11.9 %collective-permute-start.1 = (bf16[576,1024]{1,0:T(8,128)(2,1)S(1)}, bf16[576,1024]{1,0:T(8,128)(2,1)S(1)}, u32[]{:S(2)}, u32[]{:S(2)}) collective-permute-start(bf16[576,1024]{1,0:T(8,128)(2,1)S(1)} %collective-permute-done), channel_id=1, source_target_pairs={{0,2},{1,3},{2,0},{3,1},{4,6},{5,7},{6,4},{7,5},{8,10},{9,11},{10,... | collective-permute-start | bytes 3538952 | tf_op jit(solution)/shard_map/ppermute | solution.py:57
  196.2 10.4 %collective-permute-start.46 = (bf16[576,1024]{1,0:T(8,128)(2,1)}, bf16[576,1024]{1,0:T(8,128)(2,1)}, u32[]{:S(2)}, u32[]{:S(2)}) collective-permute-start(bf16[576,1024]{1,0:T(8,128)(2,1)} %collective-permute-done.45), channel_id=1, source_target_pairs={{0,2},{1,3},{2,0},{3,1},{4,6},{5,7},{6,4},{7,5},{8,10},{9,11},{10,... | collective-permute-start | bytes 3538952 | tf_op jit(solution)/shard_map/ppermute | solution.py:57
  225.6 8.2 multiply_reduce_fusion.1
  233.8 8.5 %exponential_reduce_fusion.1 = f32[4,1024]{1,0:T(4,128)S(1)} fusion(f32[4,1024,1024]{2,1,0:T(8,128)} %get-tuple-element.163, f32[4,1024]{1,0:T(4,128)S(1)} %get-tuple-element.162), kind=kLoop, calls=%fused_computation.5 | loop fusion | flops 12578816 | bytes 16809984 | tf_op jit(solution)/shard_map/reduce_sum | solution.py:129
  243.4 8.4 multiply_reduce_fusion
  251.8 8.6 %exponential_reduce_fusion = f32[4,1024]{1,0:T(4,128)S(1)} fusion(f32[4,1024,1024]{2,1,0:T(8,128)} %get-tuple-element.165, f32[4,1024]{1,0:T(4,128)S(1)} %get-tuple-element.164), kind=kLoop, calls=%fused_computation.3 | loop fusion | flops 12578816 | bytes 16809984 | tf_op jit(solution)/shard_map/reduce_sum | solution.py:129
  260.5 8.8 %convolution_convert_fusion.9 = bf16[4,72,1024]{2,1,0:T(8,128)(2,1)S(1)} fusion(bf16[4,72,1024]{2,1,0:T(8,128)(2,1)S(1)} %bitcast.539, f32[4,1024,1024]{2,1,0:T(8,128)} %get-tuple-element.163, f32[4,1024]{1,0:T(4,128)S(1)} %log_add_fusion.1), kind=kOutput, calls=%fused_computation.127 | convolution fusion | flops 616857600 | bytes 17973248 | tf_op jit(solution)/shard_map/hdk,hkq->hdq/dot_general | solution.py:131
  277.3 10.1 %collective-permute-start.23 = (bf16[1152,1024]{1,0:T(8,128)(2,1)S(1)}, bf16[1152,1024]{1,0:T(8,128)(2,1)S(1)}, u32[]{:S(2)}, u32[]{:S(2)}) collective-permute-start(bf16[1152,1024]{1,0:T(8,128)(2,1)S(1)} %get-tuple-element.166), channel_id=1, source_target_pairs={{0,2},{1,3},{2,0},{3,1},{4,6},{5,7},{6,4},{7,5},{8,10},{9,11},{10,... | collective-permute-start | bytes 7077896 | tf_op jit(solution)/shard_map/ppermute | solution.py:57
  287.4 4.9 fusion.26
  311.8 7.7 fusion.92
  330.7 5.6 fusion.90
  336.3 8.6 %fusion.96 = (f32[1152]{0:T(1024)S(1)}, bf16[1152,1024]{0,1:T(8,128)(2,1)}) fusion(f32[1152,1024]{0,1:T(8,128)S(1)} %fusion.114, f32[1152]{0:T(1024)S(1)} %copy-done.96, bf16[1152,1152]{1,0:T(8,128)(2,1)S(1)} %bitcast.565, bf16[1152,1024]{1,0:T(8,128)(2,1)S(1)} %bitcast.576), kind=kOutput, calls=%fused_computation.393 | convolution fusion | flops 2748578816 | bytes 12100608 | tf_op jit(solution)/shard_map/dot_general | solution.py:30
  344.9 8.7 %fusion.94 = (f32[1152]{0:T(1024)S(1)}, bf16[1152,1024]{0,1:T(8,128)(2,1)}) fusion(f32[1152,1024]{0,1:T(8,128)S(1)} %fusion.115, f32[1152]{0:T(1024)S(1)} %copy-done.97, bf16[1152,1152]{1,0:T(8,128)(2,1)S(1)} %bitcast.556, bf16[1152,1024]{1,0:T(8,128)(2,1)S(1)} %bitcast.577), kind=kOutput, calls=%fused_computation.392 | convolution fusion | flops 2748578816 | bytes 12100608 | tf_op jit(solution)/shard_map/dot_general | solution.py:30
  354.2 5.6 convolution_convert_fusion.2
  363.6 5.6 convolution_convert_fusion.3
  371.4 10.5 %fusion.109 = (bf16[1152,1024]{1,0:T(8,128)(2,1)}, f32[1152,1024]{1,0:T(8,128)}) fusion(f32[1152,1024]{1,0:T(8,128)} %fusion.90, bf16[1152,1152]{1,0:T(8,128)(2,1)S(1)} %bitcast.557, f32[1152,1024]{0,1:T(8,128)} %copy-done.101, f32[1152]{0:T(1024)S(1)} %copy-done.97), kind=kOutput, calls=%fused_computation.405 | convolution fusion | flops 2732064768 | bytes 19173888 | tf_op jit(solution)/shard_map/dot_general | solution.py:26
  396.1 4.5 collective-permute-done.78
  401.2 13.5 %collective-permute-done.83 = bf16[2,2,72,1152]{3,2,1,0:T(8,128)(2,1)S(1)} collective-permute-done((bf16[2,2,72,1152]{3,2,1,0:T(8,128)(2,1)S(1)}, bf16[2,2,72,1152]{3,2,1,0:T(8,128)(2,1)S(1)}, u32[]{:S(2)}, u32[]{:S(2)}) %collective-permute-start.83) | collective-permute-done | bytes 663584 | tf_op jit(solution)/shard_map/ppermute | solution.py:57
  416.6 6.8 collective-permute-done.84
  424.8 8.3 collective-permute-done.80
  438.4 4.9 fusion.98
  445.3 8.1 convolution_convert_fusion
  453.4 5.5 convolution_convert_fusion.1
  459.2 8.5 %multiply_convert_fusion = bf16[4,1024,1024]{2,1,0:T(8,128)(2,1)} fusion(f32[4,1024,1024]{2,1,0:T(8,128)S(1)} %bitcast.481, bf16[4,72,1024]{2,1,0:T(8,128)(2,1)} %bitcast.541, bf16[4,72,1024]{2,1,0:T(8,128)(2,1)S(1)} %bitcast.508, f32[4,1024]{1,0:T(4,128)S(1)} %multiply_reduce_fusion.11, f32[4,1024]{1,0:T(4,128)S(1)} %copy-done.77), kind=kOutput, calls=%fused_computation | convolution fusion | flops 624951296 | bytes 26378240 | tf_op jit(solution)/shard_map/hdk,hdq->hkq/dot_general | solution.py:143
  467.7 7.0 fusion.30
  474.8 6.0 fusion.100
  484.7 6.7 multiply_convert_fusion.1
  491.4 7.1 fusion.29
  500.9 8.3 fusion.102
  513.3 5.4 multiply_reduce_fusion.6
  519.3 4.7 collective-permute-start.44
  533.6 4.2 fusion.48
  537.8 4.7 fusion.110
  545.8 6.2 collective-permute-start.64
  560.2 8.2 collective-permute-start.86
  569.0 26.1 %collective-permute-done.65 = bf16[2,2,72,288]{3,2,1,0:T(8,128)(2,1)S(1)} collective-permute-done((bf16[2,2,72,288]{3,2,1,0:T(8,128)(2,1)S(1)}, bf16[2,2,72,288]{3,2,1,0:T(8,128)(2,1)S(1)}, u32[]{:S(2)}, u32[]{:S(2)}) %collective-permute-start.65) | collective-permute-done | bytes 165920 | tf_op jit(solution)/shard_map/ppermute | solution.py:57
  595.2 4.7 collective-permute-done.69
  617.1 9.8 %collective-permute-start.72 = (bf16[72,576]{1,0:T(8,128)(2,1)S(1)}, bf16[72,576]{1,0:T(8,128)(2,1)S(1)}, u32[]{:S(2)}, u32[]{:S(2)}) collective-permute-start(bf16[72,576]{1,0:T(8,128)(2,1)S(1)} %pad_maximum_fusion.14), channel_id=1, source_target_pairs={{0,0},{1,2},{2,1},{3,3},{4,4},{5,6},{6,5},{7,7},{8,8},{9,10},{10,9... | collective-permute-start | bytes 248840 | tf_op jit(solution)/shard_map/ppermute | solution.py:65
  635.0 14.4 %collective-permute-done.92 = bf16[2,2,72,1152]{3,2,1,0:T(8,128)(2,1)S(1)} collective-permute-done((bf16[2,2,72,1152]{3,2,1,0:T(8,128)(2,1)S(1)}, bf16[2,2,72,1152]{3,2,1,0:T(8,128)(2,1)S(1)}, u32[]{:S(2)}, u32[]{:S(2)}) %collective-permute-start.92) | collective-permute-done | bytes 663584 | tf_op jit(solution)/shard_map/ppermute | solution.py:57
  651.4 6.7 collective-permute-done.93
  660.1 7.6 collective-permute-done.89
  668.5 7.6 fusion.91
  680.3 5.1 convolution_convert_fusion.4
  691.6 4.1 copy.99
  707.0 17.0 %collective-permute-done.61 = f32[2,2,1,4,576]{4,0,1,3,2:T(2,128)S(1)} collective-permute-done((f32[2,2,1,4,576]{4,0,1,3,2:T(2,128)S(1)}, f32[2,2,1,4,576]{4,0,1,3,2:T(2,128)S(1)}, u32[]{:S(2)}, u32[]{:S(2)}) %collective-permute-start.61) | collective-permute-done | bytes 36896 | tf_op jit(solution)/shard_map/ppermute | solution.py:57
  728.1 7.6 collective-permute-start.49
  744.3 6.5 collective-permute-done.62
  761.8 5.6 collective-permute-done.76
  773.4 4.3 collective-permute-done.77
  777.8 5.5 convolution_bitcast_fusion
  785.0 9.4 %fusion.50 = f32[6,576,1152]{2,1,0:T(8,128)} fusion(bf16[16,1152,1]{1,0,2:T(8,128)(2,1)S(1)} %copy-done.78, f32[6,576,16]{1,0,2:T(8,128)S(1)} %dot_general.168), kind=kOutput, calls=%fused_computation.233 | convolution fusion | flops 764411904 | bytes 16183296 | tf_op jit(solution)/shard_map/dot_general | solution.py:347
  815.7 6.4 collective-permute-done.56
  822.9 9.4 %collective-permute-done.57 = bf16[72,864]{1,0:T(8,128)(2,1)S(1)} collective-permute-done((bf16[72,864]{1,0:T(8,128)(2,1)S(1)}, bf16[72,864]{1,0:T(8,128)(2,1)S(1)}, u32[]{:S(2)}, u32[]{:S(2)}) %collective-permute-start.57) | collective-permute-done | bytes 124448 | tf_op jit(solution)/shard_map/ppermute | solution.py:57
  833.1 5.4 collective-permute-start.58
  (756 shorter events, 328.7 us)
Async XLA Ops:
  3.6 16.1 %collective-permute-start.14 = (f32[8,576]{1,0:T(8,128)S(1)}, f32[8,576]{1,0:T(8,128)S(1)}, u32[]{:S(2)}, u32[]{:S(2)}) collective-permute-start(f32[8,576]{1,0:T(8,128)S(1)} %maximum_convert_fusion), channel_id=1, source_target_pairs={{0,0},{1,2},{2,1},{3,3},{4,4},{5,6},{6,5},{7,7},{8,8},{9,10},{10,9... | collective-permute-start | bytes 55304 | tf_op jit(solution)/shard_map/ppermute | solution.py:65
  9.9 18.2 %collective-permute-start.2 = (f32[16,576]{1,0:T(8,128)S(1)}, f32[16,576]{1,0:T(8,128)S(1)}, u32[]{:S(2)}, u32[]{:S(2)}) collective-permute-start(f32[16,576]{1,0:T(8,128)S(1)} %convolution_add_fusion.5), channel_id=1, source_target_pairs={{0,1},{1,0},{2,3},{3,2},{4,5},{5,4},{6,7},{7,6},{8,9},{9,8},{10,11... | collective-permute-start | bytes 110600 | tf_op jit(solution)/shard_map/ppermute | solution.py:57
  10.0 30.1 %collective-permute-start.4 = (bf16[72,576]{1,0:T(8,128)(2,1)}, bf16[72,576]{1,0:T(8,128)(2,1)S(1)}, u32[]{:S(2)}, u32[]{:S(2)}) collective-permute-start(bf16[72,576]{1,0:T(8,128)(2,1)} %bitcast.660), channel_id=1, source_target_pairs={{0,0},{1,2},{2,1},{3,3},{4,4},{5,6},{6,5},{7,7},{8,8},{9,10},{10,9... | collective-permute-start | bytes 248840 | tf_op jit(solution)/shard_map/ppermute | solution.py:65
  11.9 61.5 %collective-permute-start.30 = (bf16[72,2304]{1,0:T(8,128)(2,1)}, bf16[72,2304]{1,0:T(8,128)(2,1)}, u32[]{:S(2)}, u32[]{:S(2)}) collective-permute-start(bf16[72,2304]{1,0:T(8,128)(2,1)} %param.25), channel_id=1, source_target_pairs={{0,0},{1,2},{2,1},{3,3},{4,4},{5,6},{6,5},{7,7},{8,8},{9,10},{10,9... | collective-permute-start | bytes 995336 | tf_op jit(solution)/shard_map/ppermute | solution.py:65
  15.6 55.5 %collective-permute-start.25 = (bf16[72,2304]{1,0:T(8,128)(2,1)}, bf16[72,2304]{1,0:T(8,128)(2,1)}, u32[]{:S(2)}, u32[]{:S(2)}) collective-permute-start(bf16[72,2304]{1,0:T(8,128)(2,1)} %bitcast.659), channel_id=1, source_target_pairs={{0,0},{1,2},{2,1},{3,3},{4,4},{5,6},{6,5},{7,7},{8,8},{9,10},{10,9... | collective-permute-start | bytes 995336 | tf_op jit(solution)/shard_map/ppermute | solution.py:65
  24.7 40.4 %collective-permute-start.9 = (bf16[72,1728]{1,0:T(8,128)(2,1)S(1)}, bf16[72,1728]{1,0:T(8,128)(2,1)S(1)}, u32[]{:S(2)}, u32[]{:S(2)}) collective-permute-start(bf16[72,1728]{1,0:T(8,128)(2,1)S(1)} %reshape.4520), channel_id=1, source_target_pairs={{0,0},{1,2},{2,1},{3,3},{4,4},{5,6},{6,5},{7,7},{8,8},{9,10},{10,9... | collective-permute-start | bytes 746504 | tf_op jit(solution)/shard_map/ppermute | solution.py:65
  36.5 147.6 %collective-permute-start = (bf16[576,1024]{1,0:T(8,128)(2,1)}, bf16[576,1024]{1,0:T(8,128)(2,1)S(1)}, u32[]{:S(2)}, u32[]{:S(2)}) collective-permute-start(bf16[576,1024]{1,0:T(8,128)(2,1)} %bitcast), channel_id=1, source_target_pairs={{0,0},{1,2},{2,1},{3,3},{4,4},{5,6},{6,5},{7,7},{8,8},{9,10},{10,9... | collective-permute-start | bytes 3538952 | tf_op jit(solution)/shard_map/ppermute | solution.py:65
  59.4 124.9 %collective-permute-start.45 = (bf16[576,1024]{1,0:T(8,128)(2,1)}, bf16[576,1024]{1,0:T(8,128)(2,1)}, u32[]{:S(2)}, u32[]{:S(2)}) collective-permute-start(bf16[576,1024]{1,0:T(8,128)(2,1)} %bitcast.658), channel_id=1, source_target_pairs={{0,0},{1,2},{2,1},{3,3},{4,4},{5,6},{6,5},{7,7},{8,8},{9,10},{10,9... | collective-permute-start | bytes 3538952 | tf_op jit(solution)/shard_map/ppermute | solution.py:65
  65.1 21.8 %collective-permute-start.17 = (bf16[2,2,72,288]{3,2,1,0:T(8,128)(2,1)}, bf16[2,2,72,288]{3,2,1,0:T(8,128)(2,1)S(1)}, u32[]{:S(2)}, u32[]{:S(2)}) collective-permute-start(bf16[2,2,72,288]{3,2,1,0:T(8,128)(2,1)} %maximum_select_fusion.51), channel_id=1, source_target_pairs={{0,1},{1,0},{2,3},{3,2},{4,5},{5,4},{6,7},{7,6},{8,9},{9,8},{10,11... | collective-permute-start | bytes 497672 | tf_op jit(solution)/shard_map/ppermute | solution.py:57
  71.1 18.7 %collective-permute-start.7 = (bf16[2,2,72,288]{3,2,1,0:T(8,128)(2,1)}, bf16[2,2,72,288]{3,2,1,0:T(8,128)(2,1)S(1)}, u32[]{:S(2)}, u32[]{:S(2)}) collective-permute-start(bf16[2,2,72,288]{3,2,1,0:T(8,128)(2,1)} %maximum_select_fusion.49), channel_id=1, source_target_pairs={{0,4},{1,5},{2,6},{3,7},{4,0},{5,1},{6,2},{7,3},{8,12},{9,13},{10,... | collective-permute-start | bytes 497672 | tf_op jit(solution)/shard_map/ppermute | solution.py:57
  86.8 13.2 %collective-permute-start.35 = (bf16[72,1152]{1,0:T(8,128)(2,1)S(1)}, bf16[72,1152]{1,0:T(8,128)(2,1)S(1)}, u32[]{:S(2)}, u32[]{:S(2)}) collective-permute-start(bf16[72,1152]{1,0:T(8,128)(2,1)S(1)} %get-tuple-element.130), channel_id=1, source_target_pairs={{0,16},{1,17},{2,18},{3,19},{4,20},{5,21},{6,22},{7,23},{8,24},{9,... | collective-permute-start | bytes 497672 | tf_op jit(solution)/shard_map/ppermute | solution.py:57
  87.0 14.8 %collective-permute-start.26 = (bf16[72,1152]{1,0:T(8,128)(2,1)S(1)}, bf16[72,1152]{1,0:T(8,128)(2,1)S(1)}, u32[]{:S(2)}, u32[]{:S(2)}) collective-permute-start(bf16[72,1152]{1,0:T(8,128)(2,1)S(1)} %get-tuple-element.131), channel_id=1, source_target_pairs={{0,16},{1,17},{2,18},{3,19},{4,20},{5,21},{6,22},{7,23},{8,24},{9,... | collective-permute-start | bytes 497672 | tf_op jit(solution)/shard_map/ppermute | solution.py:57
  89.8 26.5 %collective-permute-start.39 = (bf16[72,1152]{1,0:T(8,128)(2,1)S(1)}, bf16[72,1152]{1,0:T(8,128)(2,1)S(1)}, u32[]{:S(2)}, u32[]{:S(2)}) collective-permute-start(bf16[72,1152]{1,0:T(8,128)(2,1)S(1)} %get-tuple-element.124), channel_id=1, source_target_pairs={{0,16},{1,17},{2,18},{3,19},{4,20},{5,21},{6,22},{7,23},{8,24},{9,... | collective-permute-start | bytes 497672 | tf_op jit(solution)/shard_map/ppermute | solution.py:57
  100.0 16.1 %collective-permute-start.31 = (bf16[72,1152]{1,0:T(8,128)(2,1)S(1)}, bf16[72,1152]{1,0:T(8,128)(2,1)S(1)}, u32[]{:S(2)}, u32[]{:S(2)}) collective-permute-start(bf16[72,1152]{1,0:T(8,128)(2,1)S(1)} %get-tuple-element.125), channel_id=1, source_target_pairs={{0,16},{1,17},{2,18},{3,19},{4,20},{5,21},{6,22},{7,23},{8,24},{9,... | collective-permute-start | bytes 497672 | tf_op jit(solution)/shard_map/ppermute | solution.py:57
  101.7 24.8 %collective-permute-start.20 = (bf16[2,72,864]{2,1,0:T(8,128)(2,1)S(1)}, bf16[2,72,864]{2,1,0:T(8,128)(2,1)S(1)}, u32[]{:S(2)}, u32[]{:S(2)}) collective-permute-start(bf16[2,72,864]{2,1,0:T(8,128)(2,1)S(1)} %maximum_select_fusion.47), channel_id=1, source_target_pairs={{0,8},{1,9},{2,10},{3,11},{4,12},{5,13},{6,14},{7,15},{8,0},{9,1},... | collective-permute-start | bytes 746504 | tf_op jit(solution)/shard_map/ppermute | solution.py:57
  127.1 28.2 %collective-permute-start.27 = (bf16[2,72,1152]{2,1,0:T(8,128)(2,1)S(1)}, bf16[2,72,1152]{2,1,0:T(8,128)(2,1)S(1)}, u32[]{:S(2)}, u32[]{:S(2)}) collective-permute-start(bf16[2,72,1152]{2,1,0:T(8,128)(2,1)S(1)} %maximum_select_fusion.37), channel_id=1, source_target_pairs={{0,8},{1,9},{2,10},{3,11},{4,12},{5,13},{6,14},{7,15},{8,0},{9,1},... | collective-permute-start | bytes 995336 | tf_op jit(solution)/shard_map/ppermute | solution.py:57
  134.1 20.7 %collective-permute-start.32 = (bf16[2,72,1152]{2,1,0:T(8,128)(2,1)S(1)}, bf16[2,72,1152]{2,1,0:T(8,128)(2,1)S(1)}, u32[]{:S(2)}, u32[]{:S(2)}) collective-permute-start(bf16[2,72,1152]{2,1,0:T(8,128)(2,1)S(1)} %maximum_select_fusion.39), channel_id=1, source_target_pairs={{0,8},{1,9},{2,10},{3,11},{4,12},{5,13},{6,14},{7,15},{8,0},{9,1},... | collective-permute-start | bytes 995336 | tf_op jit(solution)/shard_map/ppermute | solution.py:57
  135.4 18.0 %collective-permute-start.40 = (bf16[2,72,1152]{2,1,0:T(8,128)(2,1)S(1)}, bf16[2,72,1152]{2,1,0:T(8,128)(2,1)S(1)}, u32[]{:S(2)}, u32[]{:S(2)}) collective-permute-start(bf16[2,72,1152]{2,1,0:T(8,128)(2,1)S(1)} %maximum_select_fusion.43), channel_id=1, source_target_pairs={{0,8},{1,9},{2,10},{3,11},{4,12},{5,13},{6,14},{7,15},{8,0},{9,1},... | collective-permute-start | bytes 995336 | tf_op jit(solution)/shard_map/ppermute | solution.py:57
  155.3 22.0 %collective-permute-start.41 = (bf16[2,2,72,1152]{3,2,1,0:T(8,128)(2,1)S(1)}, bf16[2,2,72,1152]{3,2,1,0:T(8,128)(2,1)S(1)}, u32[]{:S(2)}, u32[]{:S(2)}) collective-permute-start(bf16[2,2,72,1152]{3,2,1,0:T(8,128)(2,1)S(1)} %maximum_select_fusion.27), channel_id=1, source_target_pairs={{0,1},{1,0},{2,3},{3,2},{4,5},{5,4},{6,7},{7,6},{8,9},{9,8},{10,11... | collective-permute-start | bytes 1990664 | tf_op jit(solution)/shard_map/ppermute | solution.py:57
  161.9 18.4 %collective-permute-start.33 = (bf16[2,2,72,1152]{3,2,1,0:T(8,128)(2,1)S(1)}, bf16[2,2,72,1152]{3,2,1,0:T(8,128)(2,1)S(1)}, u32[]{:S(2)}, u32[]{:S(2)}) collective-permute-start(bf16[2,2,72,1152]{3,2,1,0:T(8,128)(2,1)S(1)} %maximum_select_fusion.23), channel_id=1, source_target_pairs={{0,4},{1,5},{2,6},{3,7},{4,0},{5,1},{6,2},{7,3},{8,12},{9,13},{10,... | collective-permute-start | bytes 1990664 | tf_op jit(solution)/shard_map/ppermute | solution.py:57
  163.5 44.8 %collective-permute-start.37 = (bf16[2,2,72,1152]{3,2,1,0:T(8,128)(2,1)S(1)}, bf16[2,2,72,1152]{3,2,1,0:T(8,128)(2,1)S(1)}, u32[]{:S(2)}, u32[]{:S(2)}) collective-permute-start(bf16[2,2,72,1152]{3,2,1,0:T(8,128)(2,1)S(1)} %maximum_select_fusion.25), channel_id=1, source_target_pairs={{0,1},{1,0},{2,3},{3,2},{4,5},{5,4},{6,7},{7,6},{8,9},{9,8},{10,11... | collective-permute-start | bytes 1990664 | tf_op jit(solution)/shard_map/ppermute | solution.py:57
  177.3 18.9 %collective-permute-start.28 = (bf16[2,2,72,1152]{3,2,0,1:T(8,128)(2,1)S(1)}, bf16[2,2,72,1152]{3,2,0,1:T(8,128)(2,1)S(1)}, u32[]{:S(2)}, u32[]{:S(2)}) collective-permute-start(bf16[2,2,72,1152]{3,2,0,1:T(8,128)(2,1)S(1)} %maximum_select_fusion.21), channel_id=1, source_target_pairs={{0,4},{1,5},{2,6},{3,7},{4,0},{5,1},{6,2},{7,3},{8,12},{9,13},{10,... | collective-permute-start | bytes 1990664 | tf_op jit(solution)/shard_map/ppermute | solution.py:57
  180.3 32.5 %collective-permute-start.22 = (bf16[2,2,2,72,864]{4,3,2,1,0:T(8,128)(2,1)S(1)}, bf16[2,2,2,72,864]{4,3,2,1,0:T(8,128)(2,1)S(1)}, u32[]{:S(2)}, u32[]{:S(2)}) collective-permute-start(bf16[2,2,2,72,864]{4,3,2,1,0:T(8,128)(2,1)S(1)} %maximum_select_fusion.18), channel_id=1, source_target_pairs={{0,4},{1,5},{2,6},{3,7},{4,0},{5,1},{6,2},{7,3},{8,12},{9,13},{10,... | collective-permute-start | bytes 2985992 | tf_op jit(solution)/shard_map/ppermute | solution.py:57
  184.0 30.1 %collective-permute-start.13 = (bf16[2,2,2,72,864]{4,3,2,1,0:T(8,128)(2,1)S(1)}, bf16[2,2,2,72,864]{4,3,2,1,0:T(8,128)(2,1)S(1)}, u32[]{:S(2)}, u32[]{:S(2)}) collective-permute-start(bf16[2,2,2,72,864]{4,3,2,1,0:T(8,128)(2,1)S(1)} %maximum_select_fusion.16), channel_id=1, source_target_pairs={{0,1},{1,0},{2,3},{3,2},{4,5},{5,4},{6,7},{7,6},{8,9},{9,8},{10,11... | collective-permute-start | bytes 2985992 | tf_op jit(solution)/shard_map/ppermute | solution.py:57
  184.3 31.6 %collective-permute-start.1 = (bf16[576,1024]{1,0:T(8,128)(2,1)S(1)}, bf16[576,1024]{1,0:T(8,128)(2,1)S(1)}, u32[]{:S(2)}, u32[]{:S(2)}) collective-permute-start(bf16[576,1024]{1,0:T(8,128)(2,1)S(1)} %collective-permute-done), channel_id=1, source_target_pairs={{0,2},{1,3},{2,0},{3,1},{4,6},{5,7},{6,4},{7,5},{8,10},{9,11},{10,... | collective-permute-start | bytes 3538952 | tf_op jit(solution)/shard_map/ppermute | solution.py:57
  196.2 81.1 %collective-permute-start.46 = (bf16[576,1024]{1,0:T(8,128)(2,1)}, bf16[576,1024]{1,0:T(8,128)(2,1)}, u32[]{:S(2)}, u32[]{:S(2)}) collective-permute-start(bf16[576,1024]{1,0:T(8,128)(2,1)} %collective-permute-done.45), channel_id=1, source_target_pairs={{0,2},{1,3},{2,0},{3,1},{4,6},{5,7},{6,4},{7,5},{8,10},{9,11},{10,... | collective-permute-start | bytes 3538952 | tf_op jit(solution)/shard_map/ppermute | solution.py:57
  208.3 98.0 %collective-permute-start.29 = (bf16[2,2,2,72,1152]{4,3,0,1,2:T(8,128)(2,1)}, bf16[2,2,2,72,1152]{4,3,0,1,2:T(8,128)(2,1)}, u32[]{:S(2)}, u32[]{:S(2)}) collective-permute-start(bf16[2,2,2,72,1152]{4,3,0,1,2:T(8,128)(2,1)} %maximum_select_fusion.8), channel_id=1, source_target_pairs={{0,1},{1,0},{2,3},{3,2},{4,5},{5,4},{6,7},{7,6},{8,9},{9,8},{10,11... | collective-permute-start | bytes 3981320 | tf_op jit(solution)/shard_map/ppermute | solution.py:57
  212.7 83.6 %collective-permute-start.38 = (bf16[2,2,2,72,1152]{4,3,2,1,0:T(8,128)(2,1)}, bf16[2,2,2,72,1152]{4,3,2,1,0:T(8,128)(2,1)}, u32[]{:S(2)}, u32[]{:S(2)}) collective-permute-start(bf16[2,2,2,72,1152]{4,3,2,1,0:T(8,128)(2,1)} %maximum_select_fusion.12), channel_id=1, source_target_pairs={{0,4},{1,5},{2,6},{3,7},{4,0},{5,1},{6,2},{7,3},{8,12},{9,13},{10,... | collective-permute-start | bytes 3981320 | tf_op jit(solution)/shard_map/ppermute | solution.py:57
  214.1 84.6 %collective-permute-start.34 = (bf16[2,2,2,72,1152]{4,3,2,1,0:T(8,128)(2,1)}, bf16[2,2,2,72,1152]{4,3,2,1,0:T(8,128)(2,1)}, u32[]{:S(2)}, u32[]{:S(2)}) collective-permute-start(bf16[2,2,2,72,1152]{4,3,2,1,0:T(8,128)(2,1)} %maximum_select_fusion.10), channel_id=1, source_target_pairs={{0,1},{1,0},{2,3},{3,2},{4,5},{5,4},{6,7},{7,6},{8,9},{9,8},{10,11... | collective-permute-start | bytes 3981320 | tf_op jit(solution)/shard_map/ppermute | solution.py:57
  215.9 86.7 %collective-permute-start.42 = (bf16[2,2,2,72,1152]{4,3,2,1,0:T(8,128)(2,1)}, bf16[2,2,2,72,1152]{4,3,2,1,0:T(8,128)(2,1)}, u32[]{:S(2)}, u32[]{:S(2)}) collective-permute-start(bf16[2,2,2,72,1152]{4,3,2,1,0:T(8,128)(2,1)} %maximum_select_fusion.14), channel_id=1, source_target_pairs={{0,4},{1,5},{2,6},{3,7},{4,0},{5,1},{6,2},{7,3},{8,12},{9,13},{10,... | collective-permute-start | bytes 3981320 | tf_op jit(solution)/shard_map/ppermute | solution.py:57
  277.3 33.0 %collective-permute-start.23 = (bf16[1152,1024]{1,0:T(8,128)(2,1)S(1)}, bf16[1152,1024]{1,0:T(8,128)(2,1)S(1)}, u32[]{:S(2)}, u32[]{:S(2)}) collective-permute-start(bf16[1152,1024]{1,0:T(8,128)(2,1)S(1)} %get-tuple-element.166), channel_id=1, source_target_pairs={{0,2},{1,3},{2,0},{3,1},{4,6},{5,7},{6,4},{7,5},{8,10},{9,11},{10,... | collective-permute-start | bytes 7077896 | tf_op jit(solution)/shard_map/ppermute | solution.py:57
  362.4 31.0 %collective-permute-start.82 = (bf16[2,2,2,72,1152]{4,3,1,0,2:T(8,128)(2,1)}, bf16[2,2,2,72,1152]{4,3,1,0,2:T(8,128)(2,1)}, u32[]{:S(2)}, u32[]{:S(2)}) collective-permute-start(bf16[2,2,2,72,1152]{4,3,1,0,2:T(8,128)(2,1)} %bitcast.475), channel_id=1, source_target_pairs={{0,4},{1,5},{2,6},{3,7},{4,0},{5,1},{6,2},{7,3},{8,12},{9,13},{10,... | collective-permute-start | bytes 3981320 | tf_op jit(solution)/shard_map/ppermute | solution.py:57
  369.6 31.0 %collective-permute-start.78 = (bf16[2,2,2,72,1152]{4,3,1,0,2:T(8,128)(2,1)S(1)}, bf16[2,2,2,72,1152]{4,3,1,0,2:T(8,128)(2,1)S(1)}, u32[]{:S(2)}, u32[]{:S(2)}) collective-permute-start(bf16[2,2,2,72,1152]{4,3,1,0,2:T(8,128)(2,1)S(1)} %bitcast.602), channel_id=1, source_target_pairs={{0,1},{1,0},{2,3},{3,2},{4,5},{5,4},{6,7},{7,6},{8,9},{9,8},{10,11... | collective-permute-start | bytes 3981320 | tf_op jit(solution)/shard_map/ppermute | solution.py:57
  381.9 131.4 %collective-permute-start.43 = (bf16[1152,1024]{1,0:T(8,128)(2,1)}, bf16[1152,1024]{1,0:T(8,128)(2,1)}, u32[]{:S(2)}, u32[]{:S(2)}) collective-permute-start(bf16[1152,1024]{1,0:T(8,128)(2,1)} %get-tuple-element.170), channel_id=1, source_target_pairs={{0,2},{1,3},{2,0},{3,1},{4,6},{5,7},{6,4},{7,5},{8,10},{9,11},{10,... | collective-permute-start | bytes 7077896 | tf_op jit(solution)/shard_map/ppermute | solution.py:57
  389.1 44.9 %collective-permute-start.47 = (bf16[1152,1024]{1,0:T(8,128)(2,1)S(1)}, bf16[1152,1024]{1,0:T(8,128)(2,1)S(1)}, u32[]{:S(2)}, u32[]{:S(2)}) collective-permute-start(bf16[1152,1024]{1,0:T(8,128)(2,1)S(1)} %get-tuple-element.168), channel_id=1, source_target_pairs={{0,2},{1,3},{2,0},{3,1},{4,6},{5,7},{6,4},{7,5},{8,10},{9,11},{10,... | collective-permute-start | bytes 7077896 | tf_op jit(solution)/shard_map/ppermute | solution.py:57
  394.9 19.8 %collective-permute-start.83 = (bf16[2,2,72,1152]{3,2,1,0:T(8,128)(2,1)S(1)}, bf16[2,2,72,1152]{3,2,1,0:T(8,128)(2,1)S(1)}, u32[]{:S(2)}, u32[]{:S(2)}) collective-permute-start(bf16[2,2,72,1152]{3,2,1,0:T(8,128)(2,1)S(1)} %dynamic-slice_bitcast_fusion.4), channel_id=1, source_target_pairs={{0,1},{1,0},{2,3},{3,2},{4,5},{5,4},{6,7},{7,6},{8,9},{9,8},{10,11... | collective-permute-start | bytes 1990664 | tf_op jit(solution)/shard_map/ppermute | solution.py:57
  400.8 15.1 %collective-permute-start.79 = (bf16[2,2,72,1152]{3,2,1,0:T(8,128)(2,1)S(1)}, bf16[2,2,72,1152]{3,2,1,0:T(8,128)(2,1)S(1)}, u32[]{:S(2)}, u32[]{:S(2)}) collective-permute-start(bf16[2,2,72,1152]{3,2,1,0:T(8,128)(2,1)S(1)} %dynamic-slice_bitcast_fusion.5), channel_id=1, source_target_pairs={{0,4},{1,5},{2,6},{3,7},{4,0},{5,1},{6,2},{7,3},{8,12},{9,13},{10,... | collective-permute-start | bytes 1990664 | tf_op jit(solution)/shard_map/ppermute | solution.py:57
  416.0 17.1 %collective-permute-start.80 = (bf16[2,72,1152]{2,1,0:T(8,128)(2,1)S(1)}, bf16[2,72,1152]{2,1,0:T(8,128)(2,1)S(1)}, u32[]{:S(2)}, u32[]{:S(2)}) collective-permute-start(bf16[2,72,1152]{2,1,0:T(8,128)(2,1)S(1)} %dynamic-slice_bitcast_fusion.13), channel_id=1, source_target_pairs={{0,8},{1,9},{2,10},{3,11},{4,12},{5,13},{6,14},{7,15},{8,0},{9,1},... | collective-permute-start | bytes 995336 | tf_op jit(solution)/shard_map/ppermute | solution.py:57
  424.2 129.6 %collective-permute-start.85 = (bf16[72,1152]{1,0:T(8,128)(2,1)}, bf16[72,1152]{1,0:T(8,128)(2,1)}, u32[]{:S(2)}, u32[]{:S(2)}) collective-permute-start(bf16[72,1152]{1,0:T(8,128)(2,1)} %dynamic-slice_bitcast_fusion.20), channel_id=1, source_target_pairs={{0,16},{1,17},{2,18},{3,19},{4,20},{5,21},{6,22},{7,23},{8,24},{9,... | collective-permute-start | bytes 497672 | tf_op jit(solution)/shard_map/ppermute | solution.py:57
  434.0 122.2 %collective-permute-start.81 = (bf16[72,1152]{1,0:T(8,128)(2,1)}, bf16[72,1152]{1,0:T(8,128)(2,1)}, u32[]{:S(2)}, u32[]{:S(2)}) collective-permute-start(bf16[72,1152]{1,0:T(8,128)(2,1)} %dynamic-slice_bitcast_fusion.21), channel_id=1, source_target_pairs={{0,16},{1,17},{2,18},{3,19},{4,20},{5,21},{6,22},{7,23},{8,24},{9,... | collective-permute-start | bytes 497672 | tf_op jit(solution)/shard_map/ppermute | solution.py:57
  519.3 110.5 %collective-permute-start.44 = (bf16[576,1024]{1,0:T(8,128)(2,1)}, bf16[576,1024]{1,0:T(8,128)(2,1)}, u32[]{:S(2)}, u32[]{:S(2)}) collective-permute-start(bf16[576,1024]{1,0:T(8,128)(2,1)} %get-tuple-element.86), channel_id=1, source_target_pairs={{0,0},{1,2},{2,1},{3,3},{4,4},{5,6},{6,5},{7,7},{8,8},{9,10},{10,9... | collective-permute-start | bytes 3538952 | tf_op jit(solution)/shard_map/ppermute | solution.py:65
  545.8 14.5 %collective-permute-start.64 = (bf16[2,2,2,72,288]{4,3,2,1,0:T(8,128)(2,1)}, bf16[2,2,2,72,288]{4,3,2,1,0:T(8,128)(2,1)S(1)}, u32[]{:S(2)}, u32[]{:S(2)}) collective-permute-start(bf16[2,2,2,72,288]{4,3,2,1,0:T(8,128)(2,1)} %dynamic-slice_bitcast_fusion.9), channel_id=1, source_target_pairs={{0,1},{1,0},{2,3},{3,2},{4,5},{5,4},{6,7},{7,6},{8,9},{9,8},{10,11... | collective-permute-start | bytes 995336 | tf_op jit(solution)/shard_map/ppermute | solution.py:57
  552.0 16.7 %collective-permute-start.68 = (bf16[2,2,2,72,288]{4,3,2,1,0:T(8,128)(2,1)S(1)}, bf16[2,2,2,72,288]{4,3,2,1,0:T(8,128)(2,1)S(1)}, u32[]{:S(2)}, u32[]{:S(2)}) collective-permute-start(bf16[2,2,2,72,288]{4,3,2,1,0:T(8,128)(2,1)S(1)} %dynamic-slice_bitcast_fusion.8), channel_id=1, source_target_pairs={{0,4},{1,5},{2,6},{3,7},{4,0},{5,1},{6,2},{7,3},{8,12},{9,13},{10,... | collective-permute-start | bytes 995336 | tf_op jit(solution)/shard_map/ppermute | solution.py:57
  553.9 78.9 %collective-permute-start.91 = (bf16[2,2,2,72,1152]{4,3,1,0,2:T(8,128)(2,1)S(1)}, bf16[2,2,2,72,1152]{4,3,1,0,2:T(8,128)(2,1)S(1)}, u32[]{:S(2)}, u32[]{:S(2)}) collective-permute-start(bf16[2,2,2,72,1152]{4,3,1,0,2:T(8,128)(2,1)S(1)} %bitcast.601), channel_id=1, source_target_pairs={{0,4},{1,5},{2,6},{3,7},{4,0},{5,1},{6,2},{7,3},{8,12},{9,13},{10,... | collective-permute-start | bytes 3981320 | tf_op jit(solution)/shard_map/ppermute | solution.py:57
  556.2 76.9 %collective-permute-start.87 = (bf16[2,2,2,72,1152]{4,3,1,0,2:T(8,128)(2,1)S(1)}, bf16[2,2,2,72,1152]{4,3,1,0,2:T(8,128)(2,1)S(1)}, u32[]{:S(2)}, u32[]{:S(2)}) collective-permute-start(bf16[2,2,2,72,1152]{4,3,1,0,2:T(8,128)(2,1)S(1)} %bitcast.600), channel_id=1, source_target_pairs={{0,1},{1,0},{2,3},{3,2},{4,5},{5,4},{6,7},{7,6},{8,9},{9,8},{10,11... | collective-permute-start | bytes 3981320 | tf_op jit(solution)/shard_map/ppermute | solution.py:57
  560.2 66.7 %collective-permute-start.86 = (bf16[72,2304]{1,0:T(8,128)(2,1)S(1)}, bf16[72,2304]{1,0:T(8,128)(2,1)S(1)}, u32[]{:S(2)}, u32[]{:S(2)}) collective-permute-start(bf16[72,2304]{1,0:T(8,128)(2,1)S(1)} %pad_maximum_fusion.11), channel_id=1, source_target_pairs={{0,0},{1,2},{2,1},{3,3},{4,4},{5,6},{6,5},{7,7},{8,8},{9,10},{10,9... | collective-permute-start | bytes 995336 | tf_op jit(solution)/shard_map/ppermute | solution.py:65
  568.6 26.5 %collective-permute-start.65 = (bf16[2,2,72,288]{3,2,1,0:T(8,128)(2,1)S(1)}, bf16[2,2,72,288]{3,2,1,0:T(8,128)(2,1)S(1)}, u32[]{:S(2)}, u32[]{:S(2)}) collective-permute-start(bf16[2,2,72,288]{3,2,1,0:T(8,128)(2,1)S(1)} %dynamic-slice_bitcast_fusion.17), channel_id=1, source_target_pairs={{0,4},{1,5},{2,6},{3,7},{4,0},{5,1},{6,2},{7,3},{8,12},{9,13},{10,... | collective-permute-start | bytes 497672 | tf_op jit(solution)/shard_map/ppermute | solution.py:57
  617.1 12.0 %collective-permute-start.72 = (bf16[72,576]{1,0:T(8,128)(2,1)S(1)}, bf16[72,576]{1,0:T(8,128)(2,1)S(1)}, u32[]{:S(2)}, u32[]{:S(2)}) collective-permute-start(bf16[72,576]{1,0:T(8,128)(2,1)S(1)} %pad_maximum_fusion.14), channel_id=1, source_target_pairs={{0,0},{1,2},{2,1},{3,3},{4,4},{5,6},{6,5},{7,7},{8,8},{9,10},{10,9... | collective-permute-start | bytes 248840 | tf_op jit(solution)/shard_map/ppermute | solution.py:65
  627.0 41.5 %collective-permute-start.48 = (bf16[1152,1024]{1,0:T(8,128)(2,1)S(1)}, bf16[1152,1024]{1,0:T(8,128)(2,1)S(1)}, u32[]{:S(2)}, u32[]{:S(2)}) collective-permute-start(bf16[1152,1024]{1,0:T(8,128)(2,1)S(1)} %copy-done.99), channel_id=1, source_target_pairs={{0,2},{1,3},{2,0},{3,1},{4,6},{5,7},{6,4},{7,5},{8,10},{9,11},{10,... | collective-permute-start | bytes 7077896 | tf_op jit(solution)/shard_map/ppermute | solution.py:57
  633.0 16.4 %collective-permute-start.92 = (bf16[2,2,72,1152]{3,2,1,0:T(8,128)(2,1)S(1)}, bf16[2,2,72,1152]{3,2,1,0:T(8,128)(2,1)S(1)}, u32[]{:S(2)}, u32[]{:S(2)}) collective-permute-start(bf16[2,2,72,1152]{3,2,1,0:T(8,128)(2,1)S(1)} %dynamic-slice_bitcast_fusion.2), channel_id=1, source_target_pairs={{0,1},{1,0},{2,3},{3,2},{4,5},{5,4},{6,7},{7,6},{8,9},{9,8},{10,11... | collective-permute-start | bytes 1990664 | tf_op jit(solution)/shard_map/ppermute | solution.py:57
  634.3 16.5 %collective-permute-start.88 = (bf16[2,2,72,1152]{3,2,1,0:T(8,128)(2,1)S(1)}, bf16[2,2,72,1152]{3,2,1,0:T(8,128)(2,1)S(1)}, u32[]{:S(2)}, u32[]{:S(2)}) collective-permute-start(bf16[2,2,72,1152]{3,2,1,0:T(8,128)(2,1)S(1)} %dynamic-slice_bitcast_fusion.3), channel_id=1, source_target_pairs={{0,4},{1,5},{2,6},{3,7},{4,0},{5,1},{6,2},{7,3},{8,12},{9,13},{10,... | collective-permute-start | bytes 1990664 | tf_op jit(solution)/shard_map/ppermute | solution.py:57
  650.9 16.7 %collective-permute-start.89 = (bf16[2,72,1152]{2,1,0:T(8,128)(2,1)S(1)}, bf16[2,72,1152]{2,1,0:T(8,128)(2,1)S(1)}, u32[]{:S(2)}, u32[]{:S(2)}) collective-permute-start(bf16[2,72,1152]{2,1,0:T(8,128)(2,1)S(1)} %dynamic-slice_bitcast_fusion.11), channel_id=1, source_target_pairs={{0,8},{1,9},{2,10},{3,11},{4,12},{5,13},{6,14},{7,15},{8,0},{9,1},... | collective-permute-start | bytes 995336 | tf_op jit(solution)/shard_map/ppermute | solution.py:57
  658.9 77.4 %collective-permute-start.94 = (bf16[72,1152]{1,0:T(8,128)(2,1)}, bf16[72,1152]{1,0:T(8,128)(2,1)}, u32[]{:S(2)}, u32[]{:S(2)}) collective-permute-start(bf16[72,1152]{1,0:T(8,128)(2,1)} %dynamic-slice_bitcast_fusion.18), channel_id=1, source_target_pairs={{0,16},{1,17},{2,18},{3,19},{4,20},{5,21},{6,22},{7,23},{8,24},{9,... | collective-permute-start | bytes 497672 | tf_op jit(solution)/shard_map/ppermute | solution.py:57
  668.4 72.8 %collective-permute-start.90 = (bf16[72,1152]{1,0:T(8,128)(2,1)}, bf16[72,1152]{1,0:T(8,128)(2,1)}, u32[]{:S(2)}, u32[]{:S(2)}) collective-permute-start(bf16[72,1152]{1,0:T(8,128)(2,1)} %dynamic-slice_bitcast_fusion.19), channel_id=1, source_target_pairs={{0,16},{1,17},{2,18},{3,19},{4,20},{5,21},{6,22},{7,23},{8,24},{9,... | collective-permute-start | bytes 497672 | tf_op jit(solution)/shard_map/ppermute | solution.py:57
  689.2 12.4 %collective-permute-start.59 = (f32[1,4,576]{2,0,1:T(1,128)}, f32[1,4,576]{2,0,1:T(1,128)S(1)}, u32[]{:S(2)}, u32[]{:S(2)}) collective-permute-start(f32[1,4,576]{2,0,1:T(1,128)} %broadcast_in_dim.98), channel_id=1, source_target_pairs={{0,16},{1,17},{2,18},{3,19},{4,20},{5,21},{6,22},{7,23},{8,24},{9,... | collective-permute-start | bytes 27656 | tf_op jit(solution)/shard_map/ppermute | solution.py:57
  701.6 93.5 %collective-permute-start.50 = (bf16[2,2,2,72,864]{4,3,2,1,0:T(8,128)(2,1)}, bf16[2,2,2,72,864]{4,3,2,1,0:T(8,128)(2,1)}, u32[]{:S(2)}, u32[]{:S(2)}) collective-permute-start(bf16[2,2,2,72,864]{4,3,2,1,0:T(8,128)(2,1)} %dynamic-slice_bitcast_fusion.1), channel_id=1, source_target_pairs={{0,1},{1,0},{2,3},{3,2},{4,5},{5,4},{6,7},{7,6},{8,9},{9,8},{10,11... | collective-permute-start | bytes 2985992 | tf_op jit(solution)/shard_map/ppermute | solution.py:57
  701.6 96.5 %collective-permute-start.54 = (bf16[2,2,2,72,864]{4,3,2,1,0:T(8,128)(2,1)}, bf16[2,2,2,72,864]{4,3,2,1,0:T(8,128)(2,1)}, u32[]{:S(2)}, u32[]{:S(2)}) collective-permute-start(bf16[2,2,2,72,864]{4,3,2,1,0:T(8,128)(2,1)} %dynamic-slice_bitcast_fusion), channel_id=1, source_target_pairs={{0,4},{1,5},{2,6},{3,7},{4,0},{5,1},{6,2},{7,3},{8,12},{9,13},{10,... | collective-permute-start | bytes 2985992 | tf_op jit(solution)/shard_map/ppermute | solution.py:57
  706.7 17.3 %collective-permute-start.61 = (f32[2,2,1,4,576]{4,0,1,3,2:T(2,128)S(1)}, f32[2,2,1,4,576]{4,0,1,3,2:T(2,128)S(1)}, u32[]{:S(2)}, u32[]{:S(2)}) collective-permute-start(f32[2,2,1,4,576]{4,0,1,3,2:T(2,128)S(1)} %copy.102), channel_id=1, source_target_pairs={{0,4},{1,5},{2,6},{3,7},{4,0},{5,1},{6,2},{7,3},{8,12},{9,13},{10,... | collective-permute-start | bytes 110600 | tf_op jit(solution)/shard_map/ppermute | solution.py:57
  728.1 110.4 %collective-permute-start.49 = (bf16[576,1024]{1,0:T(8,128)(2,1)}, bf16[576,1024]{1,0:T(8,128)(2,1)}, u32[]{:S(2)}, u32[]{:S(2)}) collective-permute-start(bf16[576,1024]{1,0:T(8,128)(2,1)} %get-tuple-element.89), channel_id=1, source_target_pairs={{0,0},{1,2},{2,1},{3,3},{4,4},{5,6},{6,5},{7,7},{8,8},{9,10},{10,9... | collective-permute-start | bytes 3538952 | tf_op jit(solution)/shard_map/ppermute | solution.py:65
  736.3 14.5 %collective-permute-start.62 = (f32[2,2,2,1,4,576]{5,0,1,2,4,3:T(2,128)S(1)}, f32[2,2,2,1,4,576]{5,0,1,2,4,3:T(2,128)S(1)}, u32[]{:S(2)}, u32[]{:S(2)}) collective-permute-start(f32[2,2,2,1,4,576]{5,0,1,2,4,3:T(2,128)S(1)} %maximum_select_fusion.63), channel_id=1, source_target_pairs={{0,1},{1,0},{2,3},{3,2},{4,5},{5,4},{6,7},{7,6},{8,9},{9,8},{10,11... | collective-permute-start | bytes 221192 | tf_op jit(solution)/shard_map/ppermute | solution.py:57
  741.2 12.5 %collective-permute-start.75 = (f32[2,2,1,10,576]{4,0,1,3,2:T(2,128)S(1)}, f32[2,2,1,10,576]{4,0,1,3,2:T(2,128)S(1)}, u32[]{:S(2)}, u32[]{:S(2)}) collective-permute-start(f32[2,2,1,10,576]{4,0,1,3,2:T(2,128)S(1)} %copy.107), channel_id=1, source_target_pairs={{0,4},{1,5},{2,6},{3,7},{4,0},{5,1},{6,2},{7,3},{8,12},{9,13},{10,... | collective-permute-start | bytes 276488 | tf_op jit(solution)/shard_map/ppermute | solution.py:57
  750.8 20.8 %collective-permute-start.95 = (bf16[72,2304]{1,0:T(8,128)(2,1)}, bf16[72,2304]{1,0:T(8,128)(2,1)}, u32[]{:S(2)}, u32[]{:S(2)}) collective-permute-start(bf16[72,2304]{1,0:T(8,128)(2,1)} %pad_maximum_fusion.12), channel_id=1, source_target_pairs={{0,0},{1,2},{2,1},{3,3},{4,4},{5,6},{6,5},{7,7},{8,8},{9,10},{10,9... | collective-permute-start | bytes 995336 | tf_op jit(solution)/shard_map/ppermute | solution.py:65
  796.5 11.8 %collective-permute-start.51 = (bf16[2,2,72,864]{3,2,1,0:T(8,128)(2,1)S(1)}, bf16[2,2,72,864]{3,2,1,0:T(8,128)(2,1)S(1)}, u32[]{:S(2)}, u32[]{:S(2)}) collective-permute-start(bf16[2,2,72,864]{3,2,1,0:T(8,128)(2,1)S(1)} %dynamic-slice_bitcast_fusion.7), channel_id=1, source_target_pairs={{0,4},{1,5},{2,6},{3,7},{4,0},{5,1},{6,2},{7,3},{8,12},{9,13},{10,... | collective-permute-start | bytes 1493000 | tf_op jit(solution)/shard_map/ppermute | solution.py:57
  799.4 12.5 %collective-permute-start.55 = (bf16[2,2,72,864]{3,2,1,0:T(8,128)(2,1)S(1)}, bf16[2,2,72,864]{3,2,1,0:T(8,128)(2,1)S(1)}, u32[]{:S(2)}, u32[]{:S(2)}) collective-permute-start(bf16[2,2,72,864]{3,2,1,0:T(8,128)(2,1)S(1)} %dynamic-slice_bitcast_fusion.6), channel_id=1, source_target_pairs={{0,1},{1,0},{2,3},{3,2},{4,5},{5,4},{6,7},{7,6},{8,9},{9,8},{10,11... | collective-permute-start | bytes 1493000 | tf_op jit(solution)/shard_map/ppermute | solution.py:57
  (161 other events, 1815.9 us)

commit v2 on v1

v2 whole, which is shorter than its diff:
```python
import functools
import math

import jax
import jax.numpy as jnp
from jax import lax
from jax.experimental import pallas as pl
from jax.experimental.pallas import tpu as pltpu
from jax.sharding import PartitionSpec as P

D = 1152
HEAD = 72
CLASSES = 1001
EPSILON = 1e-06
GELU_COEF = 0.7978845608028654
AXES = ("rz", "ry", "rl", "ch", "cl")
ROW, COL = AXES[:3], AXES[3:]
GROUP = ("rz", "ry", "cl")
F32 = jnp.float32
BF16 = jnp.bfloat16
HIGH = lax.Precision.HIGHEST
LOG2E = math.log2(math.e)
BLOCK = 256
VMEM_LIMIT = 48 * 1024 * 1024


def gelu_tanh(values):
    return (
        0.5 * values * (1.0 + jnp.tanh(GELU_COEF * (values + 0.044715 * values * values * values)))
    )


def mm(left, right):
    return lax.dot_general(left, right, (((1,), (0,)), ((), ())), preferred_element_type=F32)


def mm_tn(left, right):
    return lax.dot_general(left, right, (((0,), (0,)), ((), ())), preferred_element_type=F32)


def mm_nt(left, right):
    return lax.dot_general(left, right, (((1,), (1,)), ((), ())), preferred_element_type=F32)


class Links:
    def __init__(self, rows, cols):
        self.count = rows * cols
        self.col_bits = cols.bit_length() - 1
        self.row_bits = rows.bit_length() - 1
        self.flat = lax.axis_index(AXES)
        self.x = 0
        self.ch = list(range(1, self.col_bits))
        self.core = self.col_bits
        self.rh = list(range(self.core + 1, self.core + self.row_bits))[::-1]
        self.order = {
            "a": self.rh + [self.x],
            "b": self.rh[:-1] + [self.x] + self.rh[-1:],
            "c": [self.x] + self.rh[::-1],
        }

    def bit(self, which):
        return (self.flat >> which) & 1

    def exchange(self, values, which):
        pairs = [(i, i ^ (1 << which)) for i in range(self.count)]
        return lax.ppermute(values, AXES, pairs)

    def swap(self, values):
        low, high = 1, 1 << self.core
        pairs = [
            (i, i ^ (low | high))
            for i in range(self.count)
            if bool(i & low) != bool(i & high)
        ]
        moved = lax.ppermute(values, AXES, pairs)
        return jnp.where(self.bit(self.x) == self.bit(self.core), values, moved)

    def joined(self, mine, theirs, which):
        low = self.bit(which) == 0
        return jnp.where(low, jnp.stack([mine, theirs]), jnp.stack([theirs, mine]))

    def gather(self, values, order):
        for which in order:
            values = self.joined(values, self.exchange(values, which), which)
        return values

    def gather_rows(self, values, stream):
        order = self.order[stream]
        natural = self.rh + [self.x]
        got = self.gather(values, order)
        have = order[::-1]
        tail = list(range(len(have), got.ndim))
        got = got.transpose([have.index(w) for w in natural] + tail)
        return got.reshape((-1,) + values.shape[1:])

    def scatter_rows(self, values, stream, rows):
        natural = self.rh + [self.x]
        sums = values.reshape((2,) * len(natural) + (values.shape[0] // rows,) + values.shape[1:])
        for which in self.order[stream][::-1]:
            axis = natural.index(which)
            natural = natural[:axis] + natural[axis + 1 :]
            own = self.bit(which)
            sent = lax.dynamic_index_in_dim(sums, 1 - own, axis, keepdims=False)
            kept = lax.dynamic_index_in_dim(sums, own, axis, keepdims=False)
            sums = kept + self.exchange(sent, which)
        return sums

    def gather_pair(self, values):
        got = self.gather(values, [self.core] + self.ch)
        return got.reshape((-1,) + values.shape[1:])

    def sum_pair(self, values):
        for which in [self.core] + self.ch:
            values = values + self.exchange(values.astype(BF16), which).astype(F32)
        return values


def norm_forward(values):
    average = jnp.mean(values, axis=0, keepdims=True)
    spread = jnp.mean(values * values, axis=0, keepdims=True) - average * average
    inverse = lax.rsqrt(spread + EPSILON)
    return (values - average) * inverse, inverse


def norm_backward(grad_normed, normed, inverse):
    first = jnp.mean(grad_normed, axis=0, keepdims=True)
    cross = jnp.mean(grad_normed * normed, axis=0, keepdims=True)
    return inverse * (grad_normed - first - normed * cross)


def attend_kernel(q_ref, k_ref, v_ref, out_ref, log_ref, *, block):
    length = q_ref.shape[1]
    scale = LOG2E / math.sqrt(HEAD)
    key_t = k_ref[...].T
    value = v_ref[...]
    for start in range(0, length, block):
        at = slice(start, start + block)
        scores = jnp.dot(key_t, q_ref[:, at], preferred_element_type=F32)
        top = jnp.max(scores, axis=0, keepdims=True)
        powers = jnp.exp2((scores - top) * scale)
        total = jnp.sum(powers, axis=0, keepdims=True)
        out = jnp.dot(value, powers.astype(BF16), preferred_element_type=F32)
        out_ref[:, at] = (out / total).astype(BF16)
        log_ref[0, :, at] = top * scale + jnp.log2(total)


def attend(query, key, value):
    width, length = query.shape
    head = pl.BlockSpec((HEAD, length), lambda h: (h, 0))
    return pl.pallas_call(
        functools.partial(attend_kernel, block=min(BLOCK, length)),
        grid=(width // HEAD,),
        in_specs=[head] * 3,
        out_specs=[head, pl.BlockSpec((1, 1, length), lambda h: (h, 0, 0))],
        out_shape=[
            jax.ShapeDtypeStruct((width, length), BF16),
            jax.ShapeDtypeStruct((width // HEAD, 1, length), F32),
        ],
        compiler_params=pltpu.CompilerParams(vmem_limit_bytes=VMEM_LIMIT),
        cost_estimate=pl.CostEstimate(
            flops=4 * width * length * length,
            transcendentals=width // HEAD * length * length,
            bytes_accessed=8 * width * length,
        ),
        name="attend",
    )(query, key, value)


def attend_back_kernel(q_ref, k_ref, v_ref, log_ref, a_ref, g_ref, dq_ref, dk_ref, dv_ref, s_ref, *, block):
    length = q_ref.shape[1]
    scale = LOG2E / math.sqrt(HEAD)
    unit = 1.0 / math.sqrt(HEAD)
    query_t, key_t, value_t, grad_t = [r[...].T for r in (q_ref, k_ref, v_ref, g_ref)]
    key = k_ref[...]
    delta = jnp.sum(g_ref[...].astype(F32) * a_ref[...].astype(F32), axis=0, keepdims=True)
    grad_key = jnp.zeros((length, HEAD), F32)
    grad_value = jnp.zeros((length, HEAD), F32)
    query_sum = jnp.zeros((HEAD, 1), F32)
    for start in range(0, length, block):
        at = slice(start, start + block)
        scores = jnp.dot(key_t, q_ref[:, at], preferred_element_type=F32)
        soft = jnp.exp2(scores * scale - log_ref[0, :, at])
        grad_soft = jnp.dot(value_t, g_ref[:, at], preferred_element_type=F32)
        grad_scores = (soft * (grad_soft - delta[:, at])).astype(BF16)
        grad_value += jnp.dot(soft.astype(BF16), grad_t[at], preferred_element_type=F32)
        grad_key += jnp.dot(grad_scores, query_t[at], preferred_element_type=F32)
        grad_query = jnp.dot(key, grad_scores, preferred_element_type=F32) * unit
        query_sum += jnp.sum(grad_query, axis=1, keepdims=True)
        dq_ref[:, at] = grad_query.astype(BF16)
    dk_ref[...] = (grad_key * unit).T.astype(BF16)
    grad_value = grad_value.T
    dv_ref[...] = grad_value.astype(BF16)
    s_ref[:, 0:1] = query_sum
    s_ref[:, 1:2] = jnp.sum(grad_value, axis=1, keepdims=True)


def attend_back(query, key, value, log_total, attended, grad_att):
    width, length = query.shape
    heads = width // HEAD
    head = pl.BlockSpec((HEAD, length), lambda h: (h, 0))
    log_spec = pl.BlockSpec((1, 1, length), lambda h: (h, 0, 0))
    array = jax.ShapeDtypeStruct((width, length), BF16)
    grad_query, grad_key, grad_value, sums = pl.pallas_call(
        functools.partial(attend_back_kernel, block=min(BLOCK, length)),
        grid=(heads,),
        in_specs=[head, head, head, log_spec, head, head],
        out_specs=[head, head, head, pl.BlockSpec((HEAD, 2), lambda h: (h, 0))],
        out_shape=[array, array, array, jax.ShapeDtypeStruct((width, 2), F32)],
        compiler_params=pltpu.CompilerParams(vmem_limit_bytes=VMEM_LIMIT),
        cost_estimate=pl.CostEstimate(
            flops=10 * width * length * length,
            transcendentals=heads * length * length,
            bytes_accessed=16 * width * length,
        ),
        name="attend_back",
    )(query, key, value, log_total, attended, grad_att)
    return jnp.concatenate([grad_query, grad_key, grad_value], axis=0), sums.T


def make_on_device(rows, cols):
    def on_device(
        latents,
        labels,
        timesteps,
        label_table,
        ada_weight,
        ada_bias,
        qkv_weight,
        qv_bias,
        proj_weight,
        proj_bias,
        expand_weight,
        expand_bias,
        contract_weight,
        contract_bias,
        cotangent,
    ):
        links = Links(rows, cols)
        after = lambda *v: lax.optimization_barrier(v)
        length = latents.shape[2]
        width = latents.shape[1]
        half = 3 * width // 2
        hidden_width = expand_weight.shape[1]
        hidden_half = hidden_width // 2
        seqs = labels.shape[0]
        chunk = qkv_weight.shape[0]
        row, col = lax.axis_index(ROW), lax.axis_index(COL)
        own_x, own_core = links.bit(links.x), links.bit(links.core)
        part = (col >> 1 << 1) + own_core

        gather = lambda v: lax.all_gather(v, GROUP, axis=0, tiled=True)
        qkv_own = links.swap(qkv_weight.reshape(chunk, 3 * width))
        others = [expand_weight, contract_weight.T, proj_weight.T]
        qkv_own, others = after(qkv_own, jnp.concatenate(others, axis=1))
        qkv_w = gather(qkv_own)
        others = links.swap(others)
        proj_w = links.gather_rows(others[:, 2 * hidden_width :], "a")
        others, latents_own = after(others, latents[0])
        latents_full = links.gather_pair(links.swap(latents_own))
        mlp_w = gather(others[:, : 2 * hidden_width])
        expand_w, contract_w = mlp_w[:, :hidden_width], mlp_w[:, hidden_width:]
        qkv_w, cotangent_own = after(qkv_w, cotangent[0])
        cotangent_full = links.gather_pair(links.swap(cotangent_own))
        bias_rows = [
            qv_bias.astype(F32),
            proj_bias.astype(F32)[None],
            contract_bias.astype(F32)[None],
            expand_bias.astype(F32).reshape(-1, width),
        ]
        bias_own = links.swap(jnp.concatenate(bias_rows, axis=0))
        qv_own = bias_own[:2, :, None]
        pair_bias = links.gather([bias_own[2:4]][0], [links.core] + links.ch)
        pair_bias = pair_bias.reshape(-1, 2, width).transpose(1, 0, 2).reshape(2, D, 1)
        proj_b, contract_b = pair_bias[0], pair_bias[1]
        expand_b = bias_own[4:].reshape(hidden_width, 1)

        feature = col * width + jnp.arange(width, dtype=jnp.int32)
        half_width = D // 2
        frequency = jnp.exp(-math.log(10000.0) * (feature % half_width).astype(F32) / half_width)
        angles = timesteps.astype(F32)[:, None] * frequency[None, :]
        embedding = jnp.where(feature[None, :] < half_width, jnp.cos(angles), jnp.sin(angles))
        label_hits = labels[:, None] == jnp.arange(CLASSES, dtype=jnp.int32)[None, :]
        cond_part = mm_nt(label_hits.astype(BF16), label_table) + embedding
        cond_all = links.gather(cond_part, [links.x] + links.ch)
        cond_all = cond_all.reshape(-1, seqs, width).transpose(1, 0, 2).reshape(seqs, D)
        silu_all = jax.nn.silu(cond_all).astype(BF16)
        flat_ada = ada_weight.reshape(6 * width, D)
        pair = lax.dynamic_slice_in_dim(silu_all, (row >> 1) * 2, 2, 0)
        pair_mod = mm_nt(pair, flat_ada) + ada_bias.astype(F32).reshape(1, 6 * width)
        mine = lax.dynamic_index_in_dim(pair_mod, own_x, 0)
        other = lax.dynamic_index_in_dim(pair_mod, 1 - own_x, 0)
        mod = links.joined(mine, links.exchange(other, links.x), links.x)
        mod = links.gather(mod, links.ch)
        mod = mod.reshape(-1, 6, width).transpose(1, 0, 2).reshape(6, D, 1)
        shift_first, scale_first, gate_first, shift_second, scale_second, gate_second = [
            mod[i] for i in range(6)
        ]
        own_part = lambda v: lax.dynamic_slice_in_dim(v, part * width, width, 0)

        start = latents_full.astype(F32)
        normed_first, inv_first = norm_forward(start)
        in_first = (normed_first * (1.0 + scale_first) + shift_first).astype(BF16)
        triple = mm_tn(qkv_w, in_first)
        query = (triple[:width] + qv_own[0]).astype(BF16)
        key = triple[width : 2 * width].astype(BF16)
        value = (triple[2 * width :] + qv_own[1]).astype(BF16)
        attended, log_total = attend(query, key, value)
        proj_out = links.sum_pair(mm(proj_w, attended)) + proj_b
        residual = start + gate_first * proj_out
        normed_second, inv_second = norm_forward(residual)
        in_second = (normed_second * (1.0 + scale_second) + shift_second).astype(BF16)
        pre_act = mm_tn(expand_w, in_second) + expand_b
        hidden = gelu_tanh(pre_act).astype(BF16)
        scatter = lambda v: lax.psum_scatter(v, GROUP, scatter_dimension=0, tiled=True)
        grad_out = cotangent_full.astype(F32)
        grad_mlp_b = (grad_out * gate_second).astype(BF16)
        contract_term = mm_nt(grad_mlp_b, hidden).astype(BF16)
        grad_hidden = mm_tn(contract_w, grad_mlp_b)
        grad_pre = jax.vjp(gelu_tanh, pre_act)[1](grad_hidden)[0]
        grad_pre_b = grad_pre.astype(BF16)
        expand_term = mm_nt(in_second, grad_pre_b).astype(BF16)
        grad_pre_b, expand_term = after(grad_pre_b, expand_term)
        mlp_grads = scatter(jnp.concatenate([expand_term, contract_term], axis=1))
        grad_in_second = links.sum_pair(mm(expand_w, grad_pre_b))
        grad_residual = grad_out + norm_backward(
            grad_in_second * (1.0 + scale_second), normed_second, inv_second
        )
        grad_proj_out = grad_residual * gate_first
        grad_proj_b = grad_proj_out.astype(BF16)
        proj_term = mm_nt(grad_proj_b, attended).astype(BF16)
        proj_term, grad_proj_b = after(proj_term, grad_proj_b)
        grad_proj = links.scatter_rows(proj_term, "b", rows)
        grad_att = mm_tn(proj_w, grad_proj_b).astype(BF16)
        triple_grad, qv_sums = attend_back(query, key, value, log_total, attended, grad_att)
        qkv_term = mm_nt(in_first, triple_grad).astype(BF16)
        qkv_term, triple_grad = after(qkv_term, triple_grad)
        grad_qkv = [
            links.scatter_rows(qkv_term[:, n : n + half], s, rows) for n, s in ((0, "a"), (half, "b"))
        ]
        grad_in_first = links.sum_pair(mm(qkv_w, triple_grad))
        hidden_late, _ = after(hidden, triple_grad)
        mlp_out = links.sum_pair(mm(contract_w, hidden_late)) + contract_b
        mlp_own = own_part(mlp_out)
        block_own = own_part(residual) + own_part(gate_second) * mlp_own
        block_out = links.swap(block_own.astype(BF16)).astype(F32)[None]
        grad_latents_full = grad_residual + norm_backward(
            grad_in_first * (1.0 + scale_first), normed_first, inv_first
        )
        grad_latents = links.swap(own_part(grad_latents_full).astype(BF16)).astype(F32)[None]

        token_sum = lambda v: jnp.sum(v, axis=1)[None]
        own_out = own_part(grad_out)
        own_in_second = own_part(grad_in_second)
        own_in_first = own_part(grad_in_first)
        early = jnp.concatenate(
            [
                token_sum(own_part(grad_residual) * own_part(proj_out)),
                token_sum(own_in_second),
                token_sum(own_in_second * own_part(normed_second)),
                token_sum(own_out * mlp_own),
                token_sum(own_part(grad_proj_out)),
                token_sum(own_out * own_part(gate_second)),
                jnp.sum(grad_pre, axis=1).reshape(-1, width),
            ],
            axis=0,
        )
        late = jnp.concatenate(
            [
                token_sum(own_in_first),
                token_sum(own_in_first * own_part(normed_first)),
                qv_sums,
            ],
            axis=0,
        )
        wide = lambda v: links.swap(links.gather_rows(v[None], "c"))
        early_all, late_all = wide(early), wide(late)
        grad_mod = jnp.concatenate([late_all[:, :2], early_all[:, :4]], axis=1)
        sums = jnp.sum(early_all[:, 4:], axis=0)
        grad_qv_bias = jnp.sum(late_all[:, 2:4], axis=0)
        grad_proj_bias, grad_contract_bias = sums[0], sums[1]
        grad_expand_bias = sums[2:].reshape(hidden_width)
        grad_ada_bias = jnp.sum(grad_mod, axis=0)
        flat_grad = grad_mod.reshape(seqs, 6 * width)
        grad_ada = lax.dot_general(
            flat_grad, silu_all.astype(F32), (((0,), (0,)), ((), ())), precision=HIGH
        ).reshape(6, width, D)
        grad_silu = jnp.dot(flat_grad, flat_ada.astype(F32), precision=HIGH)
        for which in [links.x] + links.ch:
            grad_silu = grad_silu + links.exchange(grad_silu, which)
        grad_cond_all = jax.vjp(jax.nn.silu, cond_all)[1](grad_silu)[0]
        grad_cond_cols = lax.dynamic_slice_in_dim(grad_cond_all, col * width, width, 1)
        grad_cond = lax.dynamic_slice_in_dim(grad_cond_cols, row, 1, 0)
        grad_table = lax.dot_general(
            grad_cond_cols, label_hits.astype(F32), (((0,), (0,)), ((), ())), precision=HIGH
        )

        grad_qkv = links.swap(jnp.concatenate(grad_qkv, axis=1)).astype(F32)
        mlp_grads = links.swap(mlp_grads)
        grad_expand = mlp_grads[:, :hidden_width].astype(F32)
        grad_contract = mlp_grads[:, hidden_width:].astype(F32).T
        return (
            block_out,
            grad_latents,
            grad_qkv.reshape(chunk, 3, width),
            grad_qv_bias,
            links.swap(grad_proj).astype(F32).T,
            grad_proj_bias,
            grad_expand,
            grad_expand_bias,
            grad_contract,
            grad_contract_bias,
            grad_ada,
            grad_ada_bias,
            grad_cond,
            grad_table,
        )

    return on_device


def solution(mesh):
    rows, cols = mesh.shape["row"], mesh.shape["col"]
    shape = (rows // 4, 2, 2, cols // 2, 2)
    fine = jax.sharding.Mesh(mesh.devices.reshape(shape), AXES)
    row, col = ROW, COL
    in_specs = (
        P(row, col, None),
        P(),
        P(),
        P(col, None),
        P(None, col, None),
        P(None, col),
        P(row, None, col),
        P(None, col),
        P(col, row),
        P(col),
        P(row, col),
        P(col),
        P(col, row),
        P(col),
        P(row, col, None),
    )
    out_specs = (
        P(row, col, None),
        P(row, col, None),
        P(row, None, col),
        P(None, col),
        P(col, row),
        P(col),
        P(row, col),
        P(col),
        P(col, row),
        P(col),
        P(None, col, None),
        P(None, col),
        P(row, col),
        P(col, None),
    )
    return jax.shard_map(
        make_on_device(rows, cols),
        mesh=fine,
        in_specs=in_specs,
        out_specs=out_specs,
        check_vma=False,
    )
```

time: 852 us -> 614 us (0.72)
  matrix products: 206 us -> 124 us
  starting transfers between devices: 174 us -> 92.3 us
  waiting for transfers between devices: 271 us -> 201 us
  Pallas kernels: 0 us -> 47.1 us
  other arithmetic: 121 us -> 83.8 us
  local copies, waits for them, and re-layouts: 67.6 us -> 43.1 us
  between operations: 4.03 us -> 15.6 us
    ppermute x82 -> x34, waiting for transfers between devices: 261 us -> 111 us  [exchange(): return lax.ppermute(values, AXES, pairs)]
    dot_general x12 -> x0, matrix products: 78.6 us -> none  [the longest x2 16.6 us: attend(): jnp.einsum('hdk,hdq->hkq', key, query, preferred_element_type=F32) * scale]
    ppermute x82 -> x34, starting transfers between devices: 107 us -> 37 us  [exchange(): return lax.ppermute(values, AXES, pairs)]
    all_gather x0 -> x2, waiting for transfers between devices: none -> 61.6 us  [on_device(): gather = lambda v: lax.all_gather(v, GROUP, axis=0, tiled=True)]
    pallas_call x0 -> x2, Pallas kernels: none -> 47.1 us  [the longest x1 23.9 us: attend_back(): pl.pallas_call(functools.partial(attend_back_kernel, block=min(BLOCK, len...]
    ppermute x15 -> x12, waiting for transfers between devices: 10 us -> 29 us  [swap(): moved = lax.ppermute(values, AXES, pairs)]
    reduce_sum x4 -> x0, other arithmetic: 17.6 us -> none  [the longest x2 17.1 us: attend(): jnp.sum(jnp.exp(scores - top), axis=1, keepdims=True)]
    select_n x59 -> x17, other arithmetic: 20.4 us -> 5.06 us  [joined(): return jnp.where(low, jnp.stack([mine, theirs]), jnp.stack([theirs, mine]))]
  transfers between devices with their start and end apart: 97 -> 49, of which waited for: 45 -> 26; matrix products, arithmetic and copies ran while one was open for 39% -> 31% of each run, Pallas kernels for 0% -> 8%
where the time goes in v2:
time: 614 us; the launch traced here: 607 us
  waiting for transfers between devices  201 us (33%)
  matrix products  124 us (20%)
  starting transfers between devices  92.3 us (15%)
  other arithmetic  83.8 us (14%)
  Pallas kernels  47.1 us (8%)
  local copies, waits for them, and re-layouts  43.1 us (7%)
  between operations  15.6 us (3%)
    ppermute x34, waiting for transfers between devices, exchange(): return lax.ppermute(values, AXES, pairs)  111 us
    all_gather x2, waiting for transfers between devices, on_device(): gather = lambda v: lax.all_gather(v, GROUP, axis=0, tiled=True)  61.6 us
    ppermute x12, starting transfers between devices, swap(): moved = lax.ppermute(values, AXES, pairs)  55.2 us
    dot_general x4, matrix products, mm_tn(): lax.dot_general(left, right, (((0,), (0,)), ((), ())), preferred_element_...  43.9 us
    ppermute x34, starting transfers between devices, exchange(): return lax.ppermute(values, AXES, pairs)  37 us
    dot_general x4, matrix products, mm(): lax.dot_general(left, right, (((1,), (0,)), ((), ())), preferred_element_...  32.5 us
    dot_general x6, matrix products, mm_nt(): lax.dot_general(left, right, (((1,), (1,)), ((), ())), preferred_element_...  29.7 us
    ppermute x12, waiting for transfers between devices, swap(): moved = lax.ppermute(values, AXES, pairs)  29 us
  transfers between devices with their start and end apart: 49, of which 26 were waited for; matrix products, arithmetic and copies ran while one was open for 31% of the time, Pallas kernels for 8%

profile of v2, /device:TPU:1, one launch (start us, length us, event | category | flops | bytes accessed | tf_op | source)
XLA Modules:
  0.0 606.8 jit_solution(16843734977404047648)
XLA Ops:
  8.7 4.6 collective-permute-start
  14.6 2.8 collective-permute-done
  18.2 3.6 collective-permute-start.1
  21.8 10.6 %collective-permute-done.1 = bf16[72,5184]{1,0:T(8,128)(2,1)S(1)} collective-permute-done((bf16[72,5184]{1,0:T(8,128)(2,1)S(1)}, bf16[72,5184]{1,0:T(8,128)(2,1)S(1)}, u32[]{:S(2)}, u32[]{:S(2)}) %collective-permute-start.1) | collective-permute-done | bytes 746528 | tf_op jit(solution)/shard_map/ppermute | solution.py:75
  33.6 4.2 collective-permute-start.10
  47.7 4.2 collective-permute-done.6
  51.9 3.7 collective-permute-start.7
  55.6 5.5 convolution_add_fusion
  63.6 4.4 collective-permute-done.2
  68.3 4.3 collective-permute-done.8
  76.2 29.3 %collective-permute-done.5 = f32[1,3456]{1,0:T(1,128)S(1)} collective-permute-done((f32[1,3456]{1,0:T(1,128)S(1)}, f32[1,3456]{1,0:T(1,128)S(1)}, u32[]{:S(2)}, u32[]{:S(2)}) %collective-permute-start.5) | collective-permute-done | bytes 13856 | tf_op jit(solution)/shard_map/ppermute | solution.py:66
  110.7 4.5 fusion.6
  115.3 2.9 collective-permute-start.13
  118.2 7.7 %fusion.74 = f32[1728,1024]{1,0:T(8,128)S(1)} fusion(bf16[1152,1728]{1,0:T(8,128)(2,1)} %all-gather.3.cloned.1.call-done, bf16[1152,1024]{1,0:T(8,128)(2,1)} %get-tuple-element.142), kind=kOutput, calls=%fused_computation.229 | convolution fusion | flops 4076863488 | bytes 13418496 | tf_op jit(solution)/shard_map/dot_general | solution.py:38
  126.4 23.2 %attend.1 = (bf16[576,1024]{1,0:T(8,128)(2,1)S(1)}, f32[8,1,1024]{2,1,0:T(1,128)S(1)}) custom-call(bf16[576,1024]{1,0:T(8,128)(2,1)S(1)} %get-tuple-element.134.q_ref, bf16[576,1024]{1,0:T(8,128)(2,1)S(1)} %slice.201.k_ref, bf16[576,1024]{1,0:T(8,128)(2,1)S(1)} %get-tuple-element.133.v_ref), custom_call_target="tpu_custom_call" | custom-call | flops 2415919104 | bytes 4718592 | tf_op jit(solution)/shard_map/attend/pallas_call | solution.py:150
  149.7 5.0 fusion.70
  167.6 2.9 maximum_select_fusion.1
  172.7 6.7 %fusion.64 = (f32[1024]{0:T(1024)S(1)}, f32[1024]{0:T(1024)S(1)}, f32[1152,1024]{1,0:T(8,128)S(1)}, f32[1152,1024]{1,0:T(8,128)}) fusion(f32[1152]{0:T(1024)S(1)} %mul.300, bf16[1,576,1024]{2,1,0:T(8,128)(2,1)S(1)} %bitcast.206, bf16[1,576,1024]{2,1,0:T(8,128)(2,1)S(1)} %bitcast.210, pred[]{:T(512)S(6)} %eq.21, f32[1152]{0:T(1024)S(1)} %copy-done.38, ...), kind=kLoop, calls=%fused_computation.220 | loop fusion | flops 14153728 | bytes 18891776 | tf_op jit(solution)/shard_map/reduce_sum | solution.py:119
  184.2 61.6 %all-gather.5.cloned.1.call-done = bf16[1152,4608]{1,0:T(8,128)(2,1)} async-done(((bf16[72,4608]{1,0:T(8,128)(2,1)}), bf16[1152,4608]{1,0:T(8,128)(2,1)}) %all-gather.5.cloned.1.call-update) | async-done | bytes 10616848 | tf_op jit(solution)/shard_map/all_gather | solution.py:251
  245.8 16.1 %multiply_convert_fusion = (bf16[2304,1024]{0,1:T(8,128)(2,1)}, f32[2304,1024]{0,1:T(8,128)}) fusion(f32[2304]{0:T(1024)S(1)} %copy-done.44, f32[1152,1024]{1,0:T(8,128)} %subtract_multiply_fusion, f32[1152]{0:T(1024)S(1)} %copy-done.49, f32[1152]{0:T(1024)S(1)} %add.372, bf16[1152,4608]{1,0:T(8,128)(2,1)} %all-gather.5.cloned.1.call-done), kind=kOutput, calls=%fused_computation.12 | convolution fusion | flops 5462949888 | bytes 24201216 | tf_op jit(solution)/shard_map/dot_general | solution.py:38
  261.9 17.3 %fusion.67 = (f32[2304]{0:T(1024)S(1)}, bf16[2304,1024]{0,1:T(8,128)(2,1)}) fusion(bf16[1152,1024]{1,0:T(8,128)(2,1)S(1)} %copy-done.21, bf16[1152,4608]{1,0:T(8,128)(2,1)S(1)} %copy-done.55, f32[2304,1024]{0,1:T(8,128)} %get-tuple-element.178, f32[2304]{0:T(1024)S(1)} %copy-done.44), kind=kOutput, calls=%fused_computation.222 | convolution fusion | flops 5497157632 | bytes 21844992 | tf_op jit(solution)/shard_map/dot_general | solution.py:38
  279.3 8.8 %convolution_convert_fusion.1 = bf16[1152,2304]{1,0:T(8,128)(2,1)S(1)} fusion(bf16[2304,1024]{0,1:T(8,128)(2,1)} %get-tuple-element.41, f32[1152,1024]{1,0:T(8,128)S(1)} %bitcast.213, f32[1152]{0:T(1024)S(1)} %copy-done.49, f32[1152]{0:T(1024)S(1)} %add.372), kind=kOutput, calls=%fused_computation.5 | convolution fusion | flops 5442011136 | bytes 14754816 | tf_op jit(solution)/shard_map/dot_general | solution.py:42
  288.1 10.2 %fusion.71 = (bf16[1152,1024]{1,0:T(8,128)(2,1)}, f32[1152,1024]{1,0:T(8,128)}) fusion(bf16[2304,1024]{0,1:T(8,128)(2,1)} %get-tuple-element.41, bf16[1152,4608]{1,0:T(8,128)(2,1)S(1)} %copy-done.55), kind=kOutput, calls=%fused_computation.226 | convolution fusion | flops 5436997632 | bytes 17104896 | tf_op jit(solution)/shard_map/dot_general | solution.py:34
  300.0 5.9 convolution_convert_fusion
  305.9 4.7 pad_maximum_fusion
  313.5 4.4 bitcast_convert_fusion
  318.6 5.3 multiply_reduce_fusion.3
  327.5 6.4 %fusion.66 = (bf16[1152,1024]{1,0:T(8,128)(2,1)S(1)}, f32[1152,1024]{1,0:T(8,128)}, f32[1152,1024]{1,0:T(8,128)}) fusion(f32[1152]{0:T(1024)S(1)} %mul.300, f32[1024]{0:T(1024)S(1)} %get-tuple-element.183, f32[1024]{0:T(1024)S(1)} %get-tuple-element.184, f32[1152,1024]{1,0:T(8,128)S(1)} %get-tuple-element.127, f32[1152]{0:T(1024)S(1)} %add.372, ...), kind=kLoop, calls=%fused_computation.221 | loop fusion | flops 12976128 | bytes 23618560 | tf_op jit(solution)/shard_map/convert_element_type | solution.py:329
  333.9 2.8 convolution_convert_fusion.3
  336.7 2.7 convolution_convert_fusion.4.g_ref
  339.4 23.9 %attend_back.1 = (bf16[576,1024]{1,0:T(8,128)(2,1)S(1)}, bf16[576,1024]{1,0:T(8,128)(2,1)S(1)}, bf16[576,1024]{1,0:T(8,128)(2,1)S(1)}, f32[576,2]{1,0:T(8,128)S(1)}) custom-call(bf16[576,1024]{1,0:T(8,128)(2,1)S(1)} %copy-done.5, bf16[576,1024]{1,0:T(8,128)(2,1)S(1)} %slice.201.k_ref, bf16[576,1024]{1,0:T(8,128)(2,1)} %copy-done.3, ...), custom_call_target="tpu_custom_call" | custom-call | flops 6039797760 | bytes 9437184 | tf_op jit(solution)/shard_map/attend_back/pallas_call | solution.py:203
  365.0 6.3 %convolution_convert_fusion.2 = bf16[1152,1728]{0,1:T(8,128)(2,1)} fusion(bf16[1152,1024]{1,0:T(8,128)(2,1)S(1)} %copy-done.22, bf16[1728,1024]{1,0:T(8,128)(2,1)S(1)} %constant_dynamic-update-slice_fusion), kind=kOutput, calls=%fused_computation.13 | convolution fusion | flops 4078854144 | bytes 9879552 | tf_op jit(solution)/shard_map/dot_general | solution.py:42
  371.3 6.4 %fusion.73 = (bf16[1152,1024]{1,0:T(8,128)(2,1)}, f32[1152,1024]{1,0:T(8,128)}) fusion(bf16[1152,1728]{1,0:T(8,128)(2,1)S(1)} %copy-done.56, bf16[1728,1024]{1,0:T(8,128)(2,1)S(1)} %constant_dynamic-update-slice_fusion), kind=kOutput, calls=%fused_computation.228 | convolution fusion | flops 4078043136 | bytes 14598144 | tf_op jit(solution)/shard_map/dot_general | solution.py:34
  381.2 4.5 fusion.68
  385.7 2.9 copy.74
  390.3 2.9 copy.75
  394.3 8.6 %collective-permute-done.34 = bf16[2,2,2,72,576]{4,3,2,1,0:T(8,128)(2,1)} collective-permute-done((bf16[2,2,2,72,576]{4,3,2,1,0:T(8,128)(2,1)S(1)}, bf16[2,2,2,72,576]{4,3,2,1,0:T(8,128)(2,1)}, u32[]{:S(2)}, u32[]{:S(2)}) %collective-permute-start.34) | collective-permute-done | bytes 663584 | tf_op jit(solution)/shard_map/ppermute | solution.py:66
  406.0 10.9 %fusion.72 = (bf16[1152,1024]{1,0:T(8,128)(2,1)}, f32[1152,1024]{1,0:T(8,128)}) fusion(bf16[2304,1024]{0,1:T(8,128)(2,1)} %get-tuple-element.47, bf16[1152,4608]{1,0:T(8,128)(2,1)} %all-gather.5.cloned.1.call-done), kind=kOutput, calls=%fused_computation.227 | convolution fusion | flops 5436997632 | bytes 17104896 | tf_op jit(solution)/shard_map/dot_general | solution.py:34
  417.0 4.3 collective-permute-start.16
  421.2 9.8 %collective-permute-done.35 = bf16[2,2,72,576]{3,2,1,0:T(8,128)(2,1)S(1)} collective-permute-done((bf16[2,2,72,576]{3,2,1,0:T(8,128)(2,1)S(1)}, bf16[2,2,72,576]{3,2,1,0:T(8,128)(2,1)S(1)}, u32[]{:S(2)}, u32[]{:S(2)}) %collective-permute-start.35) | collective-permute-done | bytes 331808 | tf_op jit(solution)/shard_map/ppermute | solution.py:66
  438.0 3.1 collective-permute-done.37
  441.1 11.3 %collective-permute-start.38 = (bf16[72,576]{1,0:T(8,128)(2,1)S(1)}, bf16[72,576]{1,0:T(8,128)(2,1)}, u32[]{:S(2)}, u32[]{:S(2)}) collective-permute-start(bf16[72,576]{1,0:T(8,128)(2,1)S(1)} %bitcast_add_fusion.12), channel_id=1, source_target_pairs={{1,2},{2,1},{5,6},{6,5},{9,10},{10,9},{13,14},{14,13},{17,18},{18,... | collective-permute-start | bytes 248840 | tf_op jit(solution)/shard_map/ppermute | solution.py:75
  452.6 5.1 collective-permute-done.25
  458.6 12.2 %collective-permute-done.22 = bf16[2,72,864]{2,1,0:T(8,128)(2,1)S(1)} collective-permute-done((bf16[2,72,864]{2,1,0:T(8,128)(2,1)S(1)}, bf16[2,72,864]{2,1,0:T(8,128)(2,1)S(1)}, u32[]{:S(2)}, u32[]{:S(2)}) %collective-permute-start.22) | collective-permute-done | bytes 248864 | tf_op jit(solution)/shard_map/ppermute | solution.py:66
  470.8 4.1 collective-permute-start.23
  474.9 8.7 %collective-permute-done.26 = bf16[2,72,864]{2,1,0:T(8,128)(2,1)S(1)} collective-permute-done((bf16[2,72,864]{2,1,0:T(8,128)(2,1)S(1)}, bf16[2,72,864]{2,1,0:T(8,128)(2,1)S(1)}, u32[]{:S(2)}, u32[]{:S(2)}) %collective-permute-start.26) | collective-permute-done | bytes 248864 | tf_op jit(solution)/shard_map/ppermute | solution.py:66
  484.5 4.0 collective-permute-done.27
  489.4 6.9 %collective-permute-start.28 = (bf16[72,1728]{1,0:T(8,128)(2,1)}, bf16[72,1728]{1,0:T(8,128)(2,1)}, u32[]{:S(2)}, u32[]{:S(2)}) collective-permute-start(bf16[72,1728]{1,0:T(8,128)(2,1)} %pad_maximum_fusion.2), channel_id=1, source_target_pairs={{1,2},{2,1},{5,6},{6,5},{9,10},{10,9},{13,14},{14,13},{17,18},{18,... | collective-permute-start | bytes 746504 | tf_op jit(solution)/shard_map/ppermute | solution.py:75
  506.6 5.8 fusion.63
  512.4 4.1 multiply_reduce_fusion.7
  516.8 3.9 multiply_reduce_fusion.4
  522.4 4.2 collective-permute-start.19
  531.9 2.8 collective-permute-done.31
  538.1 3.6 collective-permute-done.32
  541.7 6.5 %collective-permute-start.33 = (f32[16,4,576]{2,0,1:T(8,128)S(1)}, f32[16,4,576]{2,0,1:T(8,128)S(1)}, u32[]{:S(2)}, u32[]{:S(2)}) collective-permute-start(f32[16,4,576]{2,0,1:T(8,128)S(1)} %copy.101), channel_id=1, source_target_pairs={{1,2},{2,1},{5,6},{6,5},{9,10},{10,9},{13,14},{14,13},{17,18},{18,... | collective-permute-start | bytes 442376 | tf_op jit(solution)/shard_map/ppermute | solution.py:75
  548.7 7.4 %collective-permute-done.42 = f32[2,2,2,1,10,576]{5,2,1,0,4,3:T(2,128)S(1)} collective-permute-done((f32[2,2,2,1,10,576]{5,2,1,0,4,3:T(2,128)S(1)}, f32[2,2,2,1,10,576]{5,2,1,0,4,3:T(2,128)S(1)}, u32[]{:S(2)}, u32[]{:S(2)}) %collective-permute-start.42) | collective-permute-done | bytes 184352 | tf_op jit(solution)/shard_map/ppermute | solution.py:66
  556.6 3.3 collective-permute-start.43
  560.6 5.3 collective-permute-done.43
  566.0 5.5 convolution_bitcast_fusion
  573.3 9.3 %fusion.25 = f32[6,576,1152]{2,1,0:T(8,128)} fusion(bf16[16,1152,1]{1,0,2:T(8,128)(2,1)S(1)} %copy-done.28, f32[6,576,16]{1,0,2:T(8,128)S(1)} %dot_general.70), kind=kOutput, calls=%fused_computation.108 | convolution fusion | flops 764411904 | bytes 16183296 | tf_op jit(solution)/shard_map/dot_general | solution.py:384
  586.6 3.1 collective-permute-start.44
  589.7 2.9 bitcast_convert_fusion.1
  592.6 2.9 bitcast_convert_fusion.2
  595.5 3.3 collective-permute-done.44
  (360 shorter events, 105.2 us)
Async XLA Ops:
  7.2 30.7 %copy-start = (bf16[576,1001]{1,0:T(8,128)(2,1)S(1)}, bf16[576,1001]{1,0:T(8,128)(2,1)}, u32[]{:S(2)}) copy-start(bf16[576,1001]{1,0:T(8,128)(2,1)} %param.18) | copy-start | bytes 3459460
  7.2 108.1 %all-gather.3.cloned.1.call-start = ((), (), s32[]{:S(2)}) async-start(), calls=%async_computation.1 | async-start | bytes 4386816 | tf_op jit(solution)/shard_map/all_gather | solution.py:251
  8.7 24.8 %copy-start.50 = (bf16[2304]{0:T(1024)(128)(2,1)S(1)}, bf16[2304]{0:T(1024)(128)(2,1)}, u32[]{:S(2)}) copy-start(bf16[2304]{0:T(1024)(128)(2,1)} %param.26) | copy-start | bytes 13828
  8.7 24.9 %copy-start.53 = (bf16[576]{0:T(1024)(128)(2,1)S(1)}, bf16[576]{0:T(1024)(128)(2,1)}, u32[]{:S(2)}) copy-start(bf16[576]{0:T(1024)(128)(2,1)} %param.24) | copy-start | bytes 3460
  8.7 24.9 %copy-start.54 = (bf16[576]{0:T(1024)(128)(2,1)S(1)}, bf16[576]{0:T(1024)(128)(2,1)}, u32[]{:S(2)}) copy-start(bf16[576]{0:T(1024)(128)(2,1)} %param.28) | copy-start | bytes 3460
  8.7 24.9 %copy-start.47 = (bf16[2,576]{1,0:T(2,128)(2,1)S(1)}, bf16[2,576]{1,0:T(2,128)(2,1)}, u32[]{:S(2)}) copy-start(bf16[2,576]{1,0:T(2,128)(2,1)} %param.22) | copy-start | bytes 6916
  8.7 29.1 %copy-start.57 = (s32[16]{0:T(128)S(1)}, s32[16]{0:T(128)}, u32[]{:S(2)}) copy-start(s32[16]{0:T(128)} %param.17) | copy-start | bytes 196
  8.7 29.2 %copy-start.51 = (s32[16]{0:T(128)S(1)}, s32[16]{0:T(128)}, u32[]{:S(2)}) copy-start(s32[16]{0:T(128)} %param.16) | copy-start | bytes 196
  8.7 8.6 %collective-permute-start = (bf16[72,1728]{1,0:T(8,128)(2,1)S(1)}, bf16[72,1728]{1,0:T(8,128)(2,1)S(1)}, u32[]{:S(2)}, u32[]{:S(2)}) collective-permute-start(bf16[72,1728]{1,0:T(8,128)(2,1)S(1)} %reshape.1901), channel_id=1, source_target_pairs={{1,2},{2,1},{5,6},{6,5},{9,10},{10,9},{13,14},{14,13},{17,18},{18,... | collective-permute-start | bytes 746504 | tf_op jit(solution)/shard_map/ppermute | solution.py:75
  18.1 227.7 %all-gather.5.cloned.1.call-start = ((), (), s32[]{:S(2)}) async-start(), calls=%async_computation.2 | async-start | bytes 11280384 | tf_op jit(solution)/shard_map/all_gather | solution.py:251
  18.2 14.3 %collective-permute-start.1 = (bf16[72,5184]{1,0:T(8,128)(2,1)S(1)}, bf16[72,5184]{1,0:T(8,128)(2,1)S(1)}, u32[]{:S(2)}, u32[]{:S(2)}) collective-permute-start(bf16[72,5184]{1,0:T(8,128)(2,1)S(1)} %pad_maximum_fusion.1), channel_id=1, source_target_pairs={{1,2},{2,1},{5,6},{6,5},{9,10},{10,9},{13,14},{14,13},{17,18},{18,... | collective-permute-start | bytes 2239496 | tf_op jit(solution)/shard_map/ppermute | solution.py:75
  33.4 553.2 %reduce-scatter.2.cloned.1.call-start = ((), (), s32[]{:S(2)}) async-start(), calls=%async_computation.3 | async-start | bytes 11280384 | tf_op jit(solution)/shard_map/reduce_scatter | solution.py:314
  33.6 6.1 %collective-permute-start.10 = (f32[8,576]{1,0:T(8,128)S(1)}, f32[8,576]{1,0:T(8,128)S(1)}, u32[]{:S(2)}, u32[]{:S(2)}) collective-permute-start(f32[8,576]{1,0:T(8,128)S(1)} %maximum_convert_fusion), channel_id=1, source_target_pairs={{1,2},{2,1},{5,6},{6,5},{9,10},{10,9},{13,14},{14,13},{17,18},{18,... | collective-permute-start | bytes 55304 | tf_op jit(solution)/shard_map/ppermute | solution.py:75
  38.4 3.3 collective-permute-start.4
  42.5 25.4 %collective-permute-start.2 = (bf16[576,1024]{1,0:T(8,128)(2,1)}, bf16[576,1024]{1,0:T(8,128)(2,1)S(1)}, u32[]{:S(2)}, u32[]{:S(2)}) collective-permute-start(bf16[576,1024]{1,0:T(8,128)(2,1)} %bitcast.233), channel_id=1, source_target_pairs={{1,2},{2,1},{5,6},{6,5},{9,10},{10,9},{13,14},{14,13},{17,18},{18,... | collective-permute-start | bytes 3538952 | tf_op jit(solution)/shard_map/ppermute | solution.py:75
  45.2 6.6 %collective-permute-start.6 = (bf16[72,576]{1,0:T(8,128)(2,1)S(1)}, bf16[72,576]{1,0:T(8,128)(2,1)S(1)}, u32[]{:S(2)}, u32[]{:S(2)}) collective-permute-start(bf16[72,576]{1,0:T(8,128)(2,1)S(1)} %get-tuple-element.145), channel_id=1, source_target_pairs={{0,16},{1,17},{2,18},{3,19},{4,20},{5,21},{6,22},{7,23},{8,24},{9,... | collective-permute-start | bytes 248840 | tf_op jit(solution)/shard_map/ppermute | solution.py:66
  51.9 10.3 %collective-permute-start.7 = (bf16[2,72,576]{2,1,0:T(8,128)(2,1)S(1)}, bf16[2,72,576]{2,1,0:T(8,128)(2,1)S(1)}, u32[]{:S(2)}, u32[]{:S(2)}) collective-permute-start(bf16[2,72,576]{2,1,0:T(8,128)(2,1)S(1)} %maximum_select_fusion.10), channel_id=1, source_target_pairs={{0,8},{1,9},{2,10},{3,11},{4,12},{5,13},{6,14},{7,15},{8,0},{9,1},... | collective-permute-start | bytes 497672 | tf_op jit(solution)/shard_map/ppermute | solution.py:66
  62.3 10.3 %collective-permute-start.8 = (bf16[2,2,72,576]{3,2,1,0:T(8,128)(2,1)S(1)}, bf16[2,2,72,576]{3,2,1,0:T(8,128)(2,1)S(1)}, u32[]{:S(2)}, u32[]{:S(2)}) collective-permute-start(bf16[2,2,72,576]{3,2,1,0:T(8,128)(2,1)S(1)} %maximum_select_fusion.7), channel_id=1, source_target_pairs={{0,4},{1,5},{2,6},{3,7},{4,0},{5,1},{6,2},{7,3},{8,12},{9,13},{10,... | collective-permute-start | bytes 995336 | tf_op jit(solution)/shard_map/ppermute | solution.py:66
  68.1 104.6 %copy-start.11 = (bf16[576,1024]{1,0:T(8,128)(2,1)}, bf16[576,1024]{1,0:T(8,128)(2,1)S(1)}, u32[]{:S(2)}) copy-start(bf16[576,1024]{1,0:T(8,128)(2,1)S(1)} %broadcast_select_fusion.1) | copy-start | bytes 3538948
  68.1 41.7 %collective-permute-start.3 = (bf16[576,1024]{1,0:T(8,128)(2,1)S(1)}, bf16[576,1024]{1,0:T(8,128)(2,1)S(1)}, u32[]{:S(2)}, u32[]{:S(2)}) collective-permute-start(bf16[576,1024]{1,0:T(8,128)(2,1)S(1)} %broadcast_select_fusion.1), channel_id=1, source_target_pairs={{0,2},{1,3},{2,0},{3,1},{4,6},{5,7},{6,4},{7,5},{8,10},{9,11},{10,... | collective-permute-start | bytes 3538952 | tf_op jit(solution)/shard_map/ppermute | solution.py:66
  73.7 33.1 %collective-permute-start.9 = (bf16[2,2,2,72,576]{4,3,2,1,0:T(8,128)(2,1)}, bf16[2,2,2,72,576]{4,3,2,1,0:T(8,128)(2,1)}, u32[]{:S(2)}, u32[]{:S(2)}) collective-permute-start(bf16[2,2,2,72,576]{4,3,2,1,0:T(8,128)(2,1)} %maximum_select_fusion.4), channel_id=1, source_target_pairs={{0,1},{1,0},{2,3},{3,2},{4,5},{5,4},{6,7},{7,6},{8,9},{9,8},{10,11... | collective-permute-start | bytes 1990664 | tf_op jit(solution)/shard_map/ppermute | solution.py:66
  73.7 31.7 %collective-permute-start.5 = (f32[1,3456]{1,0:T(1,128)S(1)}, f32[1,3456]{1,0:T(1,128)S(1)}, u32[]{:S(2)}, u32[]{:S(2)}) collective-permute-start(f32[1,3456]{1,0:T(1,128)S(1)} %get-tuple-element.161), channel_id=1, source_target_pairs={{0,1},{1,0},{2,3},{3,2},{4,5},{5,4},{6,7},{7,6},{8,9},{9,8},{10,11... | collective-permute-start | bytes 41480 | tf_op jit(solution)/shard_map/ppermute | solution.py:66
  115.3 39.4 %collective-permute-start.13 = (bf16[576,1024]{1,0:T(8,128)(2,1)}, bf16[576,1024]{1,0:T(8,128)(2,1)S(1)}, u32[]{:S(2)}, u32[]{:S(2)}) collective-permute-start(bf16[576,1024]{1,0:T(8,128)(2,1)} %bitcast.24), channel_id=1, source_target_pairs={{1,2},{2,1},{5,6},{6,5},{9,10},{10,9},{13,14},{14,13},{17,18},{18,... | collective-permute-start | bytes 3538952 | tf_op jit(solution)/shard_map/ppermute | solution.py:75
  149.7 184.2 %copy-start.2 = (bf16[576,1024]{1,0:T(8,128)(2,1)}, bf16[576,1024]{1,0:T(8,128)(2,1)S(1)}, u32[]{:S(2)}) copy-start(bf16[576,1024]{1,0:T(8,128)(2,1)S(1)} %get-tuple-element.37.a_ref) | copy-start | bytes 3538948
  154.7 17.7 %collective-permute-start.11 = (bf16[1152,1024]{1,0:T(8,128)(2,1)}, bf16[1152,1024]{1,0:T(8,128)(2,1)}, u32[]{:S(2)}, u32[]{:S(2)}) collective-permute-start(bf16[1152,1024]{1,0:T(8,128)(2,1)} %get-tuple-element.172), channel_id=1, source_target_pairs={{0,2},{1,3},{2,0},{3,1},{4,6},{5,7},{6,4},{7,5},{8,10},{9,11},{10,... | collective-permute-start | bytes 7077896 | tf_op jit(solution)/shard_map/ppermute | solution.py:66
  155.8 11.7 %collective-permute-start.14 = (bf16[576,1024]{1,0:T(8,128)(2,1)}, bf16[576,1024]{1,0:T(8,128)(2,1)}, u32[]{:S(2)}, u32[]{:S(2)}) collective-permute-start(bf16[576,1024]{1,0:T(8,128)(2,1)} %broadcast_select_fusion), channel_id=1, source_target_pairs={{0,2},{1,3},{2,0},{3,1},{4,6},{5,7},{6,4},{7,5},{8,10},{9,11},{10,... | collective-permute-start | bytes 3538952 | tf_op jit(solution)/shard_map/ppermute | solution.py:66
  158.2 3.0 collective-permute-start.12
  181.5 64.3 %copy-start.44 = (f32[2304]{0:T(1024)S(1)}, f32[2304]{0:T(1024)}, u32[]{:S(2)}) copy-start(f32[2304]{0:T(1024)} %add.376) | copy-start | bytes 27652
  181.5 64.3 %copy-start.49 = (f32[1152]{0:T(1024)S(1)}, f32[1152]{0:T(1024)}, u32[]{:S(2)}) copy-start(f32[1152]{0:T(1024)} %add.373) | copy-start | bytes 13828
  245.8 33.5 %slice-start.2 = ((s8[4718592]{0:T(1024)(128)(4,1)}), s8[4194304]{0:T(1024)(128)(4,1)S(1)}, s32[]{:S(2)}) async-start(s8[4718592]{0:T(1024)(128)(4,1)} %bitcast.212), calls=%async_computation.6 | async-start | bytes 8388608
  298.2 20.3 %collective-permute-start.15 = (bf16[1152,1024]{1,0:T(8,128)(2,1)}, bf16[1152,1024]{1,0:T(8,128)(2,1)}, u32[]{:S(2)}, u32[]{:S(2)}) collective-permute-start(bf16[1152,1024]{1,0:T(8,128)(2,1)} %get-tuple-element.175), channel_id=1, source_target_pairs={{0,2},{1,3},{2,0},{3,1},{4,6},{5,7},{6,4},{7,5},{8,10},{9,11},{10,... | collective-permute-start | bytes 7077896 | tf_op jit(solution)/shard_map/ppermute | solution.py:66
  377.7 128.8 %collective-permute-start.18 = (bf16[1152,1024]{1,0:T(8,128)(2,1)}, bf16[1152,1024]{1,0:T(8,128)(2,1)}, u32[]{:S(2)}, u32[]{:S(2)}) collective-permute-start(bf16[1152,1024]{1,0:T(8,128)(2,1)} %get-tuple-element.181), channel_id=1, source_target_pairs={{0,2},{1,3},{2,0},{3,1},{4,6},{5,7},{6,4},{7,5},{8,10},{9,11},{10,... | collective-permute-start | bytes 7077896 | tf_op jit(solution)/shard_map/ppermute | solution.py:66
  379.9 23.0 %collective-permute-start.34 = (bf16[2,2,2,72,576]{4,3,2,1,0:T(8,128)(2,1)S(1)}, bf16[2,2,2,72,576]{4,3,2,1,0:T(8,128)(2,1)}, u32[]{:S(2)}, u32[]{:S(2)}) collective-permute-start(bf16[2,2,2,72,576]{4,3,2,1,0:T(8,128)(2,1)S(1)} %dynamic-slice_bitcast_fusion.2), channel_id=1, source_target_pairs={{0,4},{1,5},{2,6},{3,7},{4,0},{5,1},{6,2},{7,3},{8,12},{9,13},{10,... | collective-permute-start | bytes 1990664 | tf_op jit(solution)/shard_map/ppermute | solution.py:66
  389.8 41.8 %collective-permute-start.20 = (bf16[2,2,2,72,864]{4,3,2,1,0:T(8,128)(2,1)}, bf16[2,2,2,72,864]{4,3,2,1,0:T(8,128)(2,1)}, u32[]{:S(2)}, u32[]{:S(2)}) collective-permute-start(bf16[2,2,2,72,864]{4,3,2,1,0:T(8,128)(2,1)} %dynamic-slice_bitcast_fusion.1), channel_id=1, source_target_pairs={{0,1},{1,0},{2,3},{3,2},{4,5},{5,4},{6,7},{7,6},{8,9},{9,8},{10,11... | collective-permute-start | bytes 2985992 | tf_op jit(solution)/shard_map/ppermute | solution.py:66
  393.3 40.9 %collective-permute-start.24 = (bf16[2,2,2,72,864]{4,3,2,1,0:T(8,128)(2,1)S(1)}, bf16[2,2,2,72,864]{4,3,2,1,0:T(8,128)(2,1)S(1)}, u32[]{:S(2)}, u32[]{:S(2)}) collective-permute-start(bf16[2,2,2,72,864]{4,3,2,1,0:T(8,128)(2,1)S(1)} %dynamic-slice_bitcast_fusion), channel_id=1, source_target_pairs={{0,4},{1,5},{2,6},{3,7},{4,0},{5,1},{6,2},{7,3},{8,12},{9,13},{10,... | collective-permute-start | bytes 2985992 | tf_op jit(solution)/shard_map/ppermute | solution.py:66
  404.4 27.3 %copy-start.17 = (bf16[1152,864]{1,0:T(8,128)(2,1)S(1)}, bf16[1152,864]{1,0:T(8,128)(2,1)}, u32[]{:S(2)}) copy-start(bf16[1152,864]{1,0:T(8,128)(2,1)} %copy-done.16) | copy-start | bytes 5971972
  404.4 26.7 %collective-permute-start.35 = (bf16[2,2,72,576]{3,2,1,0:T(8,128)(2,1)S(1)}, bf16[2,2,72,576]{3,2,1,0:T(8,128)(2,1)S(1)}, u32[]{:S(2)}, u32[]{:S(2)}) collective-permute-start(bf16[2,2,72,576]{3,2,1,0:T(8,128)(2,1)S(1)} %dynamic-slice_bitcast_fusion.5), channel_id=1, source_target_pairs={{0,1},{1,0},{2,3},{3,2},{4,5},{5,4},{6,7},{7,6},{8,9},{9,8},{10,11... | collective-permute-start | bytes 995336 | tf_op jit(solution)/shard_map/ppermute | solution.py:66
  417.0 99.7 %collective-permute-start.16 = (bf16[1152,1024]{1,0:T(8,128)(2,1)}, bf16[1152,1024]{1,0:T(8,128)(2,1)}, u32[]{:S(2)}, u32[]{:S(2)}) collective-permute-start(bf16[1152,1024]{1,0:T(8,128)(2,1)} %get-tuple-element.179), channel_id=1, source_target_pairs={{0,2},{1,3},{2,0},{3,1},{4,6},{5,7},{6,4},{7,5},{8,10},{9,11},{10,... | collective-permute-start | bytes 7077896 | tf_op jit(solution)/shard_map/ppermute | solution.py:66
  431.1 4.5 collective-permute-start.36
  431.6 64.6 %slice-start.4 = ((s8[4718592]{0:T(1024)(128)(4,1)}), s8[524288]{0:T(1024)(128)(4,1)S(1)}, s32[]{:S(2)}) async-start(s8[4718592]{0:T(1024)(128)(4,1)} %bitcast.214), calls=%async_computation.8 | async-start | bytes 1048576
  433.1 19.3 %collective-permute-start.21 = (bf16[2,2,72,864]{3,2,1,0:T(8,128)(2,1)S(1)}, bf16[2,2,72,864]{3,2,1,0:T(8,128)(2,1)S(1)}, u32[]{:S(2)}, u32[]{:S(2)}) collective-permute-start(bf16[2,2,72,864]{3,2,1,0:T(8,128)(2,1)S(1)} %dynamic-slice_bitcast_fusion.4), channel_id=1, source_target_pairs={{0,4},{1,5},{2,6},{3,7},{4,0},{5,1},{6,2},{7,3},{8,12},{9,13},{10,... | collective-permute-start | bytes 1493000 | tf_op jit(solution)/shard_map/ppermute | solution.py:66
  435.6 60.6 %slice-start.5 = ((s8[4718592]{0:T(1024)(128)(4,1)}), s8[4194304]{0:T(1024)(128)(4,1)S(1)}, s32[]{:S(2)}) async-start(s8[4718592]{0:T(1024)(128)(4,1)} %bitcast.214), calls=%async_computation.9 | async-start | bytes 8388608
  435.7 5.5 collective-permute-start.37
  436.9 20.8 %collective-permute-start.25 = (bf16[2,2,72,864]{3,2,1,0:T(8,128)(2,1)S(1)}, bf16[2,2,72,864]{3,2,1,0:T(8,128)(2,1)S(1)}, u32[]{:S(2)}, u32[]{:S(2)}) collective-permute-start(bf16[2,2,72,864]{3,2,1,0:T(8,128)(2,1)S(1)} %dynamic-slice_bitcast_fusion.3), channel_id=1, source_target_pairs={{0,1},{1,0},{2,3},{3,2},{4,5},{5,4},{6,7},{7,6},{8,9},{9,8},{10,11... | collective-permute-start | bytes 1493000 | tf_op jit(solution)/shard_map/ppermute | solution.py:66
  441.1 56.1 %collective-permute-start.38 = (bf16[72,576]{1,0:T(8,128)(2,1)S(1)}, bf16[72,576]{1,0:T(8,128)(2,1)}, u32[]{:S(2)}, u32[]{:S(2)}) collective-permute-start(bf16[72,576]{1,0:T(8,128)(2,1)S(1)} %bitcast_add_fusion.12), channel_id=1, source_target_pairs={{1,2},{2,1},{5,6},{6,5},{9,10},{10,9},{13,14},{14,13},{17,18},{18,... | collective-permute-start | bytes 248840 | tf_op jit(solution)/shard_map/ppermute | solution.py:75
  452.5 18.2 %collective-permute-start.22 = (bf16[2,72,864]{2,1,0:T(8,128)(2,1)S(1)}, bf16[2,72,864]{2,1,0:T(8,128)(2,1)S(1)}, u32[]{:S(2)}, u32[]{:S(2)}) collective-permute-start(bf16[2,72,864]{2,1,0:T(8,128)(2,1)S(1)} %dynamic-slice_bitcast_fusion.7), channel_id=1, source_target_pairs={{0,8},{1,9},{2,10},{3,11},{4,12},{5,13},{6,14},{7,15},{8,0},{9,1},... | collective-permute-start | bytes 746504 | tf_op jit(solution)/shard_map/ppermute | solution.py:66
  457.9 25.8 %collective-permute-start.26 = (bf16[2,72,864]{2,1,0:T(8,128)(2,1)S(1)}, bf16[2,72,864]{2,1,0:T(8,128)(2,1)S(1)}, u32[]{:S(2)}, u32[]{:S(2)}) collective-permute-start(bf16[2,72,864]{2,1,0:T(8,128)(2,1)S(1)} %dynamic-slice_bitcast_fusion.6), channel_id=1, source_target_pairs={{0,8},{1,9},{2,10},{3,11},{4,12},{5,13},{6,14},{7,15},{8,0},{9,1},... | collective-permute-start | bytes 746504 | tf_op jit(solution)/shard_map/ppermute | solution.py:66
  470.8 13.6 %collective-permute-start.23 = (bf16[72,864]{1,0:T(8,128)(2,1)S(1)}, bf16[72,864]{1,0:T(8,128)(2,1)S(1)}, u32[]{:S(2)}, u32[]{:S(2)}) collective-permute-start(bf16[72,864]{1,0:T(8,128)(2,1)S(1)} %dynamic-slice_bitcast_fusion.10), channel_id=1, source_target_pairs={{0,16},{1,17},{2,18},{3,19},{4,20},{5,21},{6,22},{7,23},{8,24},{9,... | collective-permute-start | bytes 373256 | tf_op jit(solution)/shard_map/ppermute | solution.py:66
  483.7 4.8 collective-permute-start.27
  489.4 11.0 %collective-permute-start.28 = (bf16[72,1728]{1,0:T(8,128)(2,1)}, bf16[72,1728]{1,0:T(8,128)(2,1)}, u32[]{:S(2)}, u32[]{:S(2)}) collective-permute-start(bf16[72,1728]{1,0:T(8,128)(2,1)} %pad_maximum_fusion.2), channel_id=1, source_target_pairs={{1,2},{2,1},{5,6},{6,5},{9,10},{10,9},{13,14},{14,13},{17,18},{18,... | collective-permute-start | bytes 746504 | tf_op jit(solution)/shard_map/ppermute | solution.py:75
  516.6 11.9 %collective-permute-start.29 = (f32[1,4,576]{2,1,0:T(4,128)S(1)}, f32[1,4,576]{2,1,0:T(4,128)S(1)}, u32[]{:S(2)}, u32[]{:S(2)}) collective-permute-start(f32[1,4,576]{2,1,0:T(4,128)S(1)} %get-tuple-element.167), channel_id=1, source_target_pairs={{0,1},{1,0},{2,3},{3,2},{4,5},{5,4},{6,7},{7,6},{8,9},{9,8},{10,11... | collective-permute-start | bytes 27656 | tf_op jit(solution)/shard_map/ppermute | solution.py:66
  520.9 8.7 %collective-permute-start.39 = (f32[1,10,576]{2,0,1:T(1,128)S(1)}, f32[1,10,576]{2,0,1:T(1,128)S(1)}, u32[]{:S(2)}, u32[]{:S(2)}) collective-permute-start(f32[1,10,576]{2,0,1:T(1,128)S(1)} %broadcast_in_dim.88), channel_id=1, source_target_pairs={{0,1},{1,0},{2,3},{3,2},{4,5},{5,4},{6,7},{7,6},{8,9},{9,8},{10,11... | collective-permute-start | bytes 69128 | tf_op jit(solution)/shard_map/ppermute | solution.py:66
  522.4 67.2 %collective-permute-start.19 = (bf16[576,1024]{1,0:T(8,128)(2,1)S(1)}, bf16[576,1024]{1,0:T(8,128)(2,1)}, u32[]{:S(2)}, u32[]{:S(2)}) collective-permute-start(bf16[576,1024]{1,0:T(8,128)(2,1)S(1)} %get-tuple-element.136), channel_id=1, source_target_pairs={{1,2},{2,1},{5,6},{6,5},{9,10},{10,9},{13,14},{14,13},{17,18},{18,... | collective-permute-start | bytes 3538952 | tf_op jit(solution)/shard_map/ppermute | solution.py:75
  526.6 66.0 %collective-permute-start.17 = (bf16[576,1024]{1,0:T(8,128)(2,1)}, bf16[576,1024]{1,0:T(8,128)(2,1)}, u32[]{:S(2)}, u32[]{:S(2)}) collective-permute-start(bf16[576,1024]{1,0:T(8,128)(2,1)} %get-tuple-element.132), channel_id=1, source_target_pairs={{1,2},{2,1},{5,6},{6,5},{9,10},{10,9},{13,14},{14,13},{17,18},{18,... | collective-permute-start | bytes 3538952 | tf_op jit(solution)/shard_map/ppermute | solution.py:75
  528.6 3.2 collective-permute-start.30
  529.8 6.5 %collective-permute-start.40 = (f32[2,1,10,576]{3,0,2,1:T(2,128)S(1)}, f32[2,1,10,576]{3,0,2,1:T(2,128)S(1)}, u32[]{:S(2)}, u32[]{:S(2)}) collective-permute-start(f32[2,1,10,576]{3,0,2,1:T(2,128)S(1)} %copy.93), channel_id=1, source_target_pairs={{0,4},{1,5},{2,6},{3,7},{4,0},{5,1},{6,2},{7,3},{8,12},{9,13},{10,... | collective-permute-start | bytes 138248 | tf_op jit(solution)/shard_map/ppermute | solution.py:66
  531.8 2.9 collective-permute-start.31
  534.8 6.9 %collective-permute-start.32 = (f32[2,2,2,1,4,576]{5,4,3,2,1,0:T(4,128)S(1)}, f32[2,2,2,1,4,576]{5,4,3,2,1,0:T(4,128)S(1)}, u32[]{:S(2)}, u32[]{:S(2)}) collective-permute-start(f32[2,2,2,1,4,576]{5,4,3,2,1,0:T(4,128)S(1)} %maximum_select_fusion.16), channel_id=1, source_target_pairs={{0,16},{1,17},{2,18},{3,19},{4,20},{5,21},{6,22},{7,23},{8,24},{9,... | collective-permute-start | bytes 221192 | tf_op jit(solution)/shard_map/ppermute | solution.py:66
  536.5 11.8 %collective-permute-start.41 = (f32[2,2,1,10,576]{4,1,0,3,2:T(2,128)S(1)}, f32[2,2,1,10,576]{4,1,0,3,2:T(2,128)S(1)}, u32[]{:S(2)}, u32[]{:S(2)}) collective-permute-start(f32[2,2,1,10,576]{4,1,0,3,2:T(2,128)S(1)} %copy.94), channel_id=1, source_target_pairs={{0,8},{1,9},{2,10},{3,11},{4,12},{5,13},{6,14},{7,15},{8,0},{9,1},... | collective-permute-start | bytes 276488 | tf_op jit(solution)/shard_map/ppermute | solution.py:66
  541.7 18.2 %collective-permute-start.33 = (f32[16,4,576]{2,0,1:T(8,128)S(1)}, f32[16,4,576]{2,0,1:T(8,128)S(1)}, u32[]{:S(2)}, u32[]{:S(2)}) collective-permute-start(f32[16,4,576]{2,0,1:T(8,128)S(1)} %copy.101), channel_id=1, source_target_pairs={{1,2},{2,1},{5,6},{6,5},{9,10},{10,9},{13,14},{14,13},{17,18},{18,... | collective-permute-start | bytes 442376 | tf_op jit(solution)/shard_map/ppermute | solution.py:75
  548.4 7.8 %collective-permute-start.42 = (f32[2,2,2,1,10,576]{5,2,1,0,4,3:T(2,128)S(1)}, f32[2,2,2,1,10,576]{5,2,1,0,4,3:T(2,128)S(1)}, u32[]{:S(2)}, u32[]{:S(2)}) collective-permute-start(f32[2,2,2,1,10,576]{5,2,1,0,4,3:T(2,128)S(1)} %maximum_select_fusion.8), channel_id=1, source_target_pairs={{0,16},{1,17},{2,18},{3,19},{4,20},{5,21},{6,22},{7,23},{8,24},{9,... | collective-permute-start | bytes 552968 | tf_op jit(solution)/shard_map/ppermute | solution.py:66
  556.6 9.3 %collective-permute-start.43 = (f32[16,10,576]{2,0,1:T(8,128)S(1)}, f32[16,10,576]{2,0,1:T(8,128)S(1)}, u32[]{:S(2)}, u32[]{:S(2)}) collective-permute-start(f32[16,10,576]{2,0,1:T(8,128)S(1)} %select_n.660), channel_id=1, source_target_pairs={{1,2},{2,1},{5,6},{6,5},{9,10},{10,9},{13,14},{14,13},{17,18},{18,... | collective-permute-start | bytes 1105928 | tf_op jit(solution)/shard_map/ppermute | solution.py:75
  571.5 11.8 %collective-permute-start.45 = (f32[16,1152]{1,0:T(8,128)S(1)}, f32[16,1152]{1,0:T(8,128)S(1)}, u32[]{:S(2)}, u32[]{:S(2)}) collective-permute-start(f32[16,1152]{1,0:T(8,128)S(1)} %convolution_bitcast_fusion), channel_id=1, source_target_pairs={{0,1},{1,0},{2,3},{3,2},{4,5},{5,4},{6,7},{7,6},{8,9},{9,8},{10,11... | collective-permute-start | bytes 221192 | tf_op jit(solution)/shard_map/ppermute | solution.py:66
  586.6 12.2 %collective-permute-start.44 = (bf16[72,4608]{1,0:T(8,128)(2,1)}, bf16[72,4608]{1,0:T(8,128)(2,1)S(1)}, u32[]{:S(2)}, u32[]{:S(2)}) collective-permute-start(bf16[72,4608]{1,0:T(8,128)(2,1)} %reduce-scatter.2.cloned.1.call-done), channel_id=1, source_target_pairs={{1,2},{2,1},{5,6},{6,5},{9,10},{10,9},{13,14},{14,13},{17,18},{18,... | collective-permute-start | bytes 1990664 | tf_op jit(solution)/shard_map/ppermute | solution.py:75
  (52 other events, 468.6 us)
Sparse Core Ops, SparseCore 0:
  18.3 90.3 all-gather.2
  112.0 133.7 all-gather.4
  310.7 206.4 reduce-scatter.1

commit v3 on v2

--- a/solution.py
+++ b/solution.py
@@ -93,16 +93,23 @@
         got = got.transpose([have.index(w) for w in natural] + tail)
         return got.reshape((-1,) + values.shape[1:])
 
+    def halves(self, sums, natural, which):
+        axis = natural.index(which)
+        own = self.bit(which)
+        sent = lax.dynamic_index_in_dim(sums, 1 - own, axis, keepdims=False)
+        kept = lax.dynamic_index_in_dim(sums, own, axis, keepdims=False)
+        return kept, self.exchange(sent, which), natural[:axis] + natural[axis + 1 :]
+
+    def split_rows(self, values, rows):
+        natural = self.rh + [self.x]
+        shape = (2,) * len(natural) + (values.shape[0] // rows,) + values.shape[1:]
+        return values.reshape(shape), natural
+
     def scatter_rows(self, values, stream, rows):
-        natural = self.rh + [self.x]
-        sums = values.reshape((2,) * len(natural) + (values.shape[0] // rows,) + values.shape[1:])
+        sums, natural = self.split_rows(values, rows)
         for which in self.order[stream][::-1]:
-            axis = natural.index(which)
-            natural = natural[:axis] + natural[axis + 1 :]
-            own = self.bit(which)
-            sent = lax.dynamic_index_in_dim(sums, 1 - own, axis, keepdims=False)
-            kept = lax.dynamic_index_in_dim(sums, own, axis, keepdims=False)
-            sums = kept + self.exchange(sent, which)
+            kept, got, natural = self.halves(sums, natural, which)
+            sums = kept + got
         return sums
 
     def gather_pair(self, values):
@@ -334,51 +341,67 @@
         triple_grad, qv_sums = attend_back(query, key, value, log_total, attended, grad_att)
         qkv_term = mm_nt(in_first, triple_grad).astype(BF16)
         qkv_term, triple_grad = after(qkv_term, triple_grad)
-        grad_qkv = [
-            links.scatter_rows(qkv_term[:, n : n + half], s, rows) for n, s in ((0, "a"), (half, "b"))
+        streams = [
+            (*links.split_rows(qkv_term[:, n : n + half], rows), links.order[s][::-1])
+            for n, s in ((0, "a"), (half, "b"))
         ]
+
+        def send():
+            return [links.halves(sums, natural, order[0]) for sums, natural, order in streams]
+
+        def add(sent, *others):
+            done = after(*[got for _, got, _ in sent], *others)
+            for i, (kept, _, natural) in enumerate(sent):
+                streams[i] = (kept + done[i], natural, streams[i][2][1:])
+            return done[len(sent) :]
+
+        sent = send()
         grad_in_first = links.sum_pair(mm(qkv_w, triple_grad))
+        grad_latents_full = grad_residual + norm_backward(
+            grad_in_first * (1.0 + scale_first), normed_first, inv_first
+        )
+        grad_latents_own = own_part(grad_latents_full).astype(BF16)
+        grad_in_first, grad_latents_own = add(sent, grad_in_first, grad_latents_own)
+        sent = send()
         hidden_late, _ = after(hidden, triple_grad)
         mlp_out = links.sum_pair(mm(contract_w, hidden_late)) + contract_b
         mlp_own = own_part(mlp_out)
         block_own = own_part(residual) + own_part(gate_second) * mlp_own
-        block_out = links.swap(block_own.astype(BF16)).astype(F32)[None]
-        grad_latents_full = grad_residual + norm_backward(
-            grad_in_first * (1.0 + scale_first), normed_first, inv_first
-        )
-        grad_latents = links.swap(own_part(grad_latents_full).astype(BF16)).astype(F32)[None]
+        grad_latents_moved = links.swap(grad_latents_own)
 
         token_sum = lambda v: jnp.sum(v, axis=1)[None]
         own_out = own_part(grad_out)
         own_in_second = own_part(grad_in_second)
         own_in_first = own_part(grad_in_first)
-        early = jnp.concatenate(
+        tokens = jnp.concatenate(
             [
+                token_sum(own_in_first),
+                token_sum(own_in_first * own_part(normed_first)),
                 token_sum(own_part(grad_residual) * own_part(proj_out)),
                 token_sum(own_in_second),
                 token_sum(own_in_second * own_part(normed_second)),
                 token_sum(own_out * mlp_own),
+                qv_sums,
                 token_sum(own_part(grad_proj_out)),
                 token_sum(own_out * own_part(gate_second)),
                 jnp.sum(grad_pre, axis=1).reshape(-1, width),
             ],
             axis=0,
         )
-        late = jnp.concatenate(
-            [
-                token_sum(own_in_first),
-                token_sum(own_in_first * own_part(normed_first)),
-                qv_sums,
-            ],
-            axis=0,
-        )
-        wide = lambda v: links.swap(links.gather_rows(v[None], "c"))
-        early_all, late_all = wide(early), wide(late)
-        grad_mod = jnp.concatenate([late_all[:, :2], early_all[:, :4]], axis=1)
-        sums = jnp.sum(early_all[:, 4:], axis=0)
-        grad_qv_bias = jnp.sum(late_all[:, 2:4], axis=0)
-        grad_proj_bias, grad_contract_bias = sums[0], sums[1]
-        grad_expand_bias = sums[2:].reshape(hidden_width)
+        tokens, grad_latents_moved = add(sent, tokens, grad_latents_moved)
+        sent = send()
+        grad_latents = grad_latents_moved.astype(F32)[None]
+        block_moved = links.swap(block_own.astype(BF16))
+        tokens_all = links.swap(links.gather_rows(tokens[None], "c"))
+        tokens_all, block_moved = add(sent, tokens_all, block_moved)
+        block_out = block_moved.astype(F32)[None]
+        while streams[0][2]:
+            add(send())
+        grad_qkv = [sums for sums, _, _ in streams]
+        grad_mod = tokens_all[:, :6]
+        sums = jnp.sum(tokens_all[:, 6:], axis=0)
+        grad_qv_bias, grad_proj_bias, grad_contract_bias = sums[:2], sums[2], sums[3]
+        grad_expand_bias = sums[4:].reshape(hidden_width)
         grad_ada_bias = jnp.sum(grad_mod, axis=0)
         flat_grad = grad_mod.reshape(seqs, 6 * width)
         grad_ada = lax.dot_general(

time: 614 us -> 593 us (0.966)
  starting transfers between devices: 92.3 us -> 68 us
  local copies, waits for them, and re-layouts: 43.1 us -> 57.3 us
  waiting for transfers between devices: 201 us -> 187 us
    ppermute x34 -> x30, waiting for transfers between devices: 111 us -> 81.1 us  [exchange(): return lax.ppermute(values, AXES, pairs)]
    ppermute x12 -> x11, starting transfers between devices: 55.2 us -> 39.7 us  [swap(): moved = lax.ppermute(values, AXES, pairs)]
    ppermute x12 -> x11, waiting for transfers between devices: 29 us -> 41.1 us  [swap(): moved = lax.ppermute(values, AXES, pairs)]
    ppermute x34 -> x30, starting transfers between devices: 37 us -> 28.2 us  [exchange(): return lax.ppermute(values, AXES, pairs)]
    squeeze x12, local copies, waits for them, and re-layouts: 1.62 us -> 9.66 us  [halves(): sent = lax.dynamic_index_in_dim(sums, 1 - own, axis, keepdims=False)]
    reduce_sum x2 -> x1, other arithmetic: 7.59 us -> 0.89 us  [norm_forward(): average = jnp.mean(values, axis=0, keepdims=True)]
    reduce_sum x1 -> x2, other arithmetic: 0.04 us -> 6.74 us  [the longest x1 6.68 us: norm_forward(): jnp.mean(values * values, axis=0, keepdims=True) - average * average]
  transfers between devices with their start and end apart: 49 -> 44, of which waited for: 26 -> 20; matrix products, arithmetic and copies ran while one was open for 31% -> 34% of each run, Pallas kernels for 8% -> 8%
where the time goes in v3:
time: 593 us; the launch traced here: 584 us
  waiting for transfers between devices  187 us (32%)
  matrix products  124 us (21%)
  other arithmetic  85.4 us (14%)
  starting transfers between devices  68 us (11%)
  local copies, waits for them, and re-layouts  57.3 us (10%)
  Pallas kernels  46.3 us (8%)
  between operations  15.9 us (3%)
    ppermute x30, waiting for transfers between devices, exchange(): return lax.ppermute(values, AXES, pairs)  81.1 us
    all_gather x2, waiting for transfers between devices, on_device(): gather = lambda v: lax.all_gather(v, GROUP, axis=0, tiled=True)  65.1 us
    dot_general x4, matrix products, mm_tn(): lax.dot_general(left, right, (((0,), (0,)), ((), ())), preferred_element_...  46.9 us
    ppermute x11, waiting for transfers between devices, swap(): moved = lax.ppermute(values, AXES, pairs)  41.1 us
    ppermute x11, starting transfers between devices, swap(): moved = lax.ppermute(values, AXES, pairs)  39.7 us
    dot_general x4, matrix products, mm(): lax.dot_general(left, right, (((1,), (0,)), ((), ())), preferred_element_...  33.2 us
    ppermute x30, starting transfers between devices, exchange(): return lax.ppermute(values, AXES, pairs)  28.2 us
    dot_general x6, matrix products, mm_nt(): lax.dot_general(left, right, (((1,), (1,)), ((), ())), preferred_element_...  25.9 us
  transfers between devices with their start and end apart: 44, of which 20 were waited for; matrix products, arithmetic and copies ran while one was open for 34% of the time, Pallas kernels for 8%

profile of v3, /device:TPU:1, one launch (start us, length us, event | category | flops | bytes accessed | tf_op | source)
XLA Modules:
  0.0 583.8 jit_solution(477969429290753865)
XLA Ops:
  8.7 4.6 collective-permute-start
  14.6 2.8 collective-permute-done
  18.2 3.6 collective-permute-start.1
  21.8 10.6 %collective-permute-done.1 = bf16[72,5184]{1,0:T(8,128)(2,1)S(1)} collective-permute-done((bf16[72,5184]{1,0:T(8,128)(2,1)S(1)}, bf16[72,5184]{1,0:T(8,128)(2,1)S(1)}, u32[]{:S(2)}, u32[]{:S(2)}) %collective-permute-start.1) | collective-permute-done | bytes 746528 | tf_op jit(solution)/shard_map/ppermute | solution.py:75
  33.6 4.2 collective-permute-start.6
  44.5 3.3 collective-permute-start.2
  49.7 4.9 collective-permute-start.8
  54.6 5.5 convolution_add_fusion
  61.7 7.2 %collective-permute-done.2 = bf16[576,1024]{1,0:T(8,128)(2,1)S(1)} collective-permute-done((bf16[576,1024]{1,0:T(8,128)(2,1)}, bf16[576,1024]{1,0:T(8,128)(2,1)S(1)}, u32[]{:S(2)}, u32[]{:S(2)}) %collective-permute-start.2) | collective-permute-done | bytes 1179680 | tf_op jit(solution)/shard_map/ppermute | solution.py:75
  69.2 2.5 collective-permute-done.9
  74.4 29.9 %collective-permute-done.5 = f32[1,3456]{1,0:T(1,128)S(1)} collective-permute-done((f32[1,3456]{1,0:T(1,128)S(1)}, f32[1,3456]{1,0:T(1,128)S(1)}, u32[]{:S(2)}, u32[]{:S(2)}) %collective-permute-start.5) | collective-permute-done | bytes 13856 | tf_op jit(solution)/shard_map/ppermute | solution.py:66
  109.7 4.5 fusion.6
  114.2 3.1 collective-permute-start.11
  117.3 7.7 %fusion.65 = f32[1728,1024]{1,0:T(8,128)S(1)} fusion(bf16[1152,1728]{1,0:T(8,128)(2,1)} %all-gather.3.cloned.1.call-done, bf16[1152,1024]{1,0:T(8,128)(2,1)} %get-tuple-element.154), kind=kOutput, calls=%fused_computation.212 | convolution fusion | flops 4076863488 | bytes 13418496 | tf_op jit(solution)/shard_map/dot_general | solution.py:38
  125.6 22.8 %attend.1 = (bf16[576,1024]{1,0:T(8,128)(2,1)S(1)}, f32[8,1,1024]{2,1,0:T(1,128)S(1)}) custom-call(bf16[576,1024]{1,0:T(8,128)(2,1)S(1)} %get-tuple-element.148.q_ref, bf16[576,1024]{1,0:T(8,128)(2,1)S(1)} %slice.194.k_ref, bf16[576,1024]{1,0:T(8,128)(2,1)S(1)} %get-tuple-element.147.v_ref), custom_call_target="tpu_custom_call" | custom-call | flops 2415919104 | bytes 4718592 | tf_op jit(solution)/shard_map/attend/pallas_call | solution.py:157
  148.5 5.0 fusion.61
  165.6 2.8 maximum_select_fusion.1
  170.7 6.7 %multiply_reduce_fusion.2 = (f32[1024]{0:T(1024)S(1)}, f32[1024]{0:T(1024)S(1)}, f32[1152,1024]{1,0:T(8,128)S(1)}, f32[1152,1024]{1,0:T(8,128)}) fusion(f32[1152]{0:T(1024)S(1)} %mul.306, bf16[1,576,1024]{2,1,0:T(8,128)(2,1)S(1)} %bitcast.167, bf16[1,576,1024]{2,1,0:T(8,128)(2,1)S(1)} %bitcast.173, pred[]{:T(512)S(6)} %eq.20, f32[1152]{0:T(1024)S(1)} %copy-done.48, ...), kind=kLoop, calls=%fused_computation.28 | loop fusion | flops 14153728 | bytes 18891776 | tf_op jit(solution)/shard_map/reduce_sum | solution.py:127
  177.4 2.2 copy-done.8
  179.6 2.7 subtract_multiply_fusion
  182.3 65.1 %all-gather.5.cloned.1.call-done = bf16[1152,4608]{1,0:T(8,128)(2,1)} async-done(((bf16[72,4608]{1,0:T(8,128)(2,1)}), bf16[1152,4608]{1,0:T(8,128)(2,1)}) %all-gather.5.cloned.1.call-update) | async-done | bytes 10616848 | tf_op jit(solution)/shard_map/all_gather | solution.py:258
  247.4 15.3 %multiply_convert_fusion = (bf16[2304,1024]{0,1:T(8,128)(2,1)S(1)}, f32[2304,1024]{0,1:T(8,128)}) fusion(f32[2304]{0:T(1024)} %add.374, f32[1152,1024]{1,0:T(8,128)} %subtract_multiply_fusion, f32[1152]{0:T(1024)} %add.371, f32[1152]{0:T(1024)S(1)} %add.370, bf16[1152,4608]{1,0:T(8,128)(2,1)} %all-gather.5.cloned.1.call-done), kind=kOutput, calls=%fused_computation.12 | convolution fusion | flops 5462949888 | bytes 24207872 | tf_op jit(solution)/shard_map/dot_general | solution.py:38
  262.7 5.9 %convolution_convert_fusion = bf16[1152,2304]{1,0:T(8,128)(2,1)S(1)} fusion(bf16[1152,1024]{1,0:T(8,128)(2,1)S(1)} %copy-done.21, bf16[2304,1024]{0,1:T(8,128)(2,1)S(1)} %get-tuple-element.65), kind=kOutput, calls=%fused_computation.4 | convolution fusion | flops 5438472192 | bytes 12386304 | tf_op jit(solution)/shard_map/dot_general | solution.py:42
  268.7 18.9 %fusion.59 = (f32[2304]{0:T(1024)}, bf16[2304,1024]{0,1:T(8,128)(2,1)S(1)}) fusion(bf16[1152,1024]{1,0:T(8,128)(2,1)S(1)} %copy-done.21, bf16[1152,4608]{1,0:T(8,128)(2,1)} %all-gather.5.cloned.1.call-done, f32[2304,1024]{0,1:T(8,128)} %get-tuple-element.184, f32[2304]{0:T(1024)S(1)} %copy-done.52), kind=kOutput, calls=%fused_computation.206 | convolution fusion | flops 5497157632 | bytes 21841920 | tf_op jit(solution)/shard_map/dot_general | solution.py:38
  287.6 6.2 %convolution_convert_fusion.1 = bf16[1152,2304]{1,0:T(8,128)(2,1)S(1)} fusion(bf16[2304,1024]{0,1:T(8,128)(2,1)S(1)} %get-tuple-element.55, f32[1152,1024]{1,0:T(8,128)S(1)} %bitcast.180, f32[1152]{0:T(1024)S(1)} %copy-done.55, f32[1152]{0:T(1024)S(1)} %add.370), kind=kOutput, calls=%fused_computation.5 | convolution fusion | flops 5442011136 | bytes 14754816 | tf_op jit(solution)/shard_map/dot_general | solution.py:42
  293.8 10.2 %fusion.62 = (bf16[1152,1024]{1,0:T(8,128)(2,1)}, f32[1152,1024]{1,0:T(8,128)}) fusion(bf16[2304,1024]{0,1:T(8,128)(2,1)S(1)} %get-tuple-element.55, bf16[1152,4608]{1,0:T(8,128)(2,1)} %all-gather.5.cloned.1.call-done), kind=kOutput, calls=%fused_computation.209 | convolution fusion | flops 5436997632 | bytes 17104896 | tf_op jit(solution)/shard_map/dot_general | solution.py:34
  305.8 4.9 pad_maximum_fusion
  319.1 4.4 bitcast_convert_fusion
  324.9 5.5 multiply_reduce_fusion.3
  330.5 8.0 %fusion.58 = (bf16[1152,1024]{1,0:T(8,128)(2,1)S(1)}, f32[1152,1024]{1,0:T(8,128)}, f32[1152,1024]{1,0:T(8,128)}) fusion(f32[1152]{0:T(1024)S(1)} %mul.306, f32[1024]{0:T(1024)S(1)} %get-tuple-element.187, f32[1024]{0:T(1024)S(1)} %get-tuple-element.188, f32[1152,1024]{1,0:T(8,128)S(1)} %get-tuple-element.141, f32[1152]{0:T(1024)S(1)} %add.370, ...), kind=kLoop, calls=%fused_computation.205 | loop fusion | flops 12976128 | bytes 23618560 | tf_op jit(solution)/shard_map/convert_element_type | solution.py:336
  340.0 2.8 convolution_convert_fusion.3
  342.8 2.6 copy.59
  348.0 4.9 convolution_convert_fusion.4.g_ref
  352.9 23.5 %attend_back.1 = (bf16[576,1024]{1,0:T(8,128)(2,1)S(1)}, bf16[576,1024]{1,0:T(8,128)(2,1)S(1)}, bf16[576,1024]{1,0:T(8,128)(2,1)S(1)}, f32[576,2]{1,0:T(8,128)S(1)}) custom-call(bf16[576,1024]{1,0:T(8,128)(2,1)S(1)} %copy-done.5, bf16[576,1024]{1,0:T(8,128)(2,1)S(1)} %slice.194.k_ref, bf16[576,1024]{1,0:T(8,128)(2,1)} %copy-done.3, ...), custom_call_target="tpu_custom_call" | custom-call | flops 6039797760 | bytes 9437184 | tf_op jit(solution)/shard_map/attend_back/pallas_call | solution.py:210
  378.2 5.0 convolution_convert_fusion.2
  383.2 6.6 %fusion.63 = (bf16[1152,1024]{1,0:T(8,128)(2,1)}, f32[1152,1024]{1,0:T(8,128)}) fusion(bf16[1152,1728]{1,0:T(8,128)(2,1)S(1)} %copy-done.61, bf16[1728,1024]{1,0:T(8,128)(2,1)S(1)} %constant_dynamic-update-slice_fusion), kind=kOutput, calls=%fused_computation.210 | convolution fusion | flops 4078043136 | bytes 14598144 | tf_op jit(solution)/shard_map/dot_general | solution.py:34
  390.4 2.3 fusion.60
  394.1 4.1 copy.53
  398.5 2.4 dynamic-slice_bitcast_fusion
  400.9 3.5 collective-permute-done.35
  407.0 4.2 copy.52
  411.2 2.5 dynamic-slice_bitcast_fusion.1
  416.5 11.4 %fusion.64 = (bf16[1152,1024]{1,0:T(8,128)(2,1)}, f32[1152,1024]{1,0:T(8,128)}) fusion(bf16[2304,1024]{0,1:T(8,128)(2,1)} %copy-done.63, bf16[1152,4608]{1,0:T(8,128)(2,1)} %all-gather.5.cloned.1.call-done), kind=kOutput, calls=%fused_computation.211 | convolution fusion | flops 5436997632 | bytes 17104896 | tf_op jit(solution)/shard_map/dot_general | solution.py:34
  427.8 2.2 collective-permute-start.21
  432.1 5.8 fusion.56
  438.0 3.3 multiply_reduce_fusion.7
  441.3 8.0 %collective-permute-start.22 = (bf16[576,1024]{1,0:T(8,128)(2,1)S(1)}, bf16[576,1024]{1,0:T(8,128)(2,1)}, u32[]{:S(2)}, u32[]{:S(2)}) collective-permute-start(bf16[576,1024]{1,0:T(8,128)(2,1)S(1)} %get-tuple-element.67), channel_id=1, source_target_pairs={{1,2},{2,1},{5,6},{6,5},{9,10},{10,9},{13,14},{14,13},{17,18},{18,... | collective-permute-start | bytes 3538952 | tf_op jit(solution)/shard_map/ppermute | solution.py:75
  455.1 2.3 multiply_reduce_fusion.4
  461.4 8.4 %collective-permute-done.22 = bf16[576,1024]{1,0:T(8,128)(2,1)} collective-permute-done((bf16[576,1024]{1,0:T(8,128)(2,1)S(1)}, bf16[576,1024]{1,0:T(8,128)(2,1)}, u32[]{:S(2)}, u32[]{:S(2)}) %collective-permute-start.22) | collective-permute-done | bytes 1179680 | tf_op jit(solution)/shard_map/ppermute | solution.py:75
  471.3 3.2 collective-permute-done.20
  474.6 2.3 collective-permute-start.25
  480.4 10.8 %collective-permute-done.25 = f32[1,14,576]{2,0,1:T(1,128)S(1)} collective-permute-done((f32[1,14,576]{2,0,1:T(1,128)S(1)}, f32[1,14,576]{2,0,1:T(1,128)S(1)}, u32[]{:S(2)}, u32[]{:S(2)}) %collective-permute-start.25) | collective-permute-done | bytes 32288 | tf_op jit(solution)/shard_map/ppermute | solution.py:66
  491.6 3.4 collective-permute-done.26
  498.9 7.5 %collective-permute-done.27 = f32[2,2,1,14,576]{4,1,0,3,2:T(2,128)S(1)} collective-permute-done((f32[2,2,1,14,576]{4,1,0,3,2:T(2,128)S(1)}, f32[2,2,1,14,576]{4,1,0,3,2:T(2,128)S(1)}, u32[]{:S(2)}, u32[]{:S(2)}) %collective-permute-start.27) | collective-permute-done | bytes 129056 | tf_op jit(solution)/shard_map/ppermute | solution.py:66
  507.0 14.1 %collective-permute-done.28 = f32[2,2,2,1,14,576]{5,2,1,0,4,3:T(2,128)S(1)} collective-permute-done((f32[2,2,2,1,14,576]{5,2,1,0,4,3:T(2,128)S(1)}, f32[2,2,2,1,14,576]{5,2,1,0,4,3:T(2,128)S(1)}, u32[]{:S(2)}, u32[]{:S(2)}) %collective-permute-start.28) | collective-permute-done | bytes 258080 | tf_op jit(solution)/shard_map/ppermute | solution.py:66
  521.8 3.0 collective-permute-start.29
  527.9 4.9 collective-permute-done.29
  534.3 5.6 convolution_bitcast_fusion
  541.0 3.2 collective-permute-start.32
  547.9 9.3 %fusion.25 = f32[6,576,1152]{2,1,0:T(8,128)} fusion(bf16[16,1152,1]{1,0,2:T(8,128)(2,1)S(1)} %copy-done.33, f32[6,576,16]{1,0,2:T(8,128)S(1)} %dot_general.70), kind=kOutput, calls=%fused_computation.114 | convolution fusion | flops 764411904 | bytes 16183296 | tf_op jit(solution)/shard_map/dot_general | solution.py:407
  558.8 3.3 collective-permute-start.33
  562.1 2.4 collective-permute-start.39
  564.5 2.6 fusion.30
  568.4 6.1 %collective-permute-done.39 = bf16[72,4608]{1,0:T(8,128)(2,1)} collective-permute-done((bf16[72,4608]{1,0:T(8,128)(2,1)}, bf16[72,4608]{1,0:T(8,128)(2,1)}, u32[]{:S(2)}, u32[]{:S(2)}) %collective-permute-start.39) | collective-permute-done | bytes 663584 | tf_op jit(solution)/shard_map/ppermute | solution.py:75
  (367 shorter events, 99.1 us)
Async XLA Ops:
  7.2 30.7 %copy-start = (bf16[576,1001]{1,0:T(8,128)(2,1)S(1)}, bf16[576,1001]{1,0:T(8,128)(2,1)}, u32[]{:S(2)}) copy-start(bf16[576,1001]{1,0:T(8,128)(2,1)} %param.18) | copy-start | bytes 3459460
  7.2 107.0 %all-gather.3.cloned.1.call-start = ((), (), s32[]{:S(2)}) async-start(), calls=%async_computation.1 | async-start | bytes 4386816 | tf_op jit(solution)/shard_map/all_gather | solution.py:258
  8.7 24.8 %copy-start.59 = (bf16[576]{0:T(1024)(128)(2,1)S(1)}, bf16[576]{0:T(1024)(128)(2,1)}, u32[]{:S(2)}) copy-start(bf16[576]{0:T(1024)(128)(2,1)} %param.24) | copy-start | bytes 3460
  8.7 24.8 %copy-start.60 = (bf16[576]{0:T(1024)(128)(2,1)S(1)}, bf16[576]{0:T(1024)(128)(2,1)}, u32[]{:S(2)}) copy-start(bf16[576]{0:T(1024)(128)(2,1)} %param.28) | copy-start | bytes 3460
  8.7 24.8 %copy-start.56 = (bf16[2304]{0:T(1024)(128)(2,1)S(1)}, bf16[2304]{0:T(1024)(128)(2,1)}, u32[]{:S(2)}) copy-start(bf16[2304]{0:T(1024)(128)(2,1)} %param.26) | copy-start | bytes 13828
  8.7 24.9 %copy-start.53 = (bf16[2,576]{1,0:T(2,128)(2,1)S(1)}, bf16[2,576]{1,0:T(2,128)(2,1)}, u32[]{:S(2)}) copy-start(bf16[2,576]{1,0:T(2,128)(2,1)} %param.22) | copy-start | bytes 6916
  8.7 29.1 %copy-start.62 = (s32[16]{0:T(128)S(1)}, s32[16]{0:T(128)}, u32[]{:S(2)}) copy-start(s32[16]{0:T(128)} %param.17) | copy-start | bytes 196
  8.7 29.2 %copy-start.57 = (s32[16]{0:T(128)S(1)}, s32[16]{0:T(128)}, u32[]{:S(2)}) copy-start(s32[16]{0:T(128)} %param.16) | copy-start | bytes 196
  8.7 8.6 %collective-permute-start = (bf16[72,1728]{1,0:T(8,128)(2,1)S(1)}, bf16[72,1728]{1,0:T(8,128)(2,1)S(1)}, u32[]{:S(2)}, u32[]{:S(2)}) collective-permute-start(bf16[72,1728]{1,0:T(8,128)(2,1)S(1)} %reshape.1214), channel_id=1, source_target_pairs={{1,2},{2,1},{5,6},{6,5},{9,10},{10,9},{13,14},{14,13},{17,18},{18,... | collective-permute-start | bytes 746504 | tf_op jit(solution)/shard_map/ppermute | solution.py:75
  14.6 23.9 %copy-start.54 = (bf16[6,576]{1,0:T(8,128)(2,1)S(1)}, bf16[6,576]{1,0:T(8,128)(2,1)}, u32[]{:S(2)}) copy-start(bf16[6,576]{1,0:T(8,128)(2,1)} %param.20) | copy-start | bytes 20740
  18.1 229.2 %all-gather.5.cloned.1.call-start = ((), (), s32[]{:S(2)}) async-start(), calls=%async_computation.2 | async-start | bytes 11280384 | tf_op jit(solution)/shard_map/all_gather | solution.py:258
  18.2 14.3 %collective-permute-start.1 = (bf16[72,5184]{1,0:T(8,128)(2,1)S(1)}, bf16[72,5184]{1,0:T(8,128)(2,1)S(1)}, u32[]{:S(2)}, u32[]{:S(2)}) collective-permute-start(bf16[72,5184]{1,0:T(8,128)(2,1)S(1)} %pad_maximum_fusion.1), channel_id=1, source_target_pairs={{1,2},{2,1},{5,6},{6,5},{9,10},{10,9},{13,14},{14,13},{17,18},{18,... | collective-permute-start | bytes 2239496 | tf_op jit(solution)/shard_map/ppermute | solution.py:75
  33.4 528.6 %reduce-scatter.2.cloned.1.call-start = ((), (), s32[]{:S(2)}) async-start(), calls=%async_computation.3 | async-start | bytes 11280384 | tf_op jit(solution)/shard_map/reduce_scatter | solution.py:321
  33.6 6.1 %collective-permute-start.6 = (f32[8,576]{1,0:T(8,128)S(1)}, f32[8,576]{1,0:T(8,128)S(1)}, u32[]{:S(2)}, u32[]{:S(2)}) collective-permute-start(f32[8,576]{1,0:T(8,128)S(1)} %maximum_convert_fusion), channel_id=1, source_target_pairs={{1,2},{2,1},{5,6},{6,5},{9,10},{10,9},{13,14},{14,13},{17,18},{18,... | collective-permute-start | bytes 55304 | tf_op jit(solution)/shard_map/ppermute | solution.py:75
  38.4 3.3 collective-permute-start.4
  39.7 34.6 %copy-start.34 = (f32[8,576]{1,0:T(8,128)}, f32[8,576]{1,0:T(8,128)S(1)}, u32[]{:S(2)}) copy-start(f32[8,576]{1,0:T(8,128)S(1)} %broadcast_select_fusion.9) | copy-start | bytes 55300
  42.6 7.1 %collective-permute-start.7 = (bf16[72,576]{1,0:T(8,128)(2,1)S(1)}, bf16[72,576]{1,0:T(8,128)(2,1)S(1)}, u32[]{:S(2)}, u32[]{:S(2)}) collective-permute-start(bf16[72,576]{1,0:T(8,128)(2,1)S(1)} %get-tuple-element.157), channel_id=1, source_target_pairs={{0,16},{1,17},{2,18},{3,19},{4,20},{5,21},{6,22},{7,23},{8,24},{9,... | collective-permute-start | bytes 248840 | tf_op jit(solution)/shard_map/ppermute | solution.py:66
  44.5 24.3 %collective-permute-start.2 = (bf16[576,1024]{1,0:T(8,128)(2,1)}, bf16[576,1024]{1,0:T(8,128)(2,1)S(1)}, u32[]{:S(2)}, u32[]{:S(2)}) collective-permute-start(bf16[576,1024]{1,0:T(8,128)(2,1)} %bitcast.198), channel_id=1, source_target_pairs={{1,2},{2,1},{5,6},{6,5},{9,10},{10,9},{13,14},{14,13},{17,18},{18,... | collective-permute-start | bytes 3538952 | tf_op jit(solution)/shard_map/ppermute | solution.py:75
  49.7 11.8 %collective-permute-start.8 = (bf16[2,72,576]{2,1,0:T(8,128)(2,1)S(1)}, bf16[2,72,576]{2,1,0:T(8,128)(2,1)S(1)}, u32[]{:S(2)}, u32[]{:S(2)}) collective-permute-start(bf16[2,72,576]{2,1,0:T(8,128)(2,1)S(1)} %maximum_select_fusion.10), channel_id=1, source_target_pairs={{0,8},{1,9},{2,10},{3,11},{4,12},{5,13},{6,14},{7,15},{8,0},{9,1},... | collective-permute-start | bytes 497672 | tf_op jit(solution)/shard_map/ppermute | solution.py:66
  61.6 10.1 %collective-permute-start.9 = (bf16[2,2,72,576]{3,2,1,0:T(8,128)(2,1)S(1)}, bf16[2,2,72,576]{3,2,1,0:T(8,128)(2,1)S(1)}, u32[]{:S(2)}, u32[]{:S(2)}) collective-permute-start(bf16[2,2,72,576]{3,2,1,0:T(8,128)(2,1)S(1)} %maximum_select_fusion.7), channel_id=1, source_target_pairs={{0,4},{1,5},{2,6},{3,7},{4,0},{5,1},{6,2},{7,3},{8,12},{9,13},{10,... | collective-permute-start | bytes 995336 | tf_op jit(solution)/shard_map/ppermute | solution.py:66
  68.9 39.8 %collective-permute-start.3 = (bf16[576,1024]{1,0:T(8,128)(2,1)S(1)}, bf16[576,1024]{1,0:T(8,128)(2,1)S(1)}, u32[]{:S(2)}, u32[]{:S(2)}) collective-permute-start(bf16[576,1024]{1,0:T(8,128)(2,1)S(1)} %broadcast_select_fusion.3), channel_id=1, source_target_pairs={{0,2},{1,3},{2,0},{3,1},{4,6},{5,7},{6,4},{7,5},{8,10},{9,11},{10,... | collective-permute-start | bytes 3538952 | tf_op jit(solution)/shard_map/ppermute | solution.py:66
  72.7 32.9 %collective-permute-start.10 = (bf16[2,2,2,72,576]{4,3,2,1,0:T(8,128)(2,1)}, bf16[2,2,2,72,576]{4,3,2,1,0:T(8,128)(2,1)}, u32[]{:S(2)}, u32[]{:S(2)}) collective-permute-start(bf16[2,2,2,72,576]{4,3,2,1,0:T(8,128)(2,1)} %maximum_select_fusion.4), channel_id=1, source_target_pairs={{0,1},{1,0},{2,3},{3,2},{4,5},{5,4},{6,7},{7,6},{8,9},{9,8},{10,11... | collective-permute-start | bytes 1990664 | tf_op jit(solution)/shard_map/ppermute | solution.py:66
  72.8 31.5 %collective-permute-start.5 = (f32[1,3456]{1,0:T(1,128)S(1)}, f32[1,3456]{1,0:T(1,128)S(1)}, u32[]{:S(2)}, u32[]{:S(2)}) collective-permute-start(f32[1,3456]{1,0:T(1,128)S(1)} %get-tuple-element.169), channel_id=1, source_target_pairs={{0,1},{1,0},{2,3},{3,2},{4,5},{5,4},{6,7},{7,6},{8,9},{9,8},{10,11... | collective-permute-start | bytes 41480 | tf_op jit(solution)/shard_map/ppermute | solution.py:66
  105.2 58.3 %copy-start.44 = (f32[2,576]{1,0:T(2,128)}, f32[2,576]{1,0:T(2,128)S(1)}, u32[]{:S(2)}) copy-start(f32[2,576]{1,0:T(2,128)S(1)} %get-tuple-element.122) | copy-start | bytes 13828
  114.2 39.2 %collective-permute-start.11 = (bf16[576,1024]{1,0:T(8,128)(2,1)}, bf16[576,1024]{1,0:T(8,128)(2,1)S(1)}, u32[]{:S(2)}, u32[]{:S(2)}) collective-permute-start(bf16[576,1024]{1,0:T(8,128)(2,1)} %bitcast.11), channel_id=1, source_target_pairs={{1,2},{2,1},{5,6},{6,5},{9,10},{10,9},{13,14},{14,13},{17,18},{18,... | collective-permute-start | bytes 3538952 | tf_op jit(solution)/shard_map/ppermute | solution.py:75
  125.6 22.8 %copy-start.3 = (bf16[576,1024]{1,0:T(8,128)(2,1)}, bf16[576,1024]{1,0:T(8,128)(2,1)S(1)}, u32[]{:S(2)}) copy-start(bf16[576,1024]{1,0:T(8,128)(2,1)S(1)} %get-tuple-element.147.v_ref) | copy-start | bytes 3538948
  125.6 22.9 %copy-start.16 = (bf16[2,2,2,2,72,576]{5,4,3,2,1,0:T(8,128)(2,1)S(1)}, bf16[2,2,2,2,72,576]{5,4,3,2,1,0:T(8,128)(2,1)}, u32[]{:S(2)}) copy-start(bf16[2,2,2,2,72,576]{5,4,3,2,1,0:T(8,128)(2,1)} %copy.51) | copy-start | bytes 3981316
  148.4 190.1 %copy-start.2 = (bf16[576,1024]{1,0:T(8,128)(2,1)}, bf16[576,1024]{1,0:T(8,128)(2,1)S(1)}, u32[]{:S(2)}) copy-start(bf16[576,1024]{1,0:T(8,128)(2,1)S(1)} %get-tuple-element.52.a_ref) | copy-start | bytes 3538948
  153.4 17.0 %collective-permute-start.13 = (bf16[1152,1024]{1,0:T(8,128)(2,1)}, bf16[1152,1024]{1,0:T(8,128)(2,1)}, u32[]{:S(2)}, u32[]{:S(2)}) collective-permute-start(bf16[1152,1024]{1,0:T(8,128)(2,1)} %get-tuple-element.176), channel_id=1, source_target_pairs={{0,2},{1,3},{2,0},{3,1},{4,6},{5,7},{6,4},{7,5},{8,10},{9,11},{10,... | collective-permute-start | bytes 7077896 | tf_op jit(solution)/shard_map/ppermute | solution.py:66
  154.6 11.1 %collective-permute-start.12 = (bf16[576,1024]{1,0:T(8,128)(2,1)}, bf16[576,1024]{1,0:T(8,128)(2,1)}, u32[]{:S(2)}, u32[]{:S(2)}) collective-permute-start(bf16[576,1024]{1,0:T(8,128)(2,1)} %broadcast_select_fusion.2), channel_id=1, source_target_pairs={{0,2},{1,3},{2,0},{3,1},{4,6},{5,7},{6,4},{7,5},{8,10},{9,11},{10,... | collective-permute-start | bytes 3538952 | tf_op jit(solution)/shard_map/ppermute | solution.py:66
  157.0 3.0 collective-permute-start.14
  262.7 24.9 %slice-start.8 = ((s8[4718592]{0:T(1024)(128)(4,1)}), s8[4194304]{0:T(1024)(128)(4,1)S(1)}, s32[]{:S(2)}) async-start(s8[4718592]{0:T(1024)(128)(4,1)} %bitcast.179), calls=%async_computation.12 | async-start | bytes 8388608
  304.1 20.8 %collective-permute-start.15 = (bf16[1152,1024]{1,0:T(8,128)(2,1)}, bf16[1152,1024]{1,0:T(8,128)(2,1)}, u32[]{:S(2)}, u32[]{:S(2)}) collective-permute-start(bf16[1152,1024]{1,0:T(8,128)(2,1)} %get-tuple-element.179), channel_id=1, source_target_pairs={{0,2},{1,3},{2,0},{3,1},{4,6},{5,7},{6,4},{7,5},{8,10},{9,11},{10,... | collective-permute-start | bytes 7077896 | tf_op jit(solution)/shard_map/ppermute | solution.py:66
  346.7 43.1 %collective-permute-start.34 = (bf16[2,2,2,72,576]{4,3,2,1,0:T(8,128)(2,1)S(1)}, bf16[2,2,2,72,576]{4,3,2,1,0:T(8,128)(2,1)S(1)}, u32[]{:S(2)}, u32[]{:S(2)}) collective-permute-start(bf16[2,2,2,72,576]{4,3,2,1,0:T(8,128)(2,1)S(1)} %dynamic-slice_bitcast_fusion.2), channel_id=1, source_target_pairs={{0,4},{1,5},{2,6},{3,7},{4,0},{5,1},{6,2},{7,3},{8,12},{9,13},{10,... | collective-permute-start | bytes 1990664 | tf_op jit(solution)/shard_map/ppermute | solution.py:66
  390.0 14.4 %collective-permute-start.35 = (bf16[2,2,72,576]{3,2,1,0:T(8,128)(2,1)S(1)}, bf16[2,2,72,576]{3,2,1,0:T(8,128)(2,1)S(1)}, u32[]{:S(2)}, u32[]{:S(2)}) collective-permute-start(bf16[2,2,72,576]{3,2,1,0:T(8,128)(2,1)S(1)} %dynamic-slice_bitcast_fusion.5), channel_id=1, source_target_pairs={{0,1},{1,0},{2,3},{3,2},{4,5},{5,4},{6,7},{7,6},{8,9},{9,8},{10,11... | collective-permute-start | bytes 995336 | tf_op jit(solution)/shard_map/ppermute | solution.py:66
  398.2 33.8 %collective-permute-start.18 = (bf16[1152,1024]{1,0:T(8,128)(2,1)}, bf16[1152,1024]{1,0:T(8,128)(2,1)}, u32[]{:S(2)}, u32[]{:S(2)}) collective-permute-start(bf16[1152,1024]{1,0:T(8,128)(2,1)} %get-tuple-element.181), channel_id=1, source_target_pairs={{0,2},{1,3},{2,0},{3,1},{4,6},{5,7},{6,4},{7,5},{8,10},{9,11},{10,... | collective-permute-start | bytes 7077896 | tf_op jit(solution)/shard_map/ppermute | solution.py:66
  404.4 10.6 %collective-permute-start.36 = (bf16[2,72,576]{2,1,0:T(8,128)(2,1)S(1)}, bf16[2,72,576]{2,1,0:T(8,128)(2,1)S(1)}, u32[]{:S(2)}, u32[]{:S(2)}) collective-permute-start(bf16[2,72,576]{2,1,0:T(8,128)(2,1)S(1)} %dynamic-slice_bitcast_fusion.8), channel_id=1, source_target_pairs={{0,8},{1,9},{2,10},{3,11},{4,12},{5,13},{6,14},{7,15},{8,0},{9,1},... | collective-permute-start | bytes 497672 | tf_op jit(solution)/shard_map/ppermute | solution.py:66
  406.5 34.8 %collective-permute-start.17 = (bf16[2,2,2,72,864]{4,3,2,1,0:T(8,128)(2,1)}, bf16[2,2,2,72,864]{4,3,2,1,0:T(8,128)(2,1)}, u32[]{:S(2)}, u32[]{:S(2)}) collective-permute-start(bf16[2,2,2,72,864]{4,3,2,1,0:T(8,128)(2,1)} %dynamic-slice_bitcast_fusion), channel_id=1, source_target_pairs={{0,4},{1,5},{2,6},{3,7},{4,0},{5,1},{6,2},{7,3},{8,12},{9,13},{10,... | collective-permute-start | bytes 2985992 | tf_op jit(solution)/shard_map/ppermute | solution.py:66
  407.0 30.9 %slice-start.4 = ((s8[4718592]{0:T(1024)(128)(4,1)}), s8[524288]{0:T(1024)(128)(4,1)S(1)}, s32[]{:S(2)}) async-start(s8[4718592]{0:T(1024)(128)(4,1)} %bitcast.175), calls=%async_computation.8 | async-start | bytes 1048576
  411.2 26.7 %slice-start.12 = ((s8[4718592]{0:T(1024)(128)(4,1)}), s8[4194304]{0:T(1024)(128)(4,1)S(1)}, s32[]{:S(2)}) async-start(s8[4718592]{0:T(1024)(128)(4,1)} %bitcast.183), calls=%async_computation.16 | async-start | bytes 8388608
  413.7 27.6 %collective-permute-start.16 = (bf16[2,2,2,72,864]{4,3,2,1,0:T(8,128)(2,1)}, bf16[2,2,2,72,864]{4,3,2,1,0:T(8,128)(2,1)}, u32[]{:S(2)}, u32[]{:S(2)}) collective-permute-start(bf16[2,2,2,72,864]{4,3,2,1,0:T(8,128)(2,1)} %dynamic-slice_bitcast_fusion.1), channel_id=1, source_target_pairs={{0,1},{1,0},{2,3},{3,2},{4,5},{5,4},{6,7},{7,6},{8,9},{9,8},{10,11... | collective-permute-start | bytes 2985992 | tf_op jit(solution)/shard_map/ppermute | solution.py:66
  415.2 14.9 %collective-permute-start.37 = (bf16[72,576]{1,0:T(8,128)(2,1)S(1)}, bf16[72,576]{1,0:T(8,128)(2,1)S(1)}, u32[]{:S(2)}, u32[]{:S(2)}) collective-permute-start(bf16[72,576]{1,0:T(8,128)(2,1)S(1)} %dynamic-slice_bitcast_fusion.11), channel_id=1, source_target_pairs={{0,16},{1,17},{2,18},{3,19},{4,20},{5,21},{6,22},{7,23},{8,24},{9,... | collective-permute-start | bytes 248840 | tf_op jit(solution)/shard_map/ppermute | solution.py:66
  427.8 27.2 %collective-permute-start.21 = (bf16[1152,1024]{1,0:T(8,128)(2,1)}, bf16[1152,1024]{1,0:T(8,128)(2,1)}, u32[]{:S(2)}, u32[]{:S(2)}) collective-permute-start(bf16[1152,1024]{1,0:T(8,128)(2,1)} %get-tuple-element.185), channel_id=1, source_target_pairs={{0,2},{1,3},{2,0},{3,1},{4,6},{5,7},{6,4},{7,5},{8,10},{9,11},{10,... | collective-permute-start | bytes 7077896 | tf_op jit(solution)/shard_map/ppermute | solution.py:66
  430.1 19.2 %collective-permute-start.38 = (bf16[72,576]{1,0:T(8,128)(2,1)S(1)}, bf16[72,576]{1,0:T(8,128)(2,1)S(1)}, u32[]{:S(2)}, u32[]{:S(2)}) collective-permute-start(bf16[72,576]{1,0:T(8,128)(2,1)S(1)} %bitcast_add_fusion.12), channel_id=1, source_target_pairs={{1,2},{2,1},{5,6},{6,5},{9,10},{10,9},{13,14},{14,13},{17,18},{18,... | collective-permute-start | bytes 248840 | tf_op jit(solution)/shard_map/ppermute | solution.py:75
  432.1 23.0 %slice-start = ((s8[4718592]{0:T(1024)(128)(4,1)}), s8[4194304]{0:T(1024)(128)(4,1)S(1)}, s32[]{:S(2)}) async-start(s8[4718592]{0:T(1024)(128)(4,1)} %bitcast.162), calls=%async_computation.4 | async-start | bytes 8388608
  432.1 23.0 %slice-start.6 = ((s8[4718592]{0:T(1024)(128)(4,1)}), s8[524288]{0:T(1024)(128)(4,1)S(1)}, s32[]{:S(2)}) async-start(s8[4718592]{0:T(1024)(128)(4,1)} %bitcast.177), calls=%async_computation.10 | async-start | bytes 1048576
  441.3 28.5 %collective-permute-start.22 = (bf16[576,1024]{1,0:T(8,128)(2,1)S(1)}, bf16[576,1024]{1,0:T(8,128)(2,1)}, u32[]{:S(2)}, u32[]{:S(2)}) collective-permute-start(bf16[576,1024]{1,0:T(8,128)(2,1)S(1)} %get-tuple-element.67), channel_id=1, source_target_pairs={{1,2},{2,1},{5,6},{6,5},{9,10},{10,9},{13,14},{14,13},{17,18},{18,... | collective-permute-start | bytes 3538952 | tf_op jit(solution)/shard_map/ppermute | solution.py:75
  452.6 18.6 %collective-permute-start.19 = (bf16[2,2,72,864]{3,2,1,0:T(8,128)(2,1)}, bf16[2,2,72,864]{3,2,1,0:T(8,128)(2,1)}, u32[]{:S(2)}, u32[]{:S(2)}) collective-permute-start(bf16[2,2,72,864]{3,2,1,0:T(8,128)(2,1)} %dynamic-slice_bitcast_fusion.4), channel_id=1, source_target_pairs={{0,4},{1,5},{2,6},{3,7},{4,0},{5,1},{6,2},{7,3},{8,12},{9,13},{10,... | collective-permute-start | bytes 1493000 | tf_op jit(solution)/shard_map/ppermute | solution.py:66
  455.0 19.5 %collective-permute-start.20 = (bf16[2,2,72,864]{3,2,1,0:T(8,128)(2,1)}, bf16[2,2,72,864]{3,2,1,0:T(8,128)(2,1)}, u32[]{:S(2)}, u32[]{:S(2)}) collective-permute-start(bf16[2,2,72,864]{3,2,1,0:T(8,128)(2,1)} %dynamic-slice_bitcast_fusion.3), channel_id=1, source_target_pairs={{0,1},{1,0},{2,3},{3,2},{4,5},{5,4},{6,7},{7,6},{8,9},{9,8},{10,11... | collective-permute-start | bytes 1493000 | tf_op jit(solution)/shard_map/ppermute | solution.py:66
  457.5 69.0 %collective-permute-start.30 = (bf16[576,1024]{1,0:T(8,128)(2,1)S(1)}, bf16[576,1024]{1,0:T(8,128)(2,1)}, u32[]{:S(2)}, u32[]{:S(2)}) collective-permute-start(bf16[576,1024]{1,0:T(8,128)(2,1)S(1)} %get-tuple-element.146), channel_id=1, source_target_pairs={{1,2},{2,1},{5,6},{6,5},{9,10},{10,9},{13,14},{14,13},{17,18},{18,... | collective-permute-start | bytes 3538952 | tf_op jit(solution)/shard_map/ppermute | solution.py:75
  474.6 16.7 %collective-permute-start.25 = (f32[1,14,576]{2,0,1:T(1,128)S(1)}, f32[1,14,576]{2,0,1:T(1,128)S(1)}, u32[]{:S(2)}, u32[]{:S(2)}) collective-permute-start(f32[1,14,576]{2,0,1:T(1,128)S(1)} %broadcast_in_dim.80), channel_id=1, source_target_pairs={{0,1},{1,0},{2,3},{3,2},{4,5},{5,4},{6,7},{7,6},{8,9},{9,8},{10,11... | collective-permute-start | bytes 96776 | tf_op jit(solution)/shard_map/ppermute | solution.py:66
  478.1 43.0 %copy-start.25 = (bf16[2,2,72,864]{3,2,1,0:T(8,128)(2,1)}, bf16[2,2,72,864]{3,2,1,0:T(8,128)(2,1)S(1)}, u32[]{:S(2)}) copy-start(bf16[2,2,72,864]{3,2,1,0:T(8,128)(2,1)S(1)} %bitcast_add_fusion.4) | copy-start | bytes 1492996
  479.6 41.5 %copy-start.23 = (bf16[2,2,72,864]{3,2,1,0:T(8,128)(2,1)}, bf16[2,2,72,864]{3,2,1,0:T(8,128)(2,1)S(1)}, u32[]{:S(2)}) copy-start(bf16[2,2,72,864]{3,2,1,0:T(8,128)(2,1)S(1)} %bitcast_add_fusion.5) | copy-start | bytes 1492996
  491.4 3.6 collective-permute-start.26
  495.1 11.2 %collective-permute-start.27 = (f32[2,2,1,14,576]{4,1,0,3,2:T(2,128)S(1)}, f32[2,2,1,14,576]{4,1,0,3,2:T(2,128)S(1)}, u32[]{:S(2)}, u32[]{:S(2)}) collective-permute-start(f32[2,2,1,14,576]{4,1,0,3,2:T(2,128)S(1)} %copy.56), channel_id=1, source_target_pairs={{0,8},{1,9},{2,10},{3,11},{4,12},{5,13},{6,14},{7,15},{8,0},{9,1},... | collective-permute-start | bytes 387080 | tf_op jit(solution)/shard_map/ppermute | solution.py:66
  497.3 35.6 %collective-permute-start.24 = (bf16[2,72,864]{2,1,0:T(8,128)(2,1)}, bf16[2,72,864]{2,1,0:T(8,128)(2,1)}, u32[]{:S(2)}, u32[]{:S(2)}) collective-permute-start(bf16[2,72,864]{2,1,0:T(8,128)(2,1)} %dynamic-slice_bitcast_fusion.6), channel_id=1, source_target_pairs={{0,8},{1,9},{2,10},{3,11},{4,12},{5,13},{6,14},{7,15},{8,0},{9,1},... | collective-permute-start | bytes 746504 | tf_op jit(solution)/shard_map/ppermute | solution.py:66
  497.4 35.5 %collective-permute-start.23 = (bf16[2,72,864]{2,1,0:T(8,128)(2,1)}, bf16[2,72,864]{2,1,0:T(8,128)(2,1)}, u32[]{:S(2)}, u32[]{:S(2)}) collective-permute-start(bf16[2,72,864]{2,1,0:T(8,128)(2,1)} %dynamic-slice_bitcast_fusion.7), channel_id=1, source_target_pairs={{0,8},{1,9},{2,10},{3,11},{4,12},{5,13},{6,14},{7,15},{8,0},{9,1},... | collective-permute-start | bytes 746504 | tf_op jit(solution)/shard_map/ppermute | solution.py:66
  506.5 14.6 %collective-permute-start.28 = (f32[2,2,2,1,14,576]{5,2,1,0,4,3:T(2,128)S(1)}, f32[2,2,2,1,14,576]{5,2,1,0,4,3:T(2,128)S(1)}, u32[]{:S(2)}, u32[]{:S(2)}) collective-permute-start(f32[2,2,2,1,14,576]{5,2,1,0,4,3:T(2,128)S(1)} %maximum_select_fusion.8), channel_id=1, source_target_pairs={{0,16},{1,17},{2,18},{3,19},{4,20},{5,21},{6,22},{7,23},{8,24},{9,... | collective-permute-start | bytes 774152 | tf_op jit(solution)/shard_map/ppermute | solution.py:66
  521.8 11.0 %collective-permute-start.29 = (f32[16,14,576]{2,0,1:T(8,128)S(1)}, f32[16,14,576]{2,0,1:T(8,128)S(1)}, u32[]{:S(2)}, u32[]{:S(2)}) collective-permute-start(f32[16,14,576]{2,0,1:T(8,128)S(1)} %select_n.490), channel_id=1, source_target_pairs={{1,2},{2,1},{5,6},{6,5},{9,10},{10,9},{13,14},{14,13},{17,18},{18,... | collective-permute-start | bytes 1548296 | tf_op jit(solution)/shard_map/ppermute | solution.py:75
  539.9 18.0 %collective-permute-start.40 = (f32[16,1152]{1,0:T(8,128)S(1)}, f32[16,1152]{1,0:T(8,128)S(1)}, u32[]{:S(2)}, u32[]{:S(2)}) collective-permute-start(f32[16,1152]{1,0:T(8,128)S(1)} %convolution_bitcast_fusion), channel_id=1, source_target_pairs={{0,1},{1,0},{2,3},{3,2},{4,5},{5,4},{6,7},{7,6},{8,9},{9,8},{10,11... | collective-permute-start | bytes 221192 | tf_op jit(solution)/shard_map/ppermute | solution.py:66
  541.0 17.6 %collective-permute-start.32 = (bf16[72,864]{1,0:T(8,128)(2,1)S(1)}, bf16[72,864]{1,0:T(8,128)(2,1)S(1)}, u32[]{:S(2)}, u32[]{:S(2)}) collective-permute-start(bf16[72,864]{1,0:T(8,128)(2,1)S(1)} %dynamic-slice_bitcast_fusion.9), channel_id=1, source_target_pairs={{0,16},{1,17},{2,18},{3,19},{4,20},{5,21},{6,22},{7,23},{8,24},{9,... | collective-permute-start | bytes 373256 | tf_op jit(solution)/shard_map/ppermute | solution.py:66
  545.1 13.4 %collective-permute-start.31 = (bf16[72,864]{1,0:T(8,128)(2,1)S(1)}, bf16[72,864]{1,0:T(8,128)(2,1)S(1)}, u32[]{:S(2)}, u32[]{:S(2)}) collective-permute-start(bf16[72,864]{1,0:T(8,128)(2,1)S(1)} %dynamic-slice_bitcast_fusion.10), channel_id=1, source_target_pairs={{0,16},{1,17},{2,18},{3,19},{4,20},{5,21},{6,22},{7,23},{8,24},{9,... | collective-permute-start | bytes 373256 | tf_op jit(solution)/shard_map/ppermute | solution.py:66
  558.8 8.4 %collective-permute-start.33 = (bf16[72,1728]{1,0:T(8,128)(2,1)S(1)}, bf16[72,1728]{1,0:T(8,128)(2,1)S(1)}, u32[]{:S(2)}, u32[]{:S(2)}) collective-permute-start(bf16[72,1728]{1,0:T(8,128)(2,1)S(1)} %pad_maximum_fusion.4), channel_id=1, source_target_pairs={{1,2},{2,1},{5,6},{6,5},{9,10},{10,9},{13,14},{14,13},{17,18},{18,... | collective-permute-start | bytes 746504 | tf_op jit(solution)/shard_map/ppermute | solution.py:75
  562.1 12.4 %collective-permute-start.39 = (bf16[72,4608]{1,0:T(8,128)(2,1)}, bf16[72,4608]{1,0:T(8,128)(2,1)}, u32[]{:S(2)}, u32[]{:S(2)}) collective-permute-start(bf16[72,4608]{1,0:T(8,128)(2,1)} %reduce-scatter.2.cloned.1.call-done), channel_id=1, source_target_pairs={{1,2},{2,1},{5,6},{6,5},{9,10},{10,9},{13,14},{14,13},{17,18},{18,... | collective-permute-start | bytes 1990664 | tf_op jit(solution)/shard_map/ppermute | solution.py:75
  (58 other events, 518.9 us)
Sparse Core Ops, SparseCore 0:
  18.3 91.0 all-gather.2
  112.7 134.6 all-gather.4
  310.9 194.7 reduce-scatter.1
